TPU v7x, 32 devices: a whole 2x2x4 slice. The times are simulated.
32 devices in a mesh: shard: 4 (over y, core), context: 2 (over x), tensor: 4 (over z).
Axes of the slice: x: 2, y: 2, z: 4, core: 2. Of those that a mesh axis runs over, the one named last changes fastest.
Arguments:
- block_input: bfloat16 [8192, 1536], P(('shard', 'context')), may hold values from -6 to 6
- norm_gain: float32 [1536], replicated, may hold values from 0.5 to 1.5
- w_z: bfloat16 [1536, 3072], P('shard', 'tensor'), may hold values from -0.15625 to 0.15625
- w_x: bfloat16 [1536, 3072], P('shard', 'tensor'), may hold values from -0.15625 to 0.15625
- w_bc: bfloat16 [1536, 256], P('shard'), may hold values from -0.15625 to 0.15625
- w_dt: bfloat16 [1536, 48], P('shard', 'tensor'), may hold values from -0.15625 to 0.15625
- conv_x_weight: float32 [4, 3072], P(None, 'tensor'), may hold values from -3 to 3
- conv_x_bias: float32 [3072], P('tensor'), may hold values from -1.5 to 1.5
- conv_bc_weight: float32 [4, 256], replicated, may hold values from -3 to 3
- conv_bc_bias: float32 [256], replicated, may hold values from -1.5 to 1.5
- dt_bias: float32 [48], P('tensor'), may hold values from -4 to -1
- a_log: float32 [48], P('tensor'), may hold values from -9 to 0
- d_skip: float32 [48], P('tensor'), may hold values from 0.5 to 1.5
- gate_gain: float32 [3072], P('tensor'), may hold values from 0.5 to 1.5
- w_out: bfloat16 [3072, 1536], P('tensor', 'shard'), may hold values from -0.109375 to 0.109375
- out_cotangent: bfloat16 [8192, 1536], P(('shard', 'context')), may hold values from -6 to 6
Outputs:
- block_output: bfloat16 [8192, 1536], P(('shard', 'context'))
- input_grad: float32 [8192, 1536], P(('shard', 'context'))
- grad_w_z: float32 [1536, 3072], P(('shard', 'context'), 'tensor')
- grad_w_x: float32 [1536, 3072], P(('shard', 'context'), 'tensor')
- grad_w_bc: float32 [1536, 256], P(('shard', 'context'))
- grad_w_dt: float32 [1536, 48], P(('shard', 'context'), 'tensor')
- grad_w_out: float32 [3072, 1536], P('tensor', ('shard', 'context'))
- grad_norm_gain: float32 [1536], replicated
- grad_conv_x_weight: float32 [4, 3072], P(None, 'tensor')
- grad_conv_x_bias: float32 [3072], P('tensor')
- grad_conv_bc_weight: float32 [4, 256], replicated
- grad_conv_bc_bias: float32 [256], replicated
- grad_dt_bias: float32 [48], P('tensor')
- grad_a_log: float32 [48], P('tensor')
- grad_d_skip: float32 [48], P('tensor')
- grad_gate_gain: float32 [3072], P('tensor')
All inputs are finite; a program needn't handle non-finite values.
Results may differ from a plain program's by a relative error of at most 0.0021.
The roundings to bfloat16 on the way count: a program that leaves them out, or rounds other values in their place, can miss the bound.
Values may be sent and summed in bfloat16 or wider, within the bound.
No kernel may reach another device: no remote copies, remote signals or barrier semaphores. Data moves between devices by JAX's collectives and lax.ppermute only.
A program may use at most 192 MiB of HBM per device.

v0:
```python
import jax
import jax.numpy as jnp
from jax import lax
from jax.sharding import PartitionSpec as P

HEADS = 48
HEAD_DIM = 64
STATE = 128
CONV = 4
GROUP = 256


epsilon = 1e-05
precise = lax.Precision.HIGHEST


def shifted(shard, axis, by):
    length = lax.axis_size(axis)
    pairs = [(i, i + by) for i in range(length) if 0 <= i + by < length]
    return lax.ppermute(shard, axis, pairs)


def prefix(value, axis, join, neutral, backward):
    count, mine = (lax.axis_size(axis), lax.axis_index(axis))
    pieces = jax.tree.map(lambda part: lax.all_gather(part, axis), value)
    if backward:
        pieces = jax.tree.map(lambda part: part[::-1], pieces)
        mine = count - 1 - mine
    running = jax.tree.map(
        lambda part, zero: jnp.full_like(part, 0) + jnp.asarray(zero, part.dtype), value, neutral
    )

    def hop(position, running):
        longer = join(running, jax.tree.map(lambda part: part[position], pieces))
        return jax.tree.map(lambda new, old: jnp.where(position < mine, new, old), longer, running)

    return lax.fori_loop(0, count - 1, hop, running)


def silu_slope(value):
    sigma = jax.nn.sigmoid(value)
    return sigma * (1.0 + value * (1.0 - sigma))


def group_states(x_conv, step_size, decay_rate, b_mat, span):
    length, heads, width = x_conv.shape
    count = length // span
    log_step = (-step_size * decay_rate[None, :]).reshape(count, span, heads)
    cum_log = jnp.cumsum(log_step, axis=1)
    x_step = (x_conv * step_size[:, :, None]).reshape(count, span, heads, width)
    tail = jnp.exp(cum_log[:, -1:, :] - cum_log)
    states = jnp.einsum(
        "cqhp,cqn->chpn",
        x_step * tail[:, :, :, None],
        b_mat.reshape(count, span, -1),
        precision=precise,
    )
    return (cum_log, x_step, states)


def summarize(cum_log, states):
    totals = cum_log[:, -1, :]

    def advance(carry, item):
        total, state = item
        return (jnp.exp(total)[:, None, None] * carry + state, carry)

    final, enter = lax.scan(advance, jnp.zeros(states.shape[1:], jnp.float32), (totals, states))
    return (enter, jnp.sum(totals, axis=0), final)


def entry_scale(cum_log):
    totals = cum_log[:, -1, :]
    return jnp.exp(jnp.cumsum(totals, axis=0) - totals)


def group_output(cum_log, x_step, b_mat, c_mat, enter):
    count, span, heads, width = x_step.shape
    b_view = b_mat.reshape(count, span, -1)
    c_view = c_mat.reshape(count, span, -1)
    scores = jnp.einsum("ctn,csn->cts", c_view, b_view, precision=precise)
    cum_heads = jnp.transpose(cum_log, (0, 2, 1))
    gaps = cum_heads[:, :, :, None] - cum_heads[:, :, None, :]
    lower = jnp.arange(span)[:, None] >= jnp.arange(span)[None, :]
    decay = jnp.where(lower, jnp.exp(jnp.minimum(gaps, 0.0)), 0.0)
    inner = jnp.einsum("chts,cshp->cthp", decay * scores[:, None], x_step, precision=precise)
    outer = (
        jnp.einsum("ctn,chpn->cthp", c_view, enter, precision=precise)
        * jnp.exp(cum_log)[:, :, :, None]
    )
    return (inner + outer).reshape(count * span, heads, width)


def ssd_local(x_conv, step_size, decay_rate, b_mat, c_mat, s_in):
    span = min(GROUP, x_conv.shape[0])
    cum_log, x_step, states = group_states(x_conv, step_size, decay_rate, b_mat, span)
    enter, log_decay, s_local = summarize(cum_log, states)
    before = entry_scale(cum_log)
    enter = enter + before[:, :, None, None] * s_in[None]
    return (group_output(cum_log, x_step, b_mat, c_mat, enter), log_decay, s_local)


def combine_carry(earlier, later):
    return (earlier[0] + later[0], earlier[1] * jnp.exp(later[0])[:, None, None] + later[1])


def conv_apply(padded, conv_weight, conv_bias, length):
    total = conv_bias[None, :] + conv_weight[0] * padded[0:length]
    for offset in range(1, CONV):
        total = total + conv_weight[offset] * padded[offset : offset + length]
    return total


def conv_transpose(grad_pre, conv_weight):
    total = jnp.pad(conv_weight[0] * grad_pre, ((0, CONV - 1), (0, 0)))
    for offset in range(1, CONV):
        total = total + jnp.pad(
            conv_weight[offset] * grad_pre, ((offset, CONV - 1 - offset), (0, 0))
        )
    return total


def shards(
    block_input,
    norm_gain,
    w_z,
    w_x,
    w_bc,
    w_dt,
    conv_x_weight,
    conv_x_bias,
    conv_bc_weight,
    conv_bc_bias,
    dt_bias,
    a_log,
    d_skip,
    gate_gain,
    w_out,
    out_cotangent,
):
    full_z, full_x, full_bc, full_dt, full_out = (
        lax.all_gather(w_z, "shard", axis=0, tiled=True),
        lax.all_gather(w_x, "shard", axis=0, tiled=True),
        lax.all_gather(w_bc, "shard", axis=0, tiled=True),
        lax.all_gather(w_dt, "shard", axis=0, tiled=True),
        lax.all_gather(w_out, "shard", axis=1, tiled=True),
    )
    length = block_input.shape[0]
    local_inner = w_z.shape[1]
    heads_here = w_dt.shape[1]
    inner_width = HEADS * HEAD_DIM
    x_float = block_input.astype(jnp.float32)
    inverse = lax.rsqrt(jnp.mean(x_float * x_float, axis=1, keepdims=True) + epsilon)
    normed = (x_float * inverse * norm_gain).astype(jnp.bfloat16)
    z_part = jnp.dot(normed, full_z, preferred_element_type=jnp.float32)
    x_raw = jnp.dot(normed, full_x, preferred_element_type=jnp.float32).astype(jnp.bfloat16)
    bc_raw = jnp.dot(normed, full_bc, preferred_element_type=jnp.float32).astype(jnp.bfloat16)
    dt_raw = jnp.dot(normed, full_dt, preferred_element_type=jnp.float32)
    conv_in = jnp.concatenate([x_raw, bc_raw], axis=1)
    edge = shifted(conv_in[length - CONV + 1 :], "context", 1)
    padded = jnp.concatenate([edge, conv_in], axis=0).astype(jnp.float32)
    conv_weight = jnp.concatenate([conv_x_weight, conv_bc_weight], axis=1)
    conv_bias = jnp.concatenate([conv_x_bias, conv_bc_bias])
    pre = conv_apply(padded, conv_weight, conv_bias, length)
    act = jax.nn.silu(pre)
    x_conv = act[:, :local_inner].reshape(length, heads_here, HEAD_DIM)
    b_mat = act[:, local_inner : local_inner + STATE]
    c_mat = act[:, local_inner + STATE :]
    step_size = jax.nn.softplus(dt_raw + dt_bias)
    decay_rate = jnp.exp(a_log)
    span = min(GROUP, length)
    cum_log, x_step, states = group_states(x_conv, step_size, decay_rate, b_mat, span)
    enter, log_decay, s_local = summarize(cum_log, states)
    identity = (jnp.zeros_like(log_decay), jnp.zeros_like(s_local))
    s_in = prefix((log_decay, s_local), "context", combine_carry, identity, False)[1]
    before = entry_scale(cum_log)
    enter = enter + before[:, :, None, None] * s_in[None]
    ssd_out = group_output(cum_log, x_step, b_mat, c_mat, enter)
    mixer = (ssd_out + d_skip[None, :, None] * x_conv).reshape(length, local_inner)
    gate_value = jax.nn.silu(z_part)
    gated = mixer * gate_value
    square_sum = lax.psum(jnp.sum(gated * gated, axis=1), "tensor")
    gate_inverse = lax.rsqrt(square_sum[:, None] / inner_width + epsilon)
    gated_out = (gated * gate_inverse * gate_gain).astype(jnp.bfloat16)
    out_part = jnp.dot(gated_out, full_out, preferred_element_type=jnp.float32)
    out_total = lax.psum(out_part, "tensor")
    block_output = (x_float + out_total).astype(jnp.bfloat16)
    grad_gated_out = jnp.einsum(
        "td,kd->tk", out_cotangent, full_out, preferred_element_type=jnp.float32
    )
    grad_w_out = jnp.einsum(
        "tk,td->kd", gated_out, out_cotangent, preferred_element_type=jnp.float32
    )
    scaled = gate_gain * grad_gated_out
    row_terms = lax.psum(jnp.sum(scaled * gated, axis=1), "tensor")
    grad_gated = gate_inverse * scaled - gated * gate_inverse * gate_inverse * gate_inverse * (
        row_terms[:, None] / inner_width
    )
    grad_gate_gain = jnp.sum(grad_gated_out * gated * gate_inverse, axis=0)
    grad_mixer = grad_gated * gate_value
    grad_z = (grad_gated * mixer * silu_slope(z_part)).astype(jnp.bfloat16)
    grad_heads = grad_mixer.reshape(length, heads_here, HEAD_DIM)
    grad_d_skip = jnp.sum(grad_heads * x_conv, axis=(0, 2))
    count = length // span
    weighted = (
        grad_heads.reshape(count, span, heads_here, HEAD_DIM)
        * (jnp.exp(cum_log) * before[:, None, :])[:, :, :, None]
    )
    own_grad = jnp.einsum(
        "cqhp,cqn->hpn", weighted, c_mat.reshape(count, span, STATE), precision=precise
    )
    carried = prefix((log_decay, own_grad), "context", combine_carry, identity, True)[1]
    grad_decay = jnp.sum(carried * s_in, axis=(1, 2)) * jnp.exp(log_decay)
    unused_out, pullback = jax.vjp(ssd_local, x_conv, step_size, decay_rate, b_mat, c_mat, s_in)
    grad_xc, grad_step, grad_rate, grad_b, grad_c, unused_state = pullback(
        (grad_heads, grad_decay, carried)
    )
    grad_xc = grad_xc + d_skip[None, :, None] * grad_heads
    grad_bc = lax.psum(jnp.concatenate([grad_b, grad_c], axis=1), "tensor")
    grad_act = jnp.concatenate([grad_xc.reshape(length, local_inner), grad_bc], axis=1)
    grad_pre = grad_act * silu_slope(pre)
    grad_conv_bias = jnp.sum(grad_pre, axis=0)
    grad_conv_weight = jnp.stack(
        [jnp.sum(grad_pre * padded[offset : offset + length], axis=0) for offset in range(CONV)]
    )
    grad_padded = conv_transpose(grad_pre, conv_weight)
    back_edge = shifted(grad_padded[: CONV - 1], "context", -1)
    grad_conv_in = grad_padded[CONV - 1 :] + jnp.pad(back_edge, ((length - CONV + 1, 0), (0, 0)))
    grad_x_raw = grad_conv_in[:, :local_inner].astype(jnp.bfloat16)
    grad_bc_raw = grad_conv_in[:, local_inner:].astype(jnp.bfloat16)
    slope = jax.nn.sigmoid(dt_raw + dt_bias)
    grad_dt_bias = jnp.sum(grad_step * slope, axis=0)
    grad_dt_raw = (grad_step * slope).astype(jnp.bfloat16)
    grad_a_log = grad_rate * decay_rate
    partial_normed = (
        jnp.einsum("tk,dk->td", grad_z, full_z, preferred_element_type=jnp.float32)
        + jnp.einsum("tk,dk->td", grad_x_raw, full_x, preferred_element_type=jnp.float32)
        + jnp.einsum("tk,dk->td", grad_dt_raw, full_dt, preferred_element_type=jnp.float32)
    )
    grad_normed = lax.psum(partial_normed, "tensor") + jnp.einsum(
        "tk,dk->td", grad_bc_raw, full_bc, preferred_element_type=jnp.float32
    )
    scaled_in = norm_gain * grad_normed
    input_grad = (
        out_cotangent.astype(jnp.float32)
        + inverse * scaled_in
        - x_float
        * inverse
        * inverse
        * inverse
        * jnp.mean(scaled_in * x_float, axis=1, keepdims=True)
    )
    grad_norm_gain = jnp.sum(grad_normed * x_float * inverse, axis=0)
    grad_w_z = jnp.einsum("td,tk->dk", normed, grad_z, preferred_element_type=jnp.float32)
    grad_w_x = jnp.einsum("td,tk->dk", normed, grad_x_raw, preferred_element_type=jnp.float32)
    grad_w_bc = jnp.einsum("td,tk->dk", normed, grad_bc_raw, preferred_element_type=jnp.float32)
    grad_w_dt = jnp.einsum("td,tk->dk", normed, grad_dt_raw, preferred_element_type=jnp.float32)
    summed_z, summed_x, summed_bc, summed_dt, summed_out = (
        lax.psum_scatter(grad_w_z, ("shard", "context"), scatter_dimension=0, tiled=True),
        lax.psum_scatter(grad_w_x, ("shard", "context"), scatter_dimension=0, tiled=True),
        lax.psum_scatter(grad_w_bc, ("shard", "context"), scatter_dimension=0, tiled=True),
        lax.psum_scatter(grad_w_dt, ("shard", "context"), scatter_dimension=0, tiled=True),
        lax.psum_scatter(grad_w_out, ("shard", "context"), scatter_dimension=1, tiled=True),
    )
    (
        sum_norm_gain,
        sum_conv_x_weight,
        sum_conv_x_bias,
        sum_conv_bc_weight,
        sum_conv_bc_bias,
        sum_dt_bias,
        sum_a_log,
        sum_d_skip,
        sum_gate_gain,
    ) = lax.psum(
        (
            grad_norm_gain,
            grad_conv_weight[:, :local_inner],
            grad_conv_bias[:local_inner],
            grad_conv_weight[:, local_inner:],
            grad_conv_bias[local_inner:],
            grad_dt_bias,
            grad_a_log,
            grad_d_skip,
            grad_gate_gain,
        ),
        ("shard", "context"),
    )
    return (
        block_output,
        input_grad,
        summed_z,
        summed_x,
        summed_bc,
        summed_dt,
        summed_out,
        sum_norm_gain,
        sum_conv_x_weight,
        sum_conv_x_bias,
        sum_conv_bc_weight,
        sum_conv_bc_bias,
        sum_dt_bias,
        sum_a_log,
        sum_d_skip,
        sum_gate_gain,
    )


def solution(mesh):
    in_specs = (
        P(("shard", "context"), None),
        P(),
        P("shard", "tensor"),
        P("shard", "tensor"),
        P("shard", None),
        P("shard", "tensor"),
        P(None, "tensor"),
        P("tensor"),
        P(),
        P(),
        P("tensor"),
        P("tensor"),
        P("tensor"),
        P("tensor"),
        P("tensor", "shard"),
        P(("shard", "context"), None),
    )
    out_specs = (
        P(("shard", "context"), None),
        P(("shard", "context"), None),
        P(("shard", "context"), "tensor"),
        P(("shard", "context"), "tensor"),
        P(("shard", "context"), None),
        P(("shard", "context"), "tensor"),
        P("tensor", ("shard", "context")),
        P(),
        P(None, "tensor"),
        P("tensor"),
        P(),
        P(),
        P("tensor"),
        P("tensor"),
        P("tensor"),
        P("tensor"),
    )
    return jax.shard_map(shards, mesh=mesh, in_specs=in_specs, out_specs=out_specs, check_vma=False)
```

profile of v0, /device:TPU:0, one launch (start us, length us, event | category | flops | bytes accessed | tf_op | source)
XLA Modules:
  0.0 1077.8 jit_solution(2125863007557966451)
XLA Ops:
  12.7 6.3 all_gather.37
  27.7 12.3 %all_gather.36 = bf16[1536,256]{1,0:T(8,128)(2,1)S(1)} all-gather(bf16[384,256]{1,0:T(8,128)(2,1)S(1)} %copy-done.50), channel_id=1, replica_groups=mesh['shard'=4,'context'=2,'tensor'=4] {'shard'}, dimensions={0}, use_global_device_ids=true | all-gather | bytes 983040 | tf_op jit(solution)/shard_map/all_gather | solution.py:144
  92.1 6.4 fusion.53
  99.9 7.7 while.59
  115.8 10.9 %all-gather.1 = f32[24,64,128]{2,1,0:T(8,128)S(1)} all-gather(f32[12,64,128]{2,1,0:T(8,128)S(1)} %get-tuple-element.281), channel_id=3, replica_groups=mesh['shard'=4,'context'=2,'tensor'=4] {'context'}, dimensions={0}, use_global_device_ids=true | all-gather | bytes 1179648 | tf_op jit(solution)/shard_map/all_gather | solution.py:25
  132.9 14.6 %bitcast_add_fusion.4 = f32[4,256,12,64]{1,3,2,0:T(8,128)S(1)} fusion(f32[4,256,12,64]{1,3,2,0:T(8,128)S(1)} %fusion.67, f32[4,256,256]{2,1,0:T(8,128)S(1)} %fusion.129, f32[4,12,256]{2,1,0:T(8,128)S(1)} %copy-done.32, pred[256,256]{1,0:T(8,128)(4,1)S(1)} %copy-done.53, f32[4,256,12,64]{1,0,3,2:T(4,128)S(1)} %copy-done.6, f32[4,256,12]{1,2,0:T(8,128)S(1)} %copy-done.43, ...), kind=kOutput, calls=%fused_computation.75 | convolution fusion | flops 2430861312 | bytes 10698752 | tf_op jit(solution)/shard_map/chts,cshp->cthp/dot_general | solution.py:86
  151.9 7.9 multiply_reduce_fusion.10
  159.8 11.7 %psum.98 = f32[1024]{0:T(1024)S(1)} all-reduce(f32[1024]{0:T(1024)S(1)} %get-tuple-element.403), channel_id=1, replica_groups=mesh['shard'=4,'context'=2,'tensor'=4] {'tensor'}, use_global_device_ids=true, to_apply=%region_8.9 | all-reduce | flops 1024 | bytes 8192 | tf_op jit(solution)/shard_map/psum | solution.py:182
  171.6 8.6 multiply_reduce_fusion.4
  180.2 8.5 psum.100
  188.7 8.5 multiply_reduce_fusion.5
  200.2 6.9 multiply_reduce_fusion.11
  219.3 8.8 all-gather.2
  230.0 14.7 %while.60 = (s32[]{:T(128)}, f32[12,64,128]{2,1,0:T(8,128)S(1)}, f32[4,12,64,128]{3,2,1,0:T(8,128)}, f32[4,12]{1,0:T(4,128)}, f32[4,12,1,1]{1,3,2,0:T(1,128)}, /...) while((s32[]{:T(128)}, f32[12,64,128]{2,1,0:T(8,128)S(1)}, ...), condition=%wide.region_13.14_spmd.clone, body=%wide.region_12.13_spmd.clone.sunk | while | flops 393219 | bytes 1967968 | solution.py:68
  248.6 18.7 %while.58 = (s32[]{:T(128)}, f32[12,64,128]{2,1,0:T(8,128)S(1)}, f32[4,12]{1,0:T(4,128)}, f32[4,12,64,128]{3,2,1,0:T(8,128)}, f32[4,12,64,128]{3,2,1,0:T(8,128)}...) while((s32[]{:T(128)}, f32[12,64,128]{2,1,0:T(8,128)S(1)}, ...), condition=%wide.region_16.17_spmd, body=%wide.region_14.16_spmd.sunk | while | flops 393219 | bytes 2359869 | solution.py:68
  278.7 20.5 %fusion.60 = (f32[4,12,256]{2,1,0:T(8,128)S(1)}, f32[4,12,256]{2,1,0:T(8,128)}, f32[4,256,256]{2,1,0:T(8,128)S(1)}) fusion(f32[4,12,256]{2,1,0:T(8,128)S(1)} %copy-done.33, f32[4,256,256]{2,1,0:T(8,128)S(1)} %copy-done.40, pred[256,256]{1,0:T(8,128)(4,1)S(1)} %copy-done.54, f32[4,256,12,64]{1,0,3,2:T(4,128)S(1)} %copy-done.7, ...), kind=kOutput, calls=%fused_computation.106 | convolution fusion | flops 2463604736 | bytes 8650752 | tf_op jit(solution)/shard_map/transpose(jvp(chts,cshp->cthp))/dot_general | solution.py:86
  308.5 12.4 %bitcast_add_fusion.3 = f32[4,256,12,64]{1,3,2,0:T(8,128)} fusion(f32[4,256,12,64]{1,3,2,0:T(8,128)S(1)} %get-tuple-element.434, f32[4,256,256]{2,1,0:T(8,128)S(1)} %copy-done.40, f32[4,12,256]{2,1,0:T(8,128)S(1)} %copy-done.33, pred[256,256]{1,0:T(8,128)(4,1)S(1)} %copy-done.54, f32[4,256,12,64]{1,0,3,2:T(4,128)S(1)} %copy-done.8, ...), kind=kOutput, calls=%fused_computation.71 | convolution fusion | flops 2430074880 | bytes 10649600 | tf_op jit(solution)/shard_map/transpose(jvp(chts,cshp->cthp))/dot_general | solution.py:86
  335.4 9.9 reduce-window.16
  363.2 6.8 fusion.121
  374.8 8.5 all-reduce.14.cloned.1.call-done
  383.3 12.4 %multiply_reduce_fusion.3 = (f32[1024]{0:T(1024)S(1)}, f32[1024]{0:T(1024)S(1)}, f32[1024]{0:T(1024)S(1)}, f32[1024]{0:T(1024)S(1)}, f32[1024]{0:T(1024)S(1)}, /*index=5*/f32[1024,1024]{0,1:T(8,128)S(1)}) fusion(f32[1027,1024]{0,1:T(8,128)} %copy-done, f32[1024,1024]{0,1:T(8,128)} %get-tuple-element.406, f32[1024,256]{0,1:T(8,128)} %all-reduce.14.cloned.1.call-done, ...), kind=kLoop, calls=%fused_computation.65 | loop fusion | flops 18869248 | bytes 29380608 | tf_op jit(solution)/shard_map/reduce_sum | solution.py:224
  401.6 9.5 pad_add_fusion
  411.1 7.0 collective-permute-done.1
  422.6 8.1 add_add_fusion
  436.0 8.0 fusion.120
  458.3 397.3 %all-reduce.16.cloned.1.call-done = (f32[1024,1536]{1,0:T(8,128)}, f32[1024,1536]{1,0:T(8,128)}) async-done(((f32[1024,1536]{1,0:T(8,128)}, f32[1024,1536]{1,0:T(8,128)}), (f32[1024,1536]{1,0:T(8,128)}, f32[1024,1536]{1,0:T(8,128)})) %all-reduce.16.cloned.1.call-update) | async-done | bytes 12582928 | tf_op jit(solution)/shard_map/psum | solution.py:186
  855.6 8.2 fusion.27
  863.8 25.9 %all-reduce.9 = (f32[1536]{0:T(1024)}, f32[4,768]{1,0:T(4,128)}, f32[768]{0:T(1024)}, f32[4,256]{1,0:T(4,128)}, f32[256]{0:T(256)}, /*index=5*/f32[12]{0:T(128)}, f32[12]{0:T(128)}, f32[12]{0:T(128)}, f32[768]{0:T(1024)}) all-reduce(f32[1536]{0:T(1024)S(1)} %get-tuple-element.332, ...), channel_id=1, replica_groups=mesh['shard'=4,'context'=2,'tensor'=4] {'shard','context'}, use_global_device_ids=true, to_apply=%region_38.39 | all-reduce | flops 7460 | bytes 59680 | tf_op jit(solution)/shard_map/psum | solution.py:275
  889.7 9.2 fusion.22
  898.9 56.2 %reduce-scatter.14.cloned.1.call-done = f32[768,192]{0,1:T(8,128)} async-done(((f32[768,1536]{0,1:T(8,128)}), f32[768,192]{0,1:T(8,128)}) %reduce-scatter.14.cloned.1.call-update) | async-done | bytes 589840 | tf_op jit(solution)/shard_map/reduce_scatter | solution.py:263
  955.1 57.8 %reduce-scatter.8.cloned.1.call-done = f32[192,768]{1,0:T(8,128)} async-done(((f32[1536,768]{1,0:T(8,128)}), f32[192,768]{1,0:T(8,128)}) %reduce-scatter.8.cloned.1.call-update) | async-done | bytes 589840 | tf_op jit(solution)/shard_map/reduce_scatter | solution.py:259
  1012.9 57.7 %reduce-scatter.10.cloned.1.call-done = f32[192,768]{1,0:T(8,128)} async-done(((f32[1536,768]{1,0:T(8,128)}), f32[192,768]{1,0:T(8,128)}) %reduce-scatter.10.cloned.1.call-update) | async-done | bytes 589840 | tf_op jit(solution)/shard_map/reduce_scatter | solution.py:260
  (389 shorter events, 234.5 us)
Async XLA Ops:
  7.2 45.0 %all-gather.7.cloned.1.call-start = ((), (), s32[]{:S(2)}) async-start(), calls=%async_computation.5 | async-start | bytes 2949120 | tf_op jit(solution)/shard_map/all_gather | solution.py:143
  8.0 144.0 %all-gather.9.cloned.1.call-start = ((), (), s32[]{:S(2)}) async-start(), calls=%async_computation.6 | async-start | bytes 2949120 | tf_op jit(solution)/shard_map/all_gather | solution.py:142
  8.7 162.8 %all-gather.11.cloned.1.call-start = ((), (), s32[]{:S(2)}) async-start(), calls=%async_computation.7 | async-start | bytes 2949120 | tf_op jit(solution)/shard_map/all_gather | solution.py:146
  9.4 373.9 %all-reduce.14.cloned.1.call-start = ((), (), s32[]{:S(2)}) async-start(), calls=%async_computation.8 | async-start | bytes 2097152 | tf_op jit(solution)/shard_map/psum | solution.py:219
  26.5 19.9 %copy-start.85 = (f32[12]{0:T(128)}, f32[12]{0:T(128)S(1)}, u32[]{:S(2)}) copy-start(f32[12]{0:T(128)S(1)} %get-tuple-element.342) | copy-start | bytes 148
  27.6 16.9 %copy-start.71 = (f32[4,768]{1,0:T(4,128)S(1)}, f32[4,768]{1,0:T(4,128)}, u32[]{:S(2)}) copy-start(f32[4,768]{1,0:T(4,128)} %param.28) | copy-start | bytes 36868
  27.6 16.9 %copy-start.81 = (f32[4,256]{1,0:T(4,128)S(1)}, f32[4,256]{1,0:T(4,128)}, u32[]{:S(2)}) copy-start(f32[4,256]{1,0:T(4,128)} %param.30) | copy-start | bytes 12292
  27.6 17.6 %copy-start.92 = (u32[32]{0:T(128)S(1)}, u32[32]{0:T(128)}, u32[]{:S(2)}) copy-start(u32[32]{0:T(128)} %constant.163) | copy-start | bytes 388
  27.6 24.6 %copy-start.4 = (bf16[1024,1536]{1,0:T(8,128)(2,1)S(1)}, bf16[1024,1536]{1,0:T(8,128)(2,1)}, u32[]{:S(2)}) copy-start(bf16[1024,1536]{1,0:T(8,128)(2,1)} %copy-done.3) | copy-start | bytes 9437188
  45.2 28.2 %copy-start.59 = (f32[1,1024]{1,0:T(1,128)}, f32[1,1024]{1,0:T(1,128)S(1)}, u32[]{:S(2)}) copy-start(f32[1,1024]{1,0:T(1,128)S(1)} %get-tuple-element.424) | copy-start | bytes 12292
  57.7 13.0 %collective-permute-start = (bf16[3,1024]{0,1:T(8,128)(2,1)}, bf16[3,1024]{0,1:T(8,128)(2,1)}, u32[]{:S(2)}, u32[]{:S(2)}) collective-permute-start(bf16[3,1024]{0,1:T(8,128)(2,1)} %pad_maximum_fusion.1), channel_id=1, source_target_pairs={{0,4},{1,5},{2,6},{3,7},{8,12},{9,13},{10,14},{11,15},{16,20},{17,... | collective-permute-start | bytes 18440 | tf_op jit(solution)/shard_map/ppermute | solution.py:20
  66.9 121.8 %copy-start.57 = (f32[768]{0:T(1024)}, f32[768]{0:T(1024)S(1)}, u32[]{:S(2)}) copy-start(f32[768]{0:T(1024)S(1)} %mul.593) | copy-start | bytes 9220
  107.6 20.0 %copy-start.77 = (f32[12]{0:T(128)S(1)}, f32[12]{0:T(128)}, u32[]{:S(2)}) copy-start(f32[12]{0:T(128)} %get-tuple-element.429) | copy-start | bytes 148
  127.7 72.4 %copy-start.16 = (f32[12,64,128]{2,1,0:T(8,128)}, f32[12,64,128]{2,1,0:T(8,128)S(1)}, u32[]{:S(2)}) copy-start(f32[12,64,128]{2,1,0:T(8,128)S(1)} %fusion.102) | copy-start | bytes 1179652
  130.1 17.4 %copy-start.39 = (f32[4,256,256]{2,1,0:T(8,128)}, f32[4,256,256]{2,1,0:T(8,128)S(1)}, u32[]{:S(2)}) copy-start(f32[4,256,256]{2,1,0:T(8,128)S(1)} %fusion.129) | copy-start | bytes 3145732
  171.5 17.2 %copy-start.68 = (f32[1024]{0:T(1024)}, f32[1024]{0:T(1024)S(1)}, u32[]{:S(2)}) copy-start(f32[1024]{0:T(1024)S(1)} %add_rsqrt_fusion) | copy-start | bytes 12292
  214.6 15.4 %copy-start.9 = (f32[12,64,128]{2,1,0:T(8,128)S(1)}, f32[12,64,128]{2,1,0:T(8,128)}, u32[]{:S(2)}) copy-start(f32[12,64,128]{2,1,0:T(8,128)} %custom-call.1) | copy-start | bytes 1179652
  230.0 14.8 %copy-start.78 = (f32[12]{0:T(128)S(1)}, f32[12]{0:T(128)}, u32[]{:S(2)}) copy-start(f32[12]{0:T(128)} %get-tuple-element.429) | copy-start | bytes 148
  278.7 20.5 %copy-start.13 = (f32[4,12,64,128]{3,2,1,0:T(8,128)S(1)}, f32[4,12,64,128]{3,2,1,0:T(8,128)}, u32[]{:S(2)}) copy-start(f32[4,12,64,128]{3,2,1,0:T(8,128)} %get-tuple-element.666) | copy-start | bytes 4718596
  278.7 20.5 %copy-start.17 = (f32[12,64,128]{2,1,0:T(8,128)S(1)}, f32[12,64,128]{2,1,0:T(8,128)}, u32[]{:S(2)}) copy-start(f32[12,64,128]{2,1,0:T(8,128)} %copy-done.16) | copy-start | bytes 1179652
  278.7 20.5 %copy-start.44 = (f32[4,256,12]{1,2,0:T(8,128)S(1)}, f32[4,256,12]{1,2,0:T(8,128)}, u32[]{:S(2)}) copy-start(f32[4,256,12]{1,2,0:T(8,128)} %get-tuple-element.421) | copy-start | bytes 147460
  299.2 21.8 %copy-start.27 = (f32[4,256,256]{2,1,0:T(8,128)}, f32[4,256,256]{2,1,0:T(8,128)S(1)}, u32[]{:S(2)}) copy-start(f32[4,256,256]{2,1,0:T(8,128)S(1)} %get-tuple-element.331) | copy-start | bytes 3145732
  333.5 123.0 %reduce-scatter.16.cloned.1.call-start = ((), (), s32[]{:S(2)}) async-start(), calls=%async_computation.13 | async-start | bytes 884736
  363.1 492.5 %all-reduce.16.cloned.1.call-start = ((), (), s32[]{:S(2)}) async-start(), calls=%async_computation.14 | async-start | bytes 25165824 | tf_op jit(solution)/shard_map/psum | solution.py:186
  400.3 17.8 %collective-permute-start.1 = (f32[3,1024]{0,1:T(8,128)S(1)}, f32[3,1024]{0,1:T(8,128)S(1)}, u32[]{:S(2)}, u32[]{:S(2)}) collective-permute-start(f32[3,1024]{0,1:T(8,128)S(1)} %pad_add_fusion.1), channel_id=1, source_target_pairs={{4,0},{5,1},{6,2},{7,3},{12,8},{13,9},{14,10},{15,11},{20,16},{21,... | collective-permute-start | bytes 36872 | tf_op jit(solution)/shard_map/ppermute | solution.py:20
  430.8 468.1 %reduce-scatter.12.cloned.1.call-start = ((), (), s32[]{:S(2)}) async-start(), calls=%async_computation.11 | async-start | bytes 1769472 | tf_op jit(solution)/shard_map/reduce_scatter | solution.py:261
  435.9 519.1 %reduce-scatter.14.cloned.1.call-start = ((), (), s32[]{:S(2)}) async-start(), calls=%async_computation.12 | async-start | bytes 5308416 | tf_op jit(solution)/shard_map/reduce_scatter | solution.py:263
  444.0 568.9 %reduce-scatter.8.cloned.1.call-start = ((), (), s32[]{:S(2)}) async-start(), calls=%async_computation.9 | async-start | bytes 5308416 | tf_op jit(solution)/shard_map/reduce_scatter | solution.py:259
  449.8 620.8 %reduce-scatter.10.cloned.1.call-start = ((), (), s32[]{:S(2)}) async-start(), calls=%async_computation.10 | async-start | bytes 5308416 | tf_op jit(solution)/shard_map/reduce_scatter | solution.py:260
  455.6 400.0 %copy-start.2 = (bf16[1024,1536]{1,0:T(8,128)(2,1)S(1)}, bf16[1024,1536]{1,0:T(8,128)(2,1)}, u32[]{:S(2)}) copy-start(bf16[1024,1536]{1,0:T(8,128)(2,1)} %param.22) | copy-start | bytes 9437188
  455.6 400.0 %copy-start.52 = (f32[1536]{0:T(1024)S(1)}, f32[1536]{0:T(1024)}, u32[]{:S(2)}) copy-start(f32[1536]{0:T(1024)} %param.23) | copy-start | bytes 18436
  455.6 400.0 %copy-start.56 = (f32[1024]{0:T(1024)S(1)}, f32[1024]{0:T(1024)}, u32[]{:S(2)}) copy-start(f32[1024]{0:T(1024)} %copy-done.55) | copy-start | bytes 12292
  (73 other events, 411.8 us)
Sparse Core Ops, SparseCore 0:
  9.6 29.9 all-gather.6
  41.1 23.6 all-gather.8
  66.4 24.0 all-gather.10
  333.6 49.6 all-reduce.13
  386.3 36.3 reduce-scatter.15
  430.9 424.6 all-reduce.15
  859.5 37.7 reduce-scatter.11
  901.3 53.7 reduce-scatter.13
  959.1 53.7 reduce-scatter.7
  1016.8 53.7 reduce-scatter.9
where the time goes:
time: 1090 us; the launch traced here: 1080 us
  waiting for transfers between devices  587 us (54%)
  matrix products  181 us (17%)
  other arithmetic  106 us (10%)
  local copies, waits for them, and re-layouts  91.7 us (8%)
  blocking collectives  89.2 us (8%)
  between operations  16.5 us (2%)
    psum x1, waiting for transfers between devices, shards(): out_total = lax.psum(out_part, 'tensor')  397 us
    reduce_scatter x1, waiting for transfers between devices, shards(): lax.psum_scatter(grad_w_z, ('shard', 'context'), scatter_dimension=0, til...  57.8 us
    reduce_scatter x1, waiting for transfers between devices, shards(): lax.psum_scatter(grad_w_x, ('shard', 'context'), scatter_dimension=0, til...  57.7 us
    reduce_scatter x1, waiting for transfers between devices, shards(): lax.psum_scatter(grad_w_out, ('shard', 'context'), scatter_dimension=1, t...  56.2 us
    dot_general x3, matrix products, group_output(): jnp.einsum('chts,cshp->cthp', decay * scores[:, None], x_step, precision=...  47.4 us
    psum x1, blocking collectives, shards(): lax.psum((grad_norm_gain, grad_conv_weight[:, :local_inner], grad_conv_bi...  25.9 us
  transfers between devices with their start and end apart: 12, of which 6 were waited for; matrix products, arithmetic and copies ran while one was open for 21% of the time, Pallas kernels for 0%

commit v1 on v0

v1 whole, which is shorter than its diff:
```python
import functools

import jax
import jax.numpy as jnp
from jax import lax
from jax.experimental import pallas as pl
from jax.experimental.pallas import tpu as pltpu
from jax.sharding import PartitionSpec as P

HEADS = 48
HEAD_DIM = 64
STATE = 128
CONV = 4
SPAN = 128
LANES = 128

epsilon = 1e-05
f32 = jnp.float32
bf16 = jnp.bfloat16


def split(v):
    hi = v.astype(bf16)
    return hi, (v - hi.astype(f32)).astype(bf16)


def dot(a, b):
    return lax.dot_general(a, b, (((1,), (0,)), ((), ())), preferred_element_type=f32)


def dot_t(a, b):
    return lax.dot_general(a, b, (((1,), (1,)), ((), ())), preferred_element_type=f32)


def lhs3(parts):
    hi, lo = parts
    return jnp.concatenate([hi, lo, hi], axis=1)


def rhs3(parts):
    hi, lo = parts
    return jnp.concatenate([hi, hi, lo], axis=0)


def rhs3_t(parts):
    hi, lo = parts
    return jnp.concatenate([hi, hi, lo], axis=1)


def spread(values, spread_mat):
    hi, lo = split(values)
    return dot(jnp.concatenate([hi, lo], axis=1), spread_mat)


def gather_heads(values, gather_mat):
    hi, lo = split(values)
    return dot(jnp.concatenate([hi, lo], axis=1), gather_mat)


def tri_sum(tri2, values):
    hi, lo = split(values)
    return dot(tri2, jnp.concatenate([hi, lo], axis=0))


def sigmoid(v):
    return 1.0 / (1.0 + jnp.exp(-v))


def slope_of(v, sigma):
    return sigma * (1.0 + v * (1.0 - sigma))


def front_kernel(x_ref, bc_ref, edge_ref, cw_ref, cb_ref, step_ref, rate_ref, spread_ref, tri_ref,
                 pre_ref, act_ref, cum_ref, state_ref, total_ref, ext, state):
    c = pl.program_id(0)
    rows, inner = x_ref.shape
    wide = cw_ref.shape[1]

    @pl.when(c == 0)
    def _():
        ext[0:8, :] = edge_ref[...]
        state[...] = jnp.zeros_like(state)
        total_ref[...] = jnp.zeros_like(total_ref)

    ext[8 : 8 + rows, 0:inner] = x_ref[...].astype(f32)
    ext[8 : 8 + rows, inner:wide] = bc_ref[...].astype(f32)
    pre = cb_ref[...] + cw_ref[0:1, :] * ext[5 : 5 + rows, :]
    for k in range(1, CONV):
        pre = pre + cw_ref[k : k + 1, :] * ext[5 + k : 5 + k + rows, :]
    ext[0:8, :] = ext[rows : rows + 8, :]
    act = pre * sigmoid(pre)
    pre_ref[...] = pre
    act_ref[...] = act
    step = step_ref[...]
    cum = tri_sum(tri_ref[...], -step * rate_ref[...])
    cum_ref[...] = cum
    total = cum[rows - 1 : rows, :]
    b_t = jnp.transpose(act[:, inner : inner + STATE])
    weight = spread(step * jnp.exp(total - cum), spread_ref[...])
    decay = spread(jnp.broadcast_to(jnp.exp(total), (8, LANES)), spread_ref[...])[0:1, :]
    new = decay * state[...] + dot(lhs3(split(b_t)), rhs3(split(act[:, 0:inner] * weight)))
    state[...] = new
    state_ref[...] = new
    total_ref[...] = total_ref[...] + jnp.broadcast_to(total, (8, LANES))


def forward_kernel(act_ref, step_ref, cum_ref, z_ref, ggo_ref, s_in_ref, d_ref, gain_ref, spread_ref,
                   mixer_ref, enter_ref, exit_ref, sums_ref, state):
    c = pl.program_id(0)
    rows, inner = z_ref.shape

    @pl.when(c == 0)
    def _():
        state[...] = s_in_ref[...]

    heads = inner // HEAD_DIM
    per = LANES // HEAD_DIM
    spread_mat = spread_ref[...]
    x = act_ref[:, 0:inner]
    b_mat = act_ref[:, inner : inner + STATE]
    c_mat = act_ref[:, inner + STATE : inner + 2 * STATE]
    step = step_ref[...]
    cum = cum_ref[...]
    cum_t = jnp.transpose(cum)
    total = cum[rows - 1 : rows, :]
    wide = spread(
        jnp.concatenate([step, step * jnp.exp(total - cum), jnp.exp(cum)], axis=0), spread_mat
    )
    decay = spread(jnp.broadcast_to(jnp.exp(total), (8, LANES)), spread_mat)[0:1, :]
    x_step = x * wide[0:rows]
    c3 = lhs3(split(c_mat))
    scores = dot_t(c3, rhs3_t(split(b_mat)))
    enter = state[...]
    enter_ref[...] = enter
    outer = dot(c3, rhs3(split(enter))) * wide[2 * rows : 3 * rows]
    lower = lax.broadcasted_iota(jnp.int32, (rows, rows), 0) >= lax.broadcasted_iota(
        jnp.int32, (rows, rows), 1
    )
    lane = lax.broadcasted_iota(jnp.int32, (rows, LANES), 1)
    masked = jnp.where(lower, scores, 0.0)
    tiles = []
    for tile in range(heads // per):
        value = rhs3(split(x_step[:, tile * LANES : (tile + 1) * LANES]))
        got = None
        for j in range(per):
            h = tile * per + j
            gap = cum[:, h : h + 1] - cum_t[h : h + 1, :]
            part = dot(lhs3(split(jnp.exp(jnp.minimum(gap, 0.0)) * masked)), value)
            got = part if got is None else jnp.where(lane >= j * HEAD_DIM, part, got)
        tiles.append(got)
    inner_out = jnp.concatenate(tiles, axis=1)
    mixer = inner_out + outer + d_ref[...] * x
    mixer_ref[...] = mixer
    b_t = jnp.transpose(b_mat)
    new = decay * enter + dot(lhs3(split(b_t)), rhs3(split(x * wide[rows : 2 * rows])))
    state[...] = new
    exit_ref[...] = new
    z = z_ref[...]
    gated = mixer * (z * sigmoid(z))
    square = jnp.sum(gated * gated, axis=1, keepdims=True)
    term = jnp.sum(gain_ref[...] * ggo_ref[...] * gated, axis=1, keepdims=True)
    both = jnp.where(lane == 0, square, term)
    sums_ref[...] = jnp.transpose(both)[0:8, :]


def gate_kernel(inner_width, mixer_ref, z_ref, ggo_ref, sums_ref, act_ref, cum_ref, gain_ref, spread_ref,
                out_ref, gm_ref, gz_ref, own_ref, acc_ref, state):
    c = pl.program_id(0)
    rows, inner = z_ref.shape

    @pl.when(c == 0)
    def _():
        state[...] = jnp.zeros_like(state)
        acc_ref[...] = jnp.zeros_like(acc_ref)

    spread_mat = spread_ref[...]
    columns = jnp.transpose(jnp.concatenate([sums_ref[...]] * (LANES // 8), axis=0))
    inverse = lax.rsqrt(columns[:, 0:1] / inner_width + epsilon)
    term = columns[:, 1:2] / inner_width
    mixer = mixer_ref[...]
    z = z_ref[...]
    sigma = sigmoid(z)
    gate = z * sigma
    gated = mixer * gate
    ggo = ggo_ref[...]
    normal = gated * inverse
    out_ref[...] = (normal * gain_ref[...]).astype(bf16)
    grad_gated = inverse * (gain_ref[...] * ggo) - normal * (inverse * inverse * term)
    gm = grad_gated * gate
    gm_ref[...] = gm
    gz_ref[...] = (grad_gated * mixer * slope_of(z, sigma)).astype(bf16)
    x = act_ref[:, 0:inner]
    c_mat = act_ref[:, inner + STATE : inner + 2 * STATE]
    acc_ref[0:1, :] += jnp.sum(ggo * normal, axis=0, keepdims=True)
    acc_ref[1:2, :] += jnp.sum(gm * x, axis=0, keepdims=True)
    cum = cum_ref[...]
    total = cum[rows - 1 : rows, :]
    grown = spread(jnp.exp(cum), spread_mat)
    decay = spread(jnp.broadcast_to(jnp.exp(total), (8, LANES)), spread_mat)[0:1, :]
    new = decay * state[...] + dot(
        lhs3(split(jnp.transpose(c_mat))), rhs3(split(gm * grown))
    )
    state[...] = new
    own_ref[...] = new


def backward_kernel(gm_ref, act_ref, pre_ref, step_ref, cum_ref, mixer_ref, enter_ref, exit_ref, carried_ref,
                    x_raw_ref, cw_ref, d_ref, rate_ref, spread_ref, gather_ref, upper_ref,
                    gx_ref, tail_ref, head_ref, dbc_ref, gstep_ref, conv_ref, rate_out_ref,
                    state, ext):
    c = pl.program_id(0)
    rows, inner = gm_ref.shape

    @pl.when(c == 0)
    def _():
        state[...] = carried_ref[...]
        ext[rows : rows + 8, :] = jnp.zeros((8, inner), f32)
        conv_ref[...] = jnp.zeros_like(conv_ref)
        rate_out_ref[...] = jnp.zeros_like(rate_out_ref)

    heads = inner // HEAD_DIM
    per = LANES // HEAD_DIM
    spread_mat = spread_ref[...]
    gather_mat = gather_ref[...]
    gm = gm_ref[...]
    x = act_ref[:, 0:inner]
    b_mat = act_ref[:, inner : inner + STATE]
    c_mat = act_ref[:, inner + STATE : inner + 2 * STATE]
    step = step_ref[...]
    cum = cum_ref[...]
    cum_t = jnp.transpose(cum)
    total = cum[rows - 1 : rows, :]
    wide = spread(
        jnp.concatenate([step, jnp.exp(total - cum), jnp.exp(cum)], axis=0), spread_mat
    )
    step_wide, tail_wide, grown = wide[0:rows], wide[rows : 2 * rows], wide[2 * rows : 3 * rows]
    decay = spread(jnp.broadcast_to(jnp.exp(total), (8, LANES)), spread_mat)[0:1, :]
    x_step = x * step_wide
    b_parts, c_parts = split(b_mat), split(c_mat)
    b3 = lhs3(b_parts)
    scores_t = dot_t(b3, rhs3_t(c_parts))
    grad_exit = state[...]
    exit_parts = split(grad_exit)
    upper = lax.broadcasted_iota(jnp.int32, (rows, rows), 1) >= lax.broadcasted_iota(
        jnp.int32, (rows, rows), 0
    )
    lane = lax.broadcasted_iota(jnp.int32, (rows, LANES), 1)
    through = dot(b3, rhs3(exit_parts)) * tail_wide
    gm_hi, gm_lo = split(gm)
    xs_hi, xs_lo = split(x_step)
    tiles = []
    grad_scores = jnp.zeros((rows, rows), f32)
    zero = jnp.zeros((rows, LANES), bf16)
    for tile in range(heads // per):
        cut = slice(tile * LANES, (tile + 1) * LANES)
        g_hi, g_lo = gm_hi[:, cut], gm_lo[:, cut]
        g_rows = jnp.concatenate([g_hi, g_hi, g_lo], axis=0)
        g_lanes = jnp.concatenate([g_hi, g_hi, g_lo], axis=1)
        got = None
        for j in range(per):
            h = tile * per + j
            keep = (lane >= j * HEAD_DIM) & (lane < (j + 1) * HEAD_DIM)
            xh = jnp.where(keep, xs_hi[:, cut], zero)
            xl = jnp.where(keep, xs_lo[:, cut], zero)
            gap = cum_t[h : h + 1, :] - cum[:, h : h + 1]
            span = jnp.where(upper, jnp.exp(jnp.minimum(gap, 0.0)), 0.0)
            pairs = dot_t(jnp.concatenate([xh, xl, xh], axis=1), g_lanes)
            grad_scores = grad_scores + span * pairs
            part = dot(lhs3(split(span * scores_t)), g_rows)
            got = part if got is None else jnp.where(lane >= j * HEAD_DIM, part, got)
        tiles.append(got)
    grad_xs = jnp.concatenate(tiles, axis=1) + through
    scores_parts = split(grad_scores)
    weighted = gm * grown
    weighted_parts = split(weighted)
    enter_parts = split(enter_ref[...])
    grad_b = dot(lhs3(scores_parts), rhs3(c_parts)) + dot_t(
        lhs3(split(x_step * tail_wide)), rhs3_t(exit_parts)
    )
    grad_c = dot(lhs3(split(jnp.transpose(grad_scores))), rhs3(b_parts)) + dot_t(
        lhs3(weighted_parts), rhs3_t(enter_parts)
    )
    dbc_ref[:, 0:STATE] = grad_b
    dbc_ref[:, STATE : 2 * STATE] = grad_c
    lost = jnp.sum(grad_exit * exit_ref[...], axis=0, keepdims=True)
    state[...] = decay * grad_exit + dot(
        lhs3(split(jnp.transpose(c_mat))), rhs3(weighted_parts)
    )
    ssd = mixer_ref[...] - d_ref[...] * x
    heads_sum = gather_heads(
        jnp.concatenate([gm * ssd, x * grad_xs, jnp.broadcast_to(lost, (8, inner))], axis=0), gather_mat
    )
    by_step = heads_sum[rows : 2 * rows]
    grad_log = tri_sum(upper_ref[...], heads_sum[0:rows] - step * by_step) + heads_sum[
        2 * rows : 2 * rows + 1
    ]
    gstep_ref[...] = by_step - rate_ref[...] * grad_log
    rate_out_ref[0:1, :] += -jnp.sum(grad_log * step, axis=0, keepdims=True)
    pre = pre_ref[...]
    grad_pre = (grad_xs * step_wide + d_ref[...] * gm) * slope_of(pre, sigmoid(pre))
    ext[0:rows, :] = grad_pre
    raw = x_raw_ref[...].astype(f32)
    conv_ref[CONV : CONV + 1, :] += jnp.sum(grad_pre, axis=0, keepdims=True)
    total_in = None
    for k in range(CONV):
        moved = ext[CONV - 1 - k : CONV - 1 - k + rows, :]
        conv_ref[k : k + 1, :] += jnp.sum(moved * raw, axis=0, keepdims=True)
        piece = cw_ref[k : k + 1, :] * moved
        total_in = piece if total_in is None else total_in + piece
    gx_ref[...] = total_in.astype(bf16)

    @pl.when(c == 0)
    def _():
        tail_ref[...] = total_in[rows - 8 : rows, :]

    head_ref[...] = grad_pre[0:8, :]
    ext[rows : rows + 8, :] = grad_pre[0:8, :]


def shifted(value, axis, by):
    length = lax.axis_size(axis)
    pairs = [(i, i + by) for i in range(length) if 0 <= i + by < length]
    return lax.ppermute(value, axis, pairs)


def rotated(value, axis, by):
    length = lax.axis_size(axis)
    return lax.ppermute(value, axis, [(i, (i + by) % length) for i in range(length)])


def chain(local, decay, axis, by):
    got = None
    for _ in range(lax.axis_size(axis) - 1):
        got = shifted(local if got is None else local + decay * got, axis, by)
    return jnp.zeros_like(local) if got is None else got


def row_block(shape, index):
    return pl.BlockSpec(shape, index)


def shards(
    block_input,
    norm_gain,
    w_z,
    w_x,
    w_bc,
    w_dt,
    conv_x_weight,
    conv_x_bias,
    conv_bc_weight,
    conv_bc_bias,
    dt_bias,
    a_log,
    d_skip,
    gate_gain,
    w_out,
    out_cotangent,
):
    length, width = block_input.shape
    inner = w_z.shape[1]
    heads = w_dt.shape[1]
    wide = inner + 2 * STATE
    inner_width = HEADS * HEAD_DIM
    ranks = lax.axis_size("tensor")
    me = lax.axis_index("tensor")
    quarter = length // ranks
    rows = min(SPAN, length)
    count = length // rows

    w_cat = jnp.concatenate([w_x, jnp.pad(w_dt, ((0, 0), (0, LANES - heads))), w_bc], axis=1)
    full_cat = lax.all_gather(w_cat, "shard", axis=0, tiled=True)
    full_z = lax.all_gather(w_z, "shard", axis=0, tiled=True)
    full_out = lax.all_gather(w_out, "shard", axis=1, tiled=True)

    x_float = block_input.astype(f32)
    inverse = lax.rsqrt(jnp.mean(x_float * x_float, axis=1, keepdims=True) + epsilon)
    normed = (x_float * inverse * norm_gain).astype(bf16)
    proj = jnp.dot(normed, full_cat, preferred_element_type=f32)
    x_raw = proj[:, :inner].astype(bf16)
    dt_raw = proj[:, inner : inner + LANES]
    bc_raw = proj[:, inner + LANES :].astype(bf16)
    z_part = jnp.dot(normed, full_z, preferred_element_type=f32)

    edge = shifted(
        jnp.concatenate([x_raw[length - CONV + 1 :], bc_raw[length - CONV + 1 :]], axis=1), "context", 1
    ).astype(f32)
    edge = jnp.pad(edge, ((8 - CONV + 1, 0), (0, 0)))
    conv_weight = jnp.concatenate([conv_x_weight, conv_bc_weight], axis=1)
    conv_bias = jnp.concatenate([conv_x_bias, conv_bc_bias])[None, :]
    dt_in = dt_raw + jnp.pad(dt_bias, (0, LANES - heads))
    step = jax.nn.softplus(dt_in)
    decay_rate = jnp.exp(a_log)
    rate_row = jnp.pad(decay_rate, (0, LANES - heads))[None, :]
    d_row = jnp.repeat(d_skip, HEAD_DIM)[None, :]
    gain_row = gate_gain[None, :]
    owner = jnp.arange(inner) // HEAD_DIM
    one_hot = (jnp.arange(LANES)[:, None] == owner[None, :]).astype(bf16)
    spread_mat = jnp.concatenate([one_hot, one_hot], axis=0)
    one_hot_t = (owner[:, None] == jnp.arange(LANES)[None, :]).astype(bf16)
    gather_mat = jnp.concatenate([one_hot_t, one_hot_t], axis=0)
    place = jnp.arange(rows)
    lower = (place[:, None] >= place[None, :]).astype(bf16)
    lower2 = jnp.concatenate([lower, lower], axis=1)
    upper = (place[:, None] <= place[None, :]).astype(bf16)
    upper2 = jnp.concatenate([upper, upper], axis=1)

    def whole(shape):
        return pl.BlockSpec(shape, lambda c: (0,) * len(shape))

    def ahead(lanes, high=rows):
        return pl.BlockSpec((high, lanes), lambda c: (c, 0))

    def back(lanes, high=rows):
        return pl.BlockSpec((high, lanes), lambda c: (count - 1 - c, 0))

    def shape(*dims, dtype=f32):
        return jax.ShapeDtypeStruct(dims, dtype)

    params = pltpu.CompilerParams(dimension_semantics=("arbitrary",))

    pre, act, cum, s_local, totals = pl.pallas_call(
        front_kernel,
        grid=(count,),
        in_specs=[
            ahead(inner), ahead(2 * STATE), whole((8, wide)), whole((CONV, wide)), whole((1, wide)),
            ahead(LANES), whole((1, LANES)), whole((2 * LANES, inner)), whole((rows, 2 * rows)),
        ],
        out_specs=[ahead(wide), ahead(wide), ahead(LANES), whole((STATE, inner)), whole((8, LANES))],
        out_shape=[
            shape(length, wide), shape(length, wide), shape(length, LANES), shape(STATE, inner),
            shape(8, LANES),
        ],
        scratch_shapes=[pltpu.VMEM((rows + 8, wide), f32), pltpu.VMEM((STATE, inner), f32)],
        compiler_params=params,
        name="front",
    )(x_raw, bc_raw, edge, conv_weight, conv_bias, step, rate_row, spread_mat, lower2)
    decay = jnp.repeat(jnp.exp(totals[0, :heads]), HEAD_DIM)[None, :]
    s_in = chain(s_local, decay, "context", 1)

    ggo = jnp.einsum("td,kd->tk", out_cotangent, full_out, preferred_element_type=f32)
    mixer, enter, leave, sums = pl.pallas_call(
        forward_kernel,
        grid=(count,),
        in_specs=[
            ahead(wide), ahead(LANES), ahead(LANES), ahead(inner), ahead(inner), whole((STATE, inner)),
            whole((1, inner)), whole((1, inner)), whole((2 * LANES, inner)),
        ],
        out_specs=[
            ahead(inner), ahead(inner, STATE), ahead(inner, STATE), pl.BlockSpec((8, rows), lambda c: (0, c)),
        ],
        out_shape=[
            shape(length, inner), shape(count * STATE, inner), shape(count * STATE, inner), shape(8, length),
        ],
        scratch_shapes=[pltpu.VMEM((STATE, inner), f32)],
        compiler_params=params,
        name="forward",
    )(act, step, cum, z_part, ggo, s_in, d_row, gain_row, spread_mat)
    sums = lax.psum(sums, "tensor")

    gated_out, gm, grad_z, own, gate_acc = pl.pallas_call(
        functools.partial(gate_kernel, inner_width),
        grid=(count,),
        in_specs=[
            back(inner), back(inner), back(inner), pl.BlockSpec((8, rows), lambda c: (0, count - 1 - c)),
            back(wide), back(LANES), whole((1, inner)), whole((2 * LANES, inner)),
        ],
        out_specs=[back(inner), back(inner), back(inner), whole((STATE, inner)), whole((8, inner))],
        out_shape=[
            shape(length, inner, dtype=bf16), shape(length, inner), shape(length, inner, dtype=bf16),
            shape(STATE, inner), shape(8, inner),
        ],
        scratch_shapes=[pltpu.VMEM((STATE, inner), f32)],
        compiler_params=params,
        name="gate",
    )(mixer, z_part, ggo, sums, act, cum, gain_row, spread_mat)
    carried = chain(own, decay, "context", -1)

    def block(value, k):
        return lax.dynamic_slice_in_dim(value, ((me + k) % ranks) * quarter, quarter)

    out_own = jnp.dot(block(gated_out, 0), full_out, preferred_element_type=f32)
    for k in range(1, ranks):
        part = jnp.dot(block(gated_out, k), full_out, preferred_element_type=f32)
        out_own = out_own + rotated(part, "tensor", k)
    block_own = (block(block_input, 0).astype(f32) + out_own).astype(bf16)
    block_output = jnp.zeros((length, width), bf16)
    for k in range(ranks):
        piece = block_own if k == 0 else rotated(block_own, "tensor", k)
        block_output = lax.dynamic_update_slice_in_dim(
            block_output, piece, ((me - k) % ranks) * quarter, 0
        )
    grad_w_out = jnp.einsum("tk,td->kd", gated_out, out_cotangent, preferred_element_type=f32)
    summed_out = lax.psum_scatter(grad_w_out, ("shard", "context"), scatter_dimension=1, tiled=True)
    grad_w_z = jnp.einsum("td,tk->dk", normed, grad_z, preferred_element_type=f32)
    summed_z = lax.psum_scatter(grad_w_z, ("shard", "context"), scatter_dimension=0, tiled=True)

    gx, gx_tail, pre_head, dbc, gstep, conv_acc, rate_acc = pl.pallas_call(
        backward_kernel,
        grid=(count,),
        in_specs=[
            back(inner), back(wide), back(inner), back(LANES), back(LANES), back(inner),
            back(inner, STATE), back(inner, STATE), whole((STATE, inner)), back(inner), whole((CONV, inner)),
            whole((1, inner)), whole((1, LANES)), whole((2 * LANES, inner)), whole((2 * inner, LANES)),
            whole((rows, 2 * rows)),
        ],
        out_specs=[
            back(inner), whole((8, inner)), whole((8, inner)), back(2 * STATE), back(LANES), whole((8, inner)),
            whole((8, LANES)),
        ],
        out_shape=[
            shape(length, inner, dtype=bf16), shape(8, inner), shape(8, inner), shape(length, 2 * STATE),
            shape(length, LANES), shape(8, inner), shape(8, LANES),
        ],
        scratch_shapes=[pltpu.VMEM((STATE, inner), f32), pltpu.VMEM((rows + 8, inner), f32)],
        compiler_params=params,
        name="backward",
    )(gm, act, pre, step, cum, mixer, enter, leave, carried, x_raw, conv_x_weight, d_row, rate_row,
      spread_mat, gather_mat, upper2)

    dbc = lax.psum(dbc, "tensor")
    pre_bc = pre[:, inner:]
    grad_pre_bc = dbc * slope_of(pre_bc, jax.nn.sigmoid(pre_bc))
    next_head = shifted(
        jnp.concatenate([pre_head[: CONV - 1], grad_pre_bc[: CONV - 1]], axis=1), "context", -1
    )
    after = jnp.pad(next_head, ((CONV - 1, CONV - 1), (0, 0)))
    reach = jnp.zeros((CONV - 1, wide), f32)
    for k in range(CONV):
        reach = reach + conv_weight[k] * after[CONV - 1 - k : 2 * (CONV - 1) - k]
    gx_last = (gx_tail + jnp.pad(reach[:, :inner], ((8 - CONV + 1, 0), (0, 0)))).astype(bf16)
    gx = lax.dynamic_update_slice_in_dim(gx, gx_last, length - 8, 0)
    bc_pad = jnp.concatenate([grad_pre_bc, next_head[:, inner:]], axis=0)
    gbc = jnp.zeros((length, 2 * STATE), f32)
    for k in range(CONV):
        gbc = gbc + conv_bc_weight[k] * bc_pad[CONV - 1 - k : CONV - 1 - k + length]
    gbc = gbc.astype(bf16)
    head_pad = jnp.pad(pre_head[: CONV - 1], ((CONV - 1, CONV - 1), (0, 0)))
    entering = edge[8 - CONV + 1 :]
    extra = jnp.stack([
        jnp.sum(entering[:, :inner] * head_pad[CONV - 1 - k : 2 * (CONV - 1) - k], axis=0)
        for k in range(CONV)
    ])
    bc_in = jnp.concatenate([entering[:, inner:], bc_raw.astype(f32)], axis=0)
    grad_conv_bc = jnp.stack([jnp.sum(grad_pre_bc * bc_in[k : k + length], axis=0) for k in range(CONV)])
    grad_conv_bc_bias = jnp.sum(grad_pre_bc, axis=0)

    sigma = jax.nn.sigmoid(dt_in)
    g_dt = gstep * sigma
    grad_dt_bias = jnp.sum(g_dt, axis=0)
    g_dt = g_dt.astype(bf16)
    grad_a_log = rate_acc[0] * rate_row[0]

    g_xdt = jnp.concatenate([gx, g_dt], axis=1)
    full_xdt = full_cat[:, : inner + LANES]

    def partial_of(k):
        return jnp.einsum("tk,dk->td", block(grad_z, k), full_z, preferred_element_type=f32) + jnp.einsum(
            "tk,dk->td", block(g_xdt, k), full_xdt, preferred_element_type=f32
        )

    received = [rotated(partial_of(k).astype(bf16), "tensor", k) for k in range(1, ranks)]
    gn = partial_of(0) + jnp.einsum(
        "tk,dk->td", block(gbc, 0), full_cat[:, inner + LANES :], preferred_element_type=f32
    )
    for piece in received:
        gn = gn + piece.astype(f32)
    x_own, inv_own = block(x_float, 0), block(inverse, 0)
    scaled = norm_gain * gn
    delta = inv_own * scaled - x_own * (inv_own * inv_own * inv_own) * jnp.mean(
        scaled * x_own, axis=1, keepdims=True
    )
    delta = delta.astype(bf16)
    grad_norm_gain = jnp.sum(gn * x_own * inv_own, axis=0)
    input_grad = jnp.zeros((length, width), f32)
    for k in range(ranks):
        piece = delta if k == 0 else rotated(delta, "tensor", k)
        input_grad = lax.dynamic_update_slice_in_dim(
            input_grad,
            block(out_cotangent, -k).astype(f32) + piece.astype(f32),
            ((me - k) % ranks) * quarter,
            0,
        )

    g_cat = jnp.concatenate([g_xdt, gbc], axis=1)
    grad_w_cat = jnp.einsum("td,tk->dk", normed, g_cat, preferred_element_type=f32)
    summed_cat = lax.psum_scatter(grad_w_cat, ("shard", "context"), scatter_dimension=0, tiled=True)

    last = jnp.pad(jnp.concatenate([grad_dt_bias[:LANES], grad_a_log]), (0, inner - 2 * LANES))[None, :]
    packed = jnp.concatenate(
        [
            jnp.concatenate([conv_acc[:CONV] + extra, conv_acc[CONV : CONV + 1], gate_acc[:2], last], axis=0),
            jnp.concatenate(
                [grad_conv_bc, grad_conv_bc_bias[None, :], jnp.zeros((3, 2 * STATE), f32)], axis=0
            ),
        ],
        axis=1,
    )
    packed = lax.psum(packed, ("shard", "context"))
    sum_norm_gain = lax.psum(grad_norm_gain, ("shard", "context", "tensor"))
    return (
        block_output,
        input_grad,
        summed_z,
        summed_cat[:, :inner],
        summed_cat[:, inner + LANES :],
        summed_cat[:, inner : inner + heads],
        summed_out,
        sum_norm_gain,
        packed[:CONV, :inner],
        packed[CONV, :inner],
        packed[:CONV, inner:],
        packed[CONV, inner:],
        packed[7, :heads],
        packed[7, LANES : LANES + heads],
        jnp.sum(packed[6, :inner].reshape(heads, HEAD_DIM), axis=1),
        packed[5, :inner],
    )


def solution(mesh):
    in_specs = (
        P(("shard", "context"), None),
        P(),
        P("shard", "tensor"),
        P("shard", "tensor"),
        P("shard", None),
        P("shard", "tensor"),
        P(None, "tensor"),
        P("tensor"),
        P(),
        P(),
        P("tensor"),
        P("tensor"),
        P("tensor"),
        P("tensor"),
        P("tensor", "shard"),
        P(("shard", "context"), None),
    )
    out_specs = (
        P(("shard", "context"), None),
        P(("shard", "context"), None),
        P(("shard", "context"), "tensor"),
        P(("shard", "context"), "tensor"),
        P(("shard", "context"), None),
        P(("shard", "context"), "tensor"),
        P("tensor", ("shard", "context")),
        P(),
        P(None, "tensor"),
        P("tensor"),
        P(),
        P(),
        P("tensor"),
        P("tensor"),
        P("tensor"),
        P("tensor"),
    )
    return jax.shard_map(shards, mesh=mesh, in_specs=in_specs, out_specs=out_specs, check_vma=False)
```

time: 1090 us -> 649 us (0.60)
  waiting for transfers between devices: 587 us -> 194 us
  matrix products: 181 us -> 63.8 us
  starting transfers between devices: 5.91 us -> 110 us
  other arithmetic: 106 us -> 37 us
  Pallas kernels: 0 us -> 62.8 us
  local copies, waits for them, and re-layouts: 91.7 us -> 29.7 us
  blocking collectives: 89.2 us -> 135 us
    psum x2 -> x1, waiting for transfers between devices: 406 us -> 47.5 us  [shards(): dbc = lax.psum(dbc, 'tensor')]
    dot_general x27 -> x18, matrix products: 170 us -> 59.5 us  [the longest x4 9.05 us: partial_of(): jnp.einsum('tk,dk->td', block(grad_z, k), full_z, preferred_element_type=...]
    ppermute x2 -> x16, starting transfers between devices: 5.51 us -> 110 us  [the longest x12 102 us: rotated(): lax.ppermute(value, axis, [(i, (i + by) % length) for i in range(length)])]
    ppermute x2 -> x16, waiting for transfers between devices: 6.98 us -> 99 us  [the longest x12 87.4 us: rotated(): lax.ppermute(value, axis, [(i, (i + by) % length) for i in range(length)])]
    psum x3, blocking collectives: 46.1 us -> 135 us  [the longest x1 89.9 us: shards(): sum_norm_gain = lax.psum(grad_norm_gain, ('shard', 'context', 'tensor'))]
    pallas_call x0 -> x4, Pallas kernels: none -> 62.8 us  [the longest x1 26.9 us: shards(): pl.pallas_call(backward_kernel, grid=(count,), in_specs=[back(inner), bac...]
    reduce_scatter x1, waiting for transfers between devices: 57.8 us -> 0.01 us  [shards(): lax.psum_scatter(grad_w_z, ('shard', 'context'), scatter_dimension=0, til...]
    reduce_scatter x2 -> x1, waiting for transfers between devices: 57.7 us -> 0.01 us  [shards(): lax.psum_scatter(grad_w_cat, ('shard', 'context'), scatter_dimension=0, t...]
  transfers between devices with their start and end apart: 12 -> 23, of which waited for: 6 -> 9; matrix products, arithmetic and copies ran while one was open for 21% -> 17% of each run, Pallas kernels for 0% -> 2%
where the time goes in v1:
time: 649 us; the launch traced here: 647 us
  waiting for transfers between devices  194 us (30%)
  blocking collectives  135 us (21%)
  starting transfers between devices  110 us (17%)
  matrix products  63.8 us (10%)
  Pallas kernels  62.8 us (10%)
  other arithmetic  37 us (6%)
  local copies, waits for them, and re-layouts  29.7 us (5%)
  between operations  15 us (2%)
    ppermute x12, starting transfers between devices, rotated(): lax.ppermute(value, axis, [(i, (i + by) % length) for i in range(length)])  102 us
    psum x1, blocking collectives, shards(): sum_norm_gain = lax.psum(grad_norm_gain, ('shard', 'context', 'tensor'))  89.9 us
    ppermute x12, waiting for transfers between devices, rotated(): lax.ppermute(value, axis, [(i, (i + by) % length) for i in range(length)])  87.4 us
    psum x1, waiting for transfers between devices, shards(): dbc = lax.psum(dbc, 'tensor')  47.5 us
    all_gather x1, waiting for transfers between devices, shards(): full_cat = lax.all_gather(w_cat, 'shard', axis=0, tiled=True)  26.9 us
    pallas_call x1, Pallas kernels, shards(): pl.pallas_call(backward_kernel, grid=(count,), in_specs=[back(inner), bac...  26.9 us
    psum x1, blocking collectives, shards(): packed = lax.psum(packed, ('shard', 'context'))  24.7 us
    psum x1, blocking collectives, shards(): sums = lax.psum(sums, 'tensor')  20.2 us
  transfers between devices with their start and end apart: 23, of which 9 were waited for; matrix products, arithmetic and copies ran while one was open for 17% of the time, Pallas kernels for 2%

profile of v1, /device:TPU:0, one launch (start us, length us, event | category | flops | bytes accessed | tf_op | source)
XLA Modules:
  0.0 647.0 jit_solution(5787573332689598108)
XLA Ops:
  17.7 18.8 %all-gather.6.cloned.1.call-done = bf16[1536,768]{1,0:T(8,128)(2,1)} async-done(((bf16[384,768]{1,0:T(8,128)(2,1)}), bf16[1536,768]{1,0:T(8,128)(2,1)}) %all-gather.6.cloned.1.call-update) | async-done | bytes 2359312 | tf_op jit(solution)/shard_map/all_gather | solution.py:373
  36.5 6.0 fusion.95.z_ref
  42.5 26.9 %all-gather.4.cloned.1.call-done = bf16[1536,1152]{1,0:T(8,128)(2,1)} async-done(((bf16[384,1152]{1,0:T(8,128)(2,1)}), bf16[1536,1152]{1,0:T(8,128)(2,1)}) %all-gather.4.cloned.1.call-update) | async-done | bytes 3538960 | tf_op jit(solution)/shard_map/all_gather | solution.py:372
  69.4 6.3 fusion.101
  75.7 3.4 collective-permute-start
  83.3 11.4 %front.1 = (f32[1024,1024]{1,0:T(8,128)}, f32[1024,1024]{1,0:T(8,128)}, f32[1024,128]{1,0:T(8,128)}, f32[128,768]{1,0:T(8,128)}, f32[8,128]{1,0:T(8,128)}) custom-call(bf16[1024,768]{1,0:T(8,128)(2,1)} %slice.207.x_ref.x_raw_ref, bf16[1024,256]{1,0:T(8,128)(2,1)} %get-tuple-element.112.bc_ref, f32[8,1024]{1,0:T(8,128)} %pad.32.edge_ref, ...), custom_call_target="tpu_custom_call" | custom-call | tf_op jit(solution)/shard_map/front/pallas_call | solution.py:422
  96.8 7.0 %fusion.102.ggo_ref = f32[1024,768]{1,0:T(8,128)} fusion(bf16[1024,1536]{1,0:T(8,128)(2,1)} %param.31, bf16[768,1536]{1,0:T(8,128)(2,1)} %all-gather.8.cloned.1.call-done), kind=kOutput, calls=%fused_computation.181 | convolution fusion | flops 2415919104 | bytes 8650752 | tf_op jit(solution)/shard_map/td,kd->tk/dot_general | solution.py:441
  106.5 13.5 %forward.1 = (f32[1024,768]{1,0:T(8,128)}, f32[1024,768]{1,0:T(8,128)}, f32[1024,768]{1,0:T(8,128)}, f32[8,1024]{1,0:T(8,128)}) custom-call(f32[1024,1024]{1,0:T(8,128)} %get-tuple-element.36.act_ref, f32[1024,128]{1,0:T(8,128)} %compare_select_fusion.step_ref, f32[1024,128]{1,0:T(8,128)} %get-tuple-element.37.cum_ref, f32[1024,768]{1,0:T(8,128)} %fusion.95.z_ref, ...), custom_call_target="tpu_custom_call" | custom-call | tf_op jit(solution)/shard_map/forward/pallas_call | solution.py:442
  119.9 20.2 %psum.28.sums_ref = f32[8,1024]{1,0:T(8,128)} all-reduce(f32[8,1024]{1,0:T(8,128)} %get-tuple-element.40), channel_id=1, replica_groups=mesh['shard'=4,'context'=2,'tensor'=4] {'tensor'}, use_global_device_ids=true, to_apply=%region_1.2 | all-reduce | flops 8192 | bytes 65536 | tf_op jit(solution)/shard_map/psum | solution.py:459
  140.1 11.0 %gate.1 = (bf16[1024,768]{1,0:T(8,128)(2,1)}, f32[1024,768]{1,0:T(8,128)}, bf16[1024,768]{1,0:T(8,128)(2,1)}, f32[128,768]{1,0:T(8,128)}, f32[8,768]{1,0:T(8,128)}) custom-call(f32[1024,768]{1,0:T(8,128)} %get-tuple-element.39.mixer_ref, f32[1024,768]{1,0:T(8,128)} %fusion.95.z_ref, f32[1024,768]{1,0:T(8,128)} %fusion.102.ggo_ref, f32[8,1024]{1,0:T(8,128)} %psum.28.sums_ref, ...), custom_call_target="tpu_custom_call" | custom-call | tf_op jit(solution)/shard_map/gate/pallas_call | solution.py:461
  154.1 7.0 %collective-permute-done.8.carried_ref = f32[128,768]{1,0:T(8,128)} collective-permute-done((f32[128,768]{1,0:T(8,128)}, f32[128,768]{1,0:T(8,128)}, u32[]{:S(2)}, u32[]{:S(2)}) %collective-permute-start.8) | collective-permute-done | bytes 393248 | tf_op jit(solution)/shard_map/ppermute | solution.py:323
  161.1 26.9 %backward.1 = (bf16[1024,768]{1,0:T(8,128)(2,1)}, f32[8,768]{1,0:T(8,128)}, f32[8,768]{1,0:T(8,128)}, f32[1024,256]{1,0:T(8,128)}, f32[1024,128]{1,0:T(8,128)}, /*index=5*/f32[8,768]{1,0:T(8,128)}, f32[8,128]{1,0:T(8,128)}) custom-call(f32[1024,768]{1,0:T(8,128)} %get-tuple-element.43.gm_ref, f32[1024,1024]{1,0:T(8,128)} %get-tuple-element.36.act_ref, ...), custom_call_target="tpu_custom_call" | custom-call | tf_op jit(solution)/shard_map/backward/pallas_call | solution.py:498
  188.9 47.5 %all-reduce.10.cloned.1.call-done = f32[1024,256]{1,0:T(8,128)} async-done(((f32[1024,256]{1,0:T(8,128)}), f32[1024,256]{1,0:T(8,128)}) %all-reduce.10.cloned.1.call-update) | async-done | bytes 1048592 | tf_op jit(solution)/shard_map/psum | solution.py:521
  236.5 4.3 fusion.97
  247.9 6.6 %fusion.8 = f32[1536,1152]{1,0:T(8,128)} fusion(bf16[1024,256]{1,0:T(8,128)(2,1)S(1)} %fusion.31, bf16[1024,128]{1,0:T(8,128)(2,1)S(1)} %get-tuple-element.106, bf16[1024,768]{1,0:T(8,128)(2,1)S(1)} %fusion.65, f32[1536]{0:T(1024)S(1)} %copy-done.34, f32[1024]{0:T(1024)S(1)} %copy-done.42, bf16[1024,1536]{1,0:T(8,128)(2,1)S(1)} %copy-done.8), kind=kOutput, calls=%fused_computation.21 | convolution fusion | flops 3637248000 | bytes 12593152 | tf_op jit(solution)/shard_map/td,tk->dk/dot_general | solution.py:586
  254.6 6.0 fusion.94
  260.8 6.6 %convert_element_type.94 = f32[1024,1536]{1,0:T(8,128)} convert(bf16[1024,1536]{1,0:T(8,128)(2,1)} %param.16) | non-fusion elementwise | flops 1572864 | bytes 9437184 | tf_op jit(solution)/shard_map/convert_element_type | solution.py:376
  268.6 2.9 fusion.61
  280.3 4.3 fusion.103
  286.3 3.1 fusion.53
  302.0 24.7 %psum.31 = f32[8,1024]{1,0:T(8,128)} all-reduce(f32[8,1024]{1,0:T(8,128)} %pad_maximum_fusion.2), channel_id=1, replica_groups=mesh['shard'=4,'context'=2,'tensor'=4] {'shard','context'}, use_global_device_ids=true, to_apply=%region_19.20 | all-reduce | flops 8192 | bytes 65536 | tf_op jit(solution)/shard_map/psum | solution.py:599
  336.7 2.9 collective-permute-start.12
  340.7 37.9 %collective-permute-done.3 = f32[256,1536]{1,0:T(8,128)} collective-permute-done((f32[256,1536]{1,0:T(8,128)}, f32[256,1536]{1,0:T(8,128)}, u32[]{:S(2)}, u32[]{:S(2)}) %collective-permute-start.3) | collective-permute-done | bytes 1572896 | tf_op jit(solution)/shard_map/ppermute | solution.py:328
  378.8 4.5 constant_dynamic-update-slice_fusion.3
  383.3 65.6 %collective-permute-start.5 = (bf16[256,1536]{1,0:T(8,128)(2,1)}, bf16[256,1536]{1,0:T(8,128)(2,1)}, u32[]{:S(2)}, u32[]{:S(2)}) collective-permute-start(bf16[256,1536]{1,0:T(8,128)(2,1)} %get-tuple-element.128), channel_id=1, source_target_pairs={{0,1},{1,2},{2,3},{3,0},{4,5},{5,6},{6,7},{7,4},{8,9},{9,10},{10,1... | collective-permute-start | bytes 2359304 | tf_op jit(solution)/shard_map/ppermute | solution.py:328
  448.9 3.1 collective-permute-start.6
  452.0 42.2 %collective-permute-done.11 = bf16[256,1536]{1,0:T(8,128)(2,1)S(1)} collective-permute-done((bf16[256,1536]{1,0:T(8,128)(2,1)S(1)}, bf16[256,1536]{1,0:T(8,128)(2,1)S(1)}, u32[]{:S(2)}, u32[]{:S(2)}) %collective-permute-start.11) | collective-permute-done | bytes 786464 | tf_op jit(solution)/shard_map/ppermute | solution.py:328
  501.1 17.4 %collective-permute-start.13 = (bf16[256,1536]{1,0:T(8,128)(2,1)}, bf16[256,1536]{1,0:T(8,128)(2,1)}, u32[]{:S(2)}, u32[]{:S(2)}) collective-permute-start(bf16[256,1536]{1,0:T(8,128)(2,1)} %get-tuple-element.109), channel_id=1, source_target_pairs={{0,1},{1,2},{2,3},{3,0},{4,5},{5,6},{6,7},{7,4},{8,9},{9,10},{10,1... | collective-permute-start | bytes 2359304 | tf_op jit(solution)/shard_map/ppermute | solution.py:328
  521.6 3.1 collective-permute-start.14
  524.7 89.9 %psum.30 = f32[1536]{0:T(1024)} all-reduce(f32[1536]{0:T(1024)S(1)} %get-tuple-element.88), channel_id=1, replica_groups=mesh['shard'=4,'context'=2,'tensor'=4] {'shard','context','tensor'}, use_global_device_ids=true, to_apply=%region_8.9 | all-reduce | flops 1536 | bytes 12288 | tf_op jit(solution)/shard_map/psum | solution.py:600
  620.8 3.1 add_dynamic-update-slice_fusion.2
  626.4 7.3 %collective-permute-done.15 = bf16[256,1536]{1,0:T(8,128)(2,1)S(1)} collective-permute-done((bf16[256,1536]{1,0:T(8,128)(2,1)}, bf16[256,1536]{1,0:T(8,128)(2,1)S(1)}, u32[]{:S(2)}, u32[]{:S(2)}) %collective-permute-start.15) | collective-permute-done | bytes 786464 | tf_op jit(solution)/shard_map/ppermute | solution.py:328
  (244 shorter events, 90.5 us)
Async XLA Ops:
  7.3 29.2 %all-gather.6.cloned.1.call-start = ((), (), s32[]{:S(2)}) async-start(), calls=%async_computation.4 | async-start | bytes 2949120 | tf_op jit(solution)/shard_map/all_gather | solution.py:373
  8.0 61.3 %all-gather.4.cloned.1.call-start = ((), (), s32[]{:S(2)}) async-start(), calls=%async_computation.3 | async-start | bytes 4423680 | tf_op jit(solution)/shard_map/all_gather | solution.py:372
  11.3 85.5 %all-gather.8.cloned.1.call-start = ((), (), s32[]{:S(2)}) async-start(), calls=%async_computation.5 | async-start | bytes 2949120 | tf_op jit(solution)/shard_map/all_gather | solution.py:374
  12.0 224.4 %all-reduce.10.cloned.1.call-start = ((), (), s32[]{:S(2)}) async-start(), calls=%async_computation.6 | async-start | bytes 2097152 | tf_op jit(solution)/shard_map/psum | solution.py:521
  12.1 30.3 %copy-start.53 = (f32[12]{0:T(128)}, f32[12]{0:T(128)S(1)}, u32[]{:S(2)}) copy-start(f32[12]{0:T(128)S(1)} %exp.14) | copy-start | bytes 148
  13.5 66.8 %copy-start.46 = (f32[128]{0:T(128)}, f32[128]{0:T(128)S(1)}, u32[]{:S(2)}) copy-start(f32[128]{0:T(128)S(1)} %pad.33) | copy-start | bytes 1540
  16.9 52.5 %copy-start.41 = (f32[1024]{0:T(1024)}, f32[1024]{0:T(1024)S(1)}, u32[]{:S(2)}) copy-start(f32[1024]{0:T(1024)S(1)} %add_rsqrt_fusion) | copy-start | bytes 12292
  75.7 7.0 %collective-permute-start = (bf16[3,1024]{1,0:T(4,128)(2,1)S(1)}, bf16[3,1024]{1,0:T(4,128)(2,1)S(1)}, u32[]{:S(2)}, u32[]{:S(2)}) collective-permute-start(bf16[3,1024]{1,0:T(4,128)(2,1)S(1)} %pad_maximum_fusion.4), channel_id=1, source_target_pairs={{0,4},{1,5},{2,6},{3,7},{8,12},{9,13},{10,14},{11,15},{16,20},{17,... | collective-permute-start | bytes 18440 | tf_op jit(solution)/shard_map/ppermute | solution.py:323
  82.7 105.4 %copy-start.29 = (bf16[3,1024]{1,0:T(4,128)(2,1)}, bf16[3,1024]{1,0:T(4,128)(2,1)S(1)}, u32[]{:S(2)}) copy-start(bf16[3,1024]{1,0:T(4,128)(2,1)S(1)} %collective-permute-done) | copy-start | bytes 18436
  94.8 10.9 %collective-permute-start.1 = (f32[128,768]{1,0:T(8,128)}, f32[128,768]{1,0:T(8,128)S(1)}, u32[]{:S(2)}, u32[]{:S(2)}) collective-permute-start(f32[128,768]{1,0:T(8,128)} %get-tuple-element.38), channel_id=1, source_target_pairs={{0,4},{1,5},{2,6},{3,7},{8,12},{9,13},{10,14},{11,15},{16,20},{17,... | collective-permute-start | bytes 1179656 | tf_op jit(solution)/shard_map/ppermute | solution.py:323
  151.2 10.0 %collective-permute-start.8 = (f32[128,768]{1,0:T(8,128)}, f32[128,768]{1,0:T(8,128)}, u32[]{:S(2)}, u32[]{:S(2)}) collective-permute-start(f32[128,768]{1,0:T(8,128)} %get-tuple-element.47), channel_id=1, source_target_pairs={{4,0},{5,1},{6,2},{7,3},{12,8},{13,9},{14,10},{15,11},{20,16},{21,... | collective-permute-start | bytes 1179656 | tf_op jit(solution)/shard_map/ppermute | solution.py:323
  188.0 447.0 %reduce-scatter.6.cloned.1.call-start = ((), (), s32[]{:S(2)}) async-start(), calls=%async_computation.8 | async-start | bytes 7962624 | tf_op jit(solution)/shard_map/reduce_scatter | solution.py:587
  240.8 5.8 collective-permute-start.9
  254.5 385.6 %reduce-scatter.4.cloned.1.call-start = ((), (), s32[]{:S(2)}) async-start(), calls=%async_computation.7 | async-start | bytes 5308416 | tf_op jit(solution)/shard_map/reduce_scatter | solution.py:496
  260.6 379.5 %reduce-scatter.8.cloned.1.call-start = ((), (), s32[]{:S(2)}) async-start(), calls=%async_computation.9 | async-start | bytes 5308416 | tf_op jit(solution)/shard_map/reduce_scatter | solution.py:494
  271.6 65.1 %collective-permute-start.2 = (f32[256,1536]{1,0:T(8,128)}, f32[256,1536]{1,0:T(8,128)}, u32[]{:S(2)}, u32[]{:S(2)}) collective-permute-start(f32[256,1536]{1,0:T(8,128)} %fusion.61), channel_id=1, source_target_pairs={{0,1},{1,2},{2,3},{3,0},{4,5},{5,6},{6,7},{7,4},{8,9},{9,10},{10,1... | collective-permute-start | bytes 4718600 | tf_op jit(solution)/shard_map/ppermute | solution.py:328
  275.1 103.5 %collective-permute-start.3 = (f32[256,1536]{1,0:T(8,128)}, f32[256,1536]{1,0:T(8,128)}, u32[]{:S(2)}, u32[]{:S(2)}) collective-permute-start(f32[256,1536]{1,0:T(8,128)} %fusion.59), channel_id=1, source_target_pairs={{0,2},{1,3},{2,0},{3,1},{4,6},{5,7},{6,4},{7,5},{8,10},{9,11},{10,... | collective-permute-start | bytes 4718600 | tf_op jit(solution)/shard_map/ppermute | solution.py:328
  277.3 101.2 %collective-permute-start.4 = (f32[256,1536]{1,0:T(8,128)}, f32[256,1536]{1,0:T(8,128)}, u32[]{:S(2)}, u32[]{:S(2)}) collective-permute-start(f32[256,1536]{1,0:T(8,128)} %fusion.57), channel_id=1, source_target_pairs={{0,3},{1,0},{2,1},{3,2},{4,7},{5,4},{6,5},{7,6},{8,11},{9,8},{10,9... | collective-permute-start | bytes 4718600 | tf_op jit(solution)/shard_map/ppermute | solution.py:328
  293.4 34.5 %copy-start = (bf16[1536,1152]{1,0:T(8,128)(2,1)S(1)}, bf16[1536,1152]{1,0:T(8,128)(2,1)}, u32[]{:S(2)}) copy-start(bf16[1536,1152]{1,0:T(8,128)(2,1)} %all-gather.4.cloned.1.call-done) | copy-start | bytes 10616836
  330.7 121.3 %collective-permute-start.10 = (bf16[256,1536]{1,0:T(8,128)(2,1)S(1)}, bf16[256,1536]{1,0:T(8,128)(2,1)S(1)}, u32[]{:S(2)}, u32[]{:S(2)}) collective-permute-start(bf16[256,1536]{1,0:T(8,128)(2,1)S(1)} %fusion.4), channel_id=1, source_target_pairs={{0,1},{1,2},{2,3},{3,0},{4,5},{5,6},{6,7},{7,4},{8,9},{9,10},{10,1... | collective-permute-start | bytes 2359304 | tf_op jit(solution)/shard_map/ppermute | solution.py:328
  332.5 161.7 %collective-permute-start.11 = (bf16[256,1536]{1,0:T(8,128)(2,1)S(1)}, bf16[256,1536]{1,0:T(8,128)(2,1)S(1)}, u32[]{:S(2)}, u32[]{:S(2)}) collective-permute-start(bf16[256,1536]{1,0:T(8,128)(2,1)S(1)} %fusion.5), channel_id=1, source_target_pairs={{0,2},{1,3},{2,0},{3,1},{4,6},{5,7},{6,4},{7,5},{8,10},{9,11},{10,... | collective-permute-start | bytes 2359304 | tf_op jit(solution)/shard_map/ppermute | solution.py:328
  336.7 157.5 %collective-permute-start.12 = (bf16[256,1536]{1,0:T(8,128)(2,1)S(1)}, bf16[256,1536]{1,0:T(8,128)(2,1)S(1)}, u32[]{:S(2)}, u32[]{:S(2)}) collective-permute-start(bf16[256,1536]{1,0:T(8,128)(2,1)S(1)} %fusion.6), channel_id=1, source_target_pairs={{0,3},{1,0},{2,1},{3,2},{4,7},{5,4},{6,5},{7,6},{8,11},{9,8},{10,9... | collective-permute-start | bytes 2359304 | tf_op jit(solution)/shard_map/ppermute | solution.py:328
  339.6 154.6 %slice-start = ((s8[6291456]{0:T(1024)(128)(4,1)}), s8[4194304]{0:T(1024)(128)(4,1)S(1)}, s32[]{:S(2)}) async-start(s8[6291456]{0:T(1024)(128)(4,1)} %bitcast.44), calls=%async_computation.10 | async-start | bytes 8388608
  340.6 38.1 %copy-start.2 = (bf16[768,1536]{1,0:T(8,128)(2,1)S(1)}, bf16[768,1536]{1,0:T(8,128)(2,1)}, u32[]{:S(2)}) copy-start(bf16[768,1536]{1,0:T(8,128)(2,1)} %all-gather.8.cloned.1.call-done) | copy-start | bytes 7077892
  340.7 153.5 %slice-start.1 = ((s8[6291456]{0:T(1024)(128)(4,1)}), s8[2097152]{0:T(1024)(128)(4,1)S(1)}, s32[]{:S(2)}) async-start(s8[6291456]{0:T(1024)(128)(4,1)} %bitcast.44), calls=%async_computation.11 | async-start | bytes 4194304
  378.8 115.4 %copy-start.35 = (f32[1536]{0:T(1024)S(1)}, f32[1536]{0:T(1024)}, u32[]{:S(2)}) copy-start(f32[1536]{0:T(1024)} %param.17) | copy-start | bytes 18436
  383.3 231.4 %collective-permute-start.5 = (bf16[256,1536]{1,0:T(8,128)(2,1)}, bf16[256,1536]{1,0:T(8,128)(2,1)}, u32[]{:S(2)}, u32[]{:S(2)}) collective-permute-start(bf16[256,1536]{1,0:T(8,128)(2,1)} %get-tuple-element.128), channel_id=1, source_target_pairs={{0,1},{1,2},{2,3},{3,0},{4,5},{5,6},{6,7},{7,4},{8,9},{9,10},{10,1... | collective-permute-start | bytes 2359304 | tf_op jit(solution)/shard_map/ppermute | solution.py:328
  448.9 169.4 %collective-permute-start.6 = (bf16[256,1536]{1,0:T(8,128)(2,1)}, bf16[256,1536]{1,0:T(8,128)(2,1)}, u32[]{:S(2)}, u32[]{:S(2)}) collective-permute-start(bf16[256,1536]{1,0:T(8,128)(2,1)} %get-tuple-element.128), channel_id=1, source_target_pairs={{0,2},{1,3},{2,0},{3,1},{4,6},{5,7},{6,4},{7,5},{8,10},{9,11},{10,... | collective-permute-start | bytes 2359304 | tf_op jit(solution)/shard_map/ppermute | solution.py:328
  452.0 167.6 %collective-permute-start.7 = (bf16[256,1536]{1,0:T(8,128)(2,1)}, bf16[256,1536]{1,0:T(8,128)(2,1)}, u32[]{:S(2)}, u32[]{:S(2)}) collective-permute-start(bf16[256,1536]{1,0:T(8,128)(2,1)} %get-tuple-element.128), channel_id=1, source_target_pairs={{0,3},{1,0},{2,1},{3,2},{4,7},{5,4},{6,5},{7,6},{8,11},{9,8},{10,9... | collective-permute-start | bytes 2359304 | tf_op jit(solution)/shard_map/ppermute | solution.py:328
  501.1 119.6 %collective-permute-start.13 = (bf16[256,1536]{1,0:T(8,128)(2,1)}, bf16[256,1536]{1,0:T(8,128)(2,1)}, u32[]{:S(2)}, u32[]{:S(2)}) collective-permute-start(bf16[256,1536]{1,0:T(8,128)(2,1)} %get-tuple-element.109), channel_id=1, source_target_pairs={{0,1},{1,2},{2,3},{3,0},{4,5},{5,6},{6,7},{7,4},{8,9},{9,10},{10,1... | collective-permute-start | bytes 2359304 | tf_op jit(solution)/shard_map/ppermute | solution.py:328
  521.6 102.2 %collective-permute-start.14 = (bf16[256,1536]{1,0:T(8,128)(2,1)}, bf16[256,1536]{1,0:T(8,128)(2,1)}, u32[]{:S(2)}, u32[]{:S(2)}) collective-permute-start(bf16[256,1536]{1,0:T(8,128)(2,1)} %get-tuple-element.109), channel_id=1, source_target_pairs={{0,2},{1,3},{2,0},{3,1},{4,6},{5,7},{6,4},{7,5},{8,10},{9,11},{10,... | collective-permute-start | bytes 2359304 | tf_op jit(solution)/shard_map/ppermute | solution.py:328
  614.7 19.0 %collective-permute-start.15 = (bf16[256,1536]{1,0:T(8,128)(2,1)}, bf16[256,1536]{1,0:T(8,128)(2,1)S(1)}, u32[]{:S(2)}, u32[]{:S(2)}) collective-permute-start(bf16[256,1536]{1,0:T(8,128)(2,1)} %get-tuple-element.109), channel_id=1, source_target_pairs={{0,3},{1,0},{2,1},{3,2},{4,7},{5,4},{6,5},{7,6},{8,11},{9,8},{10,9... | collective-permute-start | bytes 2359304 | tf_op jit(solution)/shard_map/ppermute | solution.py:328
  (48 other events, 346.8 us)
Sparse Core Ops, SparseCore 0:
  9.6 26.7 all-gather.5
  38.6 30.7 all-gather.3
  70.9 24.0 all-gather.7
  188.2 48.2 all-reduce.9
  254.6 64.3 reduce-scatter.5
  322.9 53.7 reduce-scatter.3
  380.8 53.7 reduce-scatter.7

commit v2 on v1

--- a/solution.py
+++ b/solution.py
@@ -6,6 +6,7 @@
 from jax.experimental import pallas as pl
 from jax.experimental.pallas import tpu as pltpu
 from jax.sharding import PartitionSpec as P
+
 
 HEADS = 48
 HEAD_DIM = 64
@@ -323,11 +324,6 @@
     return lax.ppermute(value, axis, pairs)
 
 
-def rotated(value, axis, by):
-    length = lax.axis_size(axis)
-    return lax.ppermute(value, axis, [(i, (i + by) % length) for i in range(length)])
-
-
 def chain(local, decay, axis, by):
     got = None
     for _ in range(lax.axis_size(axis) - 1):
@@ -335,11 +331,64 @@
     return jnp.zeros_like(local) if got is None else got
 
 
-def row_block(shape, index):
-    return pl.BlockSpec(shape, index)
-
-
-def shards(
+class Ring:
+    def __init__(self, axis):
+        self.axis = axis
+        self.size = lax.axis_size(axis)
+        self.me = lax.axis_index(axis)
+        self.paired = self.size & (self.size - 1) == 0
+
+    def target(self, m):
+        return self.me ^ m if self.paired else (self.me + m) % self.size
+
+    def source(self, m):
+        return self.me ^ m if self.paired else (self.me - m) % self.size
+
+    def send(self, value, m):
+        pairs = [(i, i ^ m if self.paired else (i + m) % self.size) for i in range(self.size)]
+        return lax.ppermute(value, self.axis, pairs)
+
+    def gather(self, value):
+        if not self.paired:
+            return lax.all_gather(value, self.axis, axis=0, tiled=True)
+        pieces, step = {0: value}, self.size // 2
+        while step:
+            pieces.update({m | step: self.send(piece, step) for m, piece in pieces.items()})
+            step //= 2
+        rows = value.shape[0]
+        full = jnp.zeros((rows * self.size,) + value.shape[1:], value.dtype)
+        for m, piece in pieces.items():
+            full = lax.dynamic_update_slice_in_dim(full, piece, self.source(m) * rows, 0)
+        return full
+
+    def sum_pieces(self, piece):
+        if self.size != 4:
+            got = [self.send(piece(m).astype(bf16), m) for m in range(1, self.size)]
+            total = piece(0)
+            for value in got:
+                total = total + value.astype(f32)
+            return total
+        far = piece(3).astype(bf16)
+        handed = lax.ppermute(far, self.axis, [(0, 1), (3, 2)])
+        middle = lax.ppermute(far, self.axis, [(1, 2), (2, 1)])
+        near = self.send(piece(1).astype(bf16), 1)
+        across = self.send((piece(2) + handed.astype(f32)).astype(bf16), 2)
+        total = piece(0)
+        for value in (middle, near, across):
+            total = total + value.astype(f32)
+        return total
+
+    def all_pieces(self, own):
+        if self.size != 4:
+            return [own] + [self.send(own, m) for m in range(1, self.size)]
+        across = self.send(own, 2)
+        near = self.send(own, 1)
+        middle = lax.ppermute(own, self.axis, [(1, 2), (2, 1)])
+        handed = lax.ppermute(across, self.axis, [(1, 0), (2, 3)])
+        return [own, near, across, middle + handed]
+
+
+def body(
     block_input,
     norm_gain,
     w_z,
@@ -362,16 +411,20 @@
     heads = w_dt.shape[1]
     wide = inner + 2 * STATE
     inner_width = HEADS * HEAD_DIM
-    ranks = lax.axis_size("tensor")
-    me = lax.axis_index("tensor")
+    line = Ring("tensor")
+    ranks = line.size
     quarter = length // ranks
     rows = min(SPAN, length)
     count = length // rows
 
     w_cat = jnp.concatenate([w_x, jnp.pad(w_dt, ((0, 0), (0, LANES - heads))), w_bc], axis=1)
-    full_cat = lax.all_gather(w_cat, "shard", axis=0, tiled=True)
-    full_z = lax.all_gather(w_z, "shard", axis=0, tiled=True)
-    full_out = lax.all_gather(w_out, "shard", axis=1, tiled=True)
+    ring = Ring("shard")
+    w_out_t = w_out.T
+    full_cat = ring.gather(w_cat)
+    others = [line.send(w_out_t, m) for m in range(1, ranks)]
+    full_z = ring.gather(w_z)
+    full_out = ring.gather(w_out_t)
+    full_others = ring.gather(jnp.concatenate(others, axis=1))
 
     x_float = block_input.astype(f32)
     inverse = lax.rsqrt(jnp.mean(x_float * x_float, axis=1, keepdims=True) + epsilon)
@@ -438,7 +491,7 @@
     decay = jnp.repeat(jnp.exp(totals[0, :heads]), HEAD_DIM)[None, :]
     s_in = chain(s_local, decay, "context", 1)
 
-    ggo = jnp.einsum("td,kd->tk", out_cotangent, full_out, preferred_element_type=f32)
+    ggo = jnp.dot(out_cotangent, full_out, preferred_element_type=f32)
     mixer, enter, leave, sums = pl.pallas_call(
         forward_kernel,
         grid=(count,),
@@ -476,20 +529,10 @@
     )(mixer, z_part, ggo, sums, act, cum, gain_row, spread_mat)
     carried = chain(own, decay, "context", -1)
 
-    def block(value, k):
-        return lax.dynamic_slice_in_dim(value, ((me + k) % ranks) * quarter, quarter)
-
-    out_own = jnp.dot(block(gated_out, 0), full_out, preferred_element_type=f32)
-    for k in range(1, ranks):
-        part = jnp.dot(block(gated_out, k), full_out, preferred_element_type=f32)
-        out_own = out_own + rotated(part, "tensor", k)
-    block_own = (block(block_input, 0).astype(f32) + out_own).astype(bf16)
-    block_output = jnp.zeros((length, width), bf16)
-    for k in range(ranks):
-        piece = block_own if k == 0 else rotated(block_own, "tensor", k)
-        block_output = lax.dynamic_update_slice_in_dim(
-            block_output, piece, ((me - k) % ranks) * quarter, 0
-        )
+    def block(value, rank):
+        return lax.dynamic_slice_in_dim(value, rank * quarter, quarter)
+
+    mixed = [line.send(block(gated_out, line.target(m)), m) for m in range(1, ranks)]
     grad_w_out = jnp.einsum("tk,td->kd", gated_out, out_cotangent, preferred_element_type=f32)
     summed_out = lax.psum_scatter(grad_w_out, ("shard", "context"), scatter_dimension=1, tiled=True)
     grad_w_z = jnp.einsum("td,tk->dk", normed, grad_z, preferred_element_type=f32)
@@ -518,19 +561,24 @@
     )(gm, act, pre, step, cum, mixer, enter, leave, carried, x_raw, conv_x_weight, d_row, rate_row,
       spread_mat, gather_mat, upper2)
 
-    dbc = lax.psum(dbc, "tensor")
+    got = [line.send(block(dbc, line.target(m)), m) for m in range(1, ranks)]
+    bc_own = block(dbc, line.me)
+    for value in got:
+        bc_own = bc_own + value
+    pieces = line.all_pieces(bc_own)
+    for m in range(ranks):
+        dbc = lax.dynamic_update_slice_in_dim(dbc, pieces[m], line.source(m) * quarter, 0)
     pre_bc = pre[:, inner:]
     grad_pre_bc = dbc * slope_of(pre_bc, jax.nn.sigmoid(pre_bc))
-    next_head = shifted(
-        jnp.concatenate([pre_head[: CONV - 1], grad_pre_bc[: CONV - 1]], axis=1), "context", -1
-    )
+    next_head = shifted(pre_head[: CONV - 1], "context", -1)
+    next_bc_head = shifted(grad_pre_bc[: CONV - 1], "context", -1)
     after = jnp.pad(next_head, ((CONV - 1, CONV - 1), (0, 0)))
-    reach = jnp.zeros((CONV - 1, wide), f32)
+    reach = jnp.zeros((CONV - 1, inner), f32)
     for k in range(CONV):
-        reach = reach + conv_weight[k] * after[CONV - 1 - k : 2 * (CONV - 1) - k]
-    gx_last = (gx_tail + jnp.pad(reach[:, :inner], ((8 - CONV + 1, 0), (0, 0)))).astype(bf16)
+        reach = reach + conv_x_weight[k] * after[CONV - 1 - k : 2 * (CONV - 1) - k]
+    gx_last = (gx_tail + jnp.pad(reach, ((8 - CONV + 1, 0), (0, 0)))).astype(bf16)
     gx = lax.dynamic_update_slice_in_dim(gx, gx_last, length - 8, 0)
-    bc_pad = jnp.concatenate([grad_pre_bc, next_head[:, inner:]], axis=0)
+    bc_pad = jnp.concatenate([grad_pre_bc, next_bc_head], axis=0)
     gbc = jnp.zeros((length, 2 * STATE), f32)
     for k in range(CONV):
         gbc = gbc + conv_bc_weight[k] * bc_pad[CONV - 1 - k : CONV - 1 - k + length]
@@ -554,31 +602,45 @@
     g_xdt = jnp.concatenate([gx, g_dt], axis=1)
     full_xdt = full_cat[:, : inner + LANES]
 
-    def partial_of(k):
-        return jnp.einsum("tk,dk->td", block(grad_z, k), full_z, preferred_element_type=f32) + jnp.einsum(
-            "tk,dk->td", block(g_xdt, k), full_xdt, preferred_element_type=f32
+    def partial_of(m):
+        rank = line.target(m)
+        return jnp.einsum("tk,dk->td", block(grad_z, rank), full_z, preferred_element_type=f32) + jnp.einsum(
+            "tk,dk->td", block(g_xdt, rank), full_xdt, preferred_element_type=f32
         )
 
-    received = [rotated(partial_of(k).astype(bf16), "tensor", k) for k in range(1, ranks)]
-    gn = partial_of(0) + jnp.einsum(
-        "tk,dk->td", block(gbc, 0), full_cat[:, inner + LANES :], preferred_element_type=f32
-    )
-    for piece in received:
-        gn = gn + piece.astype(f32)
-    x_own, inv_own = block(x_float, 0), block(inverse, 0)
+    gn = line.sum_pieces(partial_of)
+    gn = gn + jnp.einsum(
+        "tk,dk->td", block(gbc, line.me), full_cat[:, inner + LANES :], preferred_element_type=f32
+    )
+
+    out_own = jnp.einsum("tk,dk->td", block(gated_out, line.me), full_out, preferred_element_type=f32)
+    if ranks > 1:
+        out_own = out_own + jnp.einsum(
+            "tk,dk->td", jnp.concatenate(mixed, axis=1), full_others, preferred_element_type=f32
+        )
+    block_own = (block(block_input, line.me).astype(f32) + out_own).astype(bf16)
+    pieces = line.all_pieces(block_own)
+    block_output = jnp.zeros((length, width), bf16)
+    for m in range(ranks):
+        block_output = lax.dynamic_update_slice_in_dim(
+            block_output, pieces[m], line.source(m) * quarter, 0
+        )
+
+    x_own, inv_own = block(x_float, line.me), block(inverse, line.me)
     scaled = norm_gain * gn
     delta = inv_own * scaled - x_own * (inv_own * inv_own * inv_own) * jnp.mean(
         scaled * x_own, axis=1, keepdims=True
     )
     delta = delta.astype(bf16)
     grad_norm_gain = jnp.sum(gn * x_own * inv_own, axis=0)
+    pieces = line.all_pieces(delta)
     input_grad = jnp.zeros((length, width), f32)
-    for k in range(ranks):
-        piece = delta if k == 0 else rotated(delta, "tensor", k)
+    for m in range(ranks):
+        rank = line.source(m)
         input_grad = lax.dynamic_update_slice_in_dim(
             input_grad,
-            block(out_cotangent, -k).astype(f32) + piece.astype(f32),
-            ((me - k) % ranks) * quarter,
+            block(out_cotangent, rank).astype(f32) + pieces[m].astype(f32),
+            rank * quarter,
             0,
         )
 
@@ -596,8 +658,16 @@
         ],
         axis=1,
     )
-    packed = lax.psum(packed, ("shard", "context"))
-    sum_norm_gain = lax.psum(grad_norm_gain, ("shard", "context", "tensor"))
+    wide_lanes = packed.shape[1]
+    spare = (-width) % wide_lanes
+    gain_rows = jnp.pad(grad_norm_gain, (0, spare)).reshape(-1, wide_lanes)
+    packed = lax.psum(jnp.concatenate([packed, gain_rows], axis=0), ("shard", "context"))
+    gain_rows = packed[8:]
+    parts = [gain_rows] + [line.send(gain_rows, m) for m in range(1, ranks)]
+    ordered = jnp.zeros((ranks,) + gain_rows.shape, f32)
+    for m in range(ranks):
+        ordered = lax.dynamic_update_slice_in_dim(ordered, parts[m][None], line.source(m), 0)
+    sum_norm_gain = jnp.sum(ordered, axis=0).reshape(-1)[:width]
     return (
         block_output,
         input_grad,
@@ -655,4 +725,4 @@
         P("tensor"),
         P("tensor"),
     )
-    return jax.shard_map(shards, mesh=mesh, in_specs=in_specs, out_specs=out_specs, check_vma=False)
+    return jax.shard_map(body, mesh=mesh, in_specs=in_specs, out_specs=out_specs, check_vma=False)

time: 649 us -> 590 us (0.909); the launches traced: 647 us -> 579 us
  blocking collectives: 135 us -> 46 us
  local copies, waits for them, and re-layouts: 29.7 us -> 86.8 us
  starting transfers between devices: 110 us -> 82.4 us
  waiting for transfers between devices: 194 us -> 178 us
    psum x3 -> x2, blocking collectives: 135 us -> 46 us  [the longest x1 25.5 us: body(): lax.psum(jnp.concatenate([packed, gain_rows], axis=0), ('shard', 'context'))]
    ppermute x12 -> x40, waiting for transfers between devices: 87.4 us -> 167 us  [the longest x32 133 us: send(): return lax.ppermute(value, self.axis, pairs)]
    psum x1 -> x0, waiting for transfers between devices: 47.5 us -> none  [shards(): dbc = lax.psum(dbc, 'tensor')]
    all_gather x3 -> x0, waiting for transfers between devices: 45.7 us -> none  [the longest x1 26.9 us: shards(): full_cat = lax.all_gather(w_cat, 'shard', axis=0, tiled=True)]
    dynamic_update_slice x3 -> x23, local copies, waits for them, and re-layouts: 3.73 us -> 35.9 us  [the longest x15 30.3 us: gather(): lax.dynamic_update_slice_in_dim(full, piece, self.source(m) * rows, 0)]
    ppermute x12 -> x40, starting transfers between devices: 102 us -> 70.3 us  [the longest x32 46.7 us: send(): return lax.ppermute(value, self.axis, pairs)]
    broadcast_in_dim x7 -> x10, local copies, waits for them, and re-layouts: 3.32 us -> 11 us  [the longest x2 3.63 us: gather(): full = jnp.zeros((rows * self.size,) + value.shape[1:], value.dtype)]
    dot_general x19 -> x17, matrix products: 63.8 us -> 69.3 us  [the longest x4 12.7 us: partial_of(): jnp.einsum('tk,dk->td', block(grad_z, rank), full_z, preferred_element_ty...]
  transfers between devices with their start and end apart: 23 -> 48, of which waited for: 9 -> 19; matrix products, arithmetic and copies ran while one was open for 17% -> 29% of each run, Pallas kernels for 2% -> 0%
where the time goes in v2:
time: 590 us; the launch traced here: 579 us
  waiting for transfers between devices  178 us (30%)
  local copies, waits for them, and re-layouts  86.8 us (15%)
  starting transfers between devices  82.4 us (14%)
  matrix products  69.3 us (12%)
  Pallas kernels  62.8 us (11%)
  blocking collectives  46 us (8%)
  other arithmetic  39.6 us (7%)
  between operations  14.8 us (3%)
    ppermute x32, waiting for transfers between devices, send(): return lax.ppermute(value, self.axis, pairs)  133 us
    ppermute x32, starting transfers between devices, send(): return lax.ppermute(value, self.axis, pairs)  46.7 us
    dynamic_update_slice x15, local copies, waits for them, and re-layouts, gather(): lax.dynamic_update_slice_in_dim(full, piece, self.source(m) * rows, 0)  30.3 us
    ppermute x3, waiting for transfers between devices, all_pieces(): handed = lax.ppermute(across, self.axis, [(1, 0), (2, 3)])  26.9 us
    pallas_call x1, Pallas kernels, body(): pl.pallas_call(backward_kernel, grid=(count,), in_specs=[back(inner), bac...  26.9 us
    psum x1, blocking collectives, body(): lax.psum(jnp.concatenate([packed, gain_rows], axis=0), ('shard', 'context'))  25.5 us
    psum x1, blocking collectives, body(): sums = lax.psum(sums, 'tensor')  20.5 us
    ppermute x1, starting transfers between devices, sum_pieces(): handed = lax.ppermute(far, self.axis, [(0, 1), (3, 2)])  15.9 us
  transfers between devices with their start and end apart: 48, of which 19 were waited for; matrix products, arithmetic and copies ran while one was open for 29% of the time, Pallas kernels for 0%

profile of v2, /device:TPU:0, one launch (start us, length us, event | category | flops | bytes accessed | tf_op | source)
XLA Modules:
  0.0 579.4 jit_solution(7288820116216106290)
XLA Ops:
  50.9 4.6 collective-permute-done
  64.3 7.1 %fusion.94.z_ref = f32[1024,768]{1,0:T(8,128)} fusion(bf16[1536,768]{0,1:T(8,128)(2,1)} %constant_dynamic-update-slice_fusion.19, f32[1536]{0:T(1024)S(1)} %copy-done.31, f32[1024]{0:T(1024)S(1)} %copy-done.42, bf16[1024,1536]{1,0:T(8,128)(2,1)} %param.16), kind=kOutput, calls=%fused_computation.208 | convolution fusion | flops 2422210560 | bytes 8660992 | tf_op jit(solution)/shard_map/dot_general | solution.py:436
  72.7 4.3 fusion.99
  85.0 11.5 %front.1 = (f32[1024,1024]{1,0:T(8,128)}, f32[1024,1024]{1,0:T(8,128)}, f32[1024,128]{1,0:T(8,128)}, f32[128,768]{1,0:T(8,128)}, f32[8,128]{1,0:T(8,128)}) custom-call(bf16[1024,768]{1,0:T(8,128)(2,1)} %slice.207.x_ref.x_raw_ref, bf16[1024,256]{1,0:T(8,128)(2,1)} %get-tuple-element.117.bc_ref, f32[8,1024]{1,0:T(8,128)} %pad.35.edge_ref, ...), custom_call_target="tpu_custom_call" | custom-call | tf_op jit(solution)/shard_map/front/pallas_call | solution.py:475
  96.4 4.4 collective-permute-start.10
  100.8 6.9 %convolution_bitcast_fusion.ggo_ref = f32[1024,768]{1,0:T(8,128)} fusion(bf16[1536,768]{0,1:T(8,128)(2,1)} %constant_dynamic-update-slice_fusion.15, bf16[1024,1536]{1,0:T(8,128)(2,1)} %param.31), kind=kOutput, calls=%fused_computation.29 | convolution fusion | flops 2415919104 | bytes 8650752 | tf_op jit(solution)/shard_map/dot_general | solution.py:494
  107.8 13.5 %forward.1 = (f32[1024,768]{1,0:T(8,128)}, f32[1024,768]{1,0:T(8,128)}, f32[1024,768]{1,0:T(8,128)}, f32[8,1024]{1,0:T(8,128)}) custom-call(f32[1024,1024]{1,0:T(8,128)} %get-tuple-element.36.act_ref, f32[1024,128]{1,0:T(8,128)} %compare_select_fusion.step_ref, f32[1024,128]{1,0:T(8,128)} %get-tuple-element.37.cum_ref, f32[1024,768]{1,0:T(8,128)} %fusion.94.z_ref, ...), custom_call_target="tpu_custom_call" | custom-call | tf_op jit(solution)/shard_map/forward/pallas_call | solution.py:495
  121.3 20.5 %psum.14.sums_ref = f32[8,1024]{1,0:T(8,128)} all-reduce(f32[8,1024]{1,0:T(8,128)} %get-tuple-element.40), channel_id=1, replica_groups=mesh['shard'=4,'context'=2,'tensor'=4] {'tensor'}, use_global_device_ids=true, to_apply=%region_1.2 | all-reduce | flops 8192 | bytes 65536 | tf_op jit(solution)/shard_map/psum | solution.py:512
  141.8 11.0 %gate.1 = (bf16[1024,768]{1,0:T(8,128)(2,1)}, f32[1024,768]{1,0:T(8,128)}, bf16[1024,768]{1,0:T(8,128)(2,1)}, f32[128,768]{1,0:T(8,128)}, f32[8,768]{1,0:T(8,128)}) custom-call(f32[1024,768]{1,0:T(8,128)} %get-tuple-element.39.mixer_ref, f32[1024,768]{1,0:T(8,128)} %fusion.94.z_ref, f32[1024,768]{1,0:T(8,128)} %convolution_bitcast_fusion.ggo_ref, ...), custom_call_target="tpu_custom_call" | custom-call | tf_op jit(solution)/shard_map/gate/pallas_call | solution.py:514
  156.6 6.2 %collective-permute-done.24.carried_ref = f32[128,768]{1,0:T(8,128)} collective-permute-done((f32[128,768]{1,0:T(8,128)}, f32[128,768]{1,0:T(8,128)}, u32[]{:S(2)}, u32[]{:S(2)}) %collective-permute-start.24) | collective-permute-done | bytes 393248 | tf_op jit(solution)/shard_map/ppermute | solution.py:324
  162.8 26.9 %backward.1 = (bf16[1024,768]{1,0:T(8,128)(2,1)}, f32[8,768]{1,0:T(8,128)}, f32[8,768]{1,0:T(8,128)}, f32[1024,256]{1,0:T(8,128)}, f32[1024,128]{1,0:T(8,128)}, /*index=5*/f32[8,768]{1,0:T(8,128)}, f32[8,128]{1,0:T(8,128)}) custom-call(f32[1024,768]{1,0:T(8,128)} %get-tuple-element.43.gm_ref, f32[1024,1024]{1,0:T(8,128)} %get-tuple-element.36.act_ref, ...), custom_call_target="tpu_custom_call" | custom-call | tf_op jit(solution)/shard_map/backward/pallas_call | solution.py:541
  196.1 6.0 %collective-permute-done.30 = f32[256,256]{1,0:T(8,128)} collective-permute-done((f32[256,256]{1,0:T(8,128)}, f32[256,256]{1,0:T(8,128)}, u32[]{:S(2)}, u32[]{:S(2)}) %collective-permute-start.30) | collective-permute-done | bytes 262176 | tf_op jit(solution)/shard_map/ppermute | solution.py:349
  202.1 6.8 %collective-permute-done.31 = f32[256,256]{1,0:T(8,128)} collective-permute-done((f32[256,256]{1,0:T(8,128)}, f32[256,256]{1,0:T(8,128)}, u32[]{:S(2)}, u32[]{:S(2)}) %collective-permute-start.31) | collective-permute-done | bytes 262176 | tf_op jit(solution)/shard_map/ppermute | solution.py:349
  220.4 5.2 collective-permute-done.34
  229.3 4.6 collective-permute-done.36
  244.8 6.6 %fusion.9 = f32[1536,1152]{1,0:T(8,128)} fusion(bf16[1024,256]{1,0:T(8,128)(2,1)S(1)} %fusion.42, bf16[1024,128]{1,0:T(8,128)(2,1)S(1)} %get-tuple-element.110, bf16[1024,768]{1,0:T(8,128)(2,1)S(1)} %constant_dynamic-update-slice_fusion.6, f32[1536]{0:T(1024)S(1)} %copy-done.32, f32[1024]{0:T(1024)S(1)} %copy-done.43, bf16[1024,1536]{1,0:T(8,128)(2,1)S(1)} %copy-done.5), kind=kOutput, calls=%fused_computation.23 | convolution fusion | flops 3637248000 | bytes 12593152 | tf_op jit(solution)/shard_map/td,tk->dk/dot_general | solution.py:648
  251.7 7.4 %fusion.93 = f32[1536,768]{1,0:T(8,128)} fusion(bf16[1024,768]{1,0:T(8,128)(2,1)} %get-tuple-element.42, f32[1536]{0:T(1024)S(1)} %copy-done.32, f32[1024]{0:T(1024)S(1)} %copy-done.43, bf16[1024,1536]{1,0:T(8,128)(2,1)} %param.16), kind=kOutput, calls=%fused_computation.207 | convolution fusion | flops 2422210560 | bytes 9447424 | tf_op jit(solution)/shard_map/td,tk->dk/dot_general | solution.py:538
  263.6 16.8 %collective-permute-done.14 = bf16[384,768]{0,1:T(8,128)(2,1)S(1)} collective-permute-done((bf16[384,768]{0,1:T(8,128)(2,1)}, bf16[384,768]{0,1:T(8,128)(2,1)S(1)}, u32[]{:S(2)}, u32[]{:S(2)}) %collective-permute-start.14) | collective-permute-done | bytes 589856 | tf_op jit(solution)/shard_map/ppermute | solution.py:349
  281.3 20.7 %collective-permute-done.15 = bf16[384,768]{0,1:T(8,128)(2,1)S(1)} collective-permute-done((bf16[384,768]{0,1:T(8,128)(2,1)}, bf16[384,768]{0,1:T(8,128)(2,1)S(1)}, u32[]{:S(2)}, u32[]{:S(2)}) %collective-permute-start.15) | collective-permute-done | bytes 589856 | tf_op jit(solution)/shard_map/ppermute | solution.py:349
  318.3 7.6 %collective-permute-start.11 = (bf16[256,768]{1,0:T(8,128)(2,1)}, bf16[256,768]{1,0:T(8,128)(2,1)}, u32[]{:S(2)}, u32[]{:S(2)}) collective-permute-start(bf16[256,768]{1,0:T(8,128)(2,1)} %get-tuple-element.118), channel_id=1, source_target_pairs={{0,1},{1,0},{2,3},{3,2},{4,5},{5,4},{6,7},{7,6},{8,9},{9,8},{10,11... | collective-permute-start | bytes 1179656 | tf_op jit(solution)/shard_map/ppermute | solution.py:349
  328.2 4.5 fusion.100
  332.8 10.9 %collective-permute-done.17 = bf16[384,2304]{0,1:T(8,128)(2,1)} collective-permute-done((bf16[384,2304]{0,1:T(8,128)(2,1)}, bf16[384,2304]{0,1:T(8,128)(2,1)}, u32[]{:S(2)}, u32[]{:S(2)}) %collective-permute-start.17) | collective-permute-done | bytes 1769504 | tf_op jit(solution)/shard_map/ppermute | solution.py:349
  356.9 15.9 %collective-permute-start.28 = (bf16[256,1536]{1,0:T(8,128)(2,1)}, bf16[256,1536]{1,0:T(8,128)(2,1)}, u32[]{:S(2)}, u32[]{:S(2)}) collective-permute-start(bf16[256,1536]{1,0:T(8,128)(2,1)} %fusion.7), channel_id=1, source_target_pairs={{0,1},{3,2},{4,5},{7,6},{8,9},{11,10},{12,13},{15,14},{16,17},{19,... | collective-permute-start | bytes 2359304 | tf_op jit(solution)/shard_map/ppermute | solution.py:372
  382.8 6.8 %collective-permute-done.28 = bf16[256,1536]{1,0:T(8,128)(2,1)} collective-permute-done((bf16[256,1536]{1,0:T(8,128)(2,1)}, bf16[256,1536]{1,0:T(8,128)(2,1)}, u32[]{:S(2)}, u32[]{:S(2)}) %collective-permute-start.28) | collective-permute-done | bytes 786464 | tf_op jit(solution)/shard_map/ppermute | solution.py:372
  393.7 5.6 collective-permute-start.27
  402.5 5.7 fusion.25
  415.6 6.7 %collective-permute-done.27 = bf16[256,1536]{1,0:T(8,128)(2,1)S(1)} collective-permute-done((bf16[256,1536]{1,0:T(8,128)(2,1)S(1)}, bf16[256,1536]{1,0:T(8,128)(2,1)S(1)}, u32[]{:S(2)}, u32[]{:S(2)}) %collective-permute-start.27) | collective-permute-done | bytes 786464 | tf_op jit(solution)/shard_map/ppermute | solution.py:349
  422.3 25.5 %collective-permute-done.29 = bf16[256,1536]{1,0:T(8,128)(2,1)S(1)} collective-permute-done((bf16[256,1536]{1,0:T(8,128)(2,1)S(1)}, bf16[256,1536]{1,0:T(8,128)(2,1)S(1)}, u32[]{:S(2)}, u32[]{:S(2)}) %collective-permute-start.29) | collective-permute-done | bytes 786464 | tf_op jit(solution)/shard_map/ppermute | solution.py:349
  455.3 25.5 %psum.15 = f32[10,1024]{1,0:T(8,128)S(1)} all-reduce(f32[10,1024]{1,0:T(8,128)S(1)} %pad_maximum_fusion.2), channel_id=1, replica_groups=mesh['shard'=4,'context'=2,'tensor'=4] {'shard','context'}, use_global_device_ids=true, to_apply=%region_17.18 | all-reduce | flops 10240 | bytes 81920 | tf_op jit(solution)/shard_map/psum | solution.py:664
  508.0 27.3 %collective-permute-done.39 = bf16[256,1536]{1,0:T(8,128)(2,1)} collective-permute-done((bf16[256,1536]{1,0:T(8,128)(2,1)}, bf16[256,1536]{1,0:T(8,128)(2,1)}, u32[]{:S(2)}, u32[]{:S(2)}) %collective-permute-start.39) | collective-permute-done | bytes 786464 | tf_op jit(solution)/shard_map/ppermute | solution.py:349
  541.6 8.8 %collective-permute-done.23 = bf16[256,1536]{1,0:T(8,128)(2,1)S(1)} collective-permute-done((bf16[256,1536]{1,0:T(8,128)(2,1)}, bf16[256,1536]{1,0:T(8,128)(2,1)S(1)}, u32[]{:S(2)}, u32[]{:S(2)}) %collective-permute-start.23) | collective-permute-done | bytes 786464 | tf_op jit(solution)/shard_map/ppermute | solution.py:387
  552.6 13.5 %collective-permute-done.41 = bf16[256,1536]{1,0:T(8,128)(2,1)S(1)} collective-permute-done((bf16[256,1536]{1,0:T(8,128)(2,1)}, bf16[256,1536]{1,0:T(8,128)(2,1)S(1)}, u32[]{:S(2)}, u32[]{:S(2)}) %collective-permute-start.41) | collective-permute-done | bytes 786464 | tf_op jit(solution)/shard_map/ppermute | solution.py:387
  (311 shorter events, 209.5 us)
Async XLA Ops:
  7.2 560.4 %reduce-scatter.6.cloned.1.call-start = ((), (), s32[]{:S(2)}) async-start(), calls=%async_computation.4 | async-start | bytes 7962624 | tf_op jit(solution)/shard_map/reduce_scatter | solution.py:649
  7.2 32.9 %collective-permute-start.7 = (bf16[384,768]{0,1:T(8,128)(2,1)}, bf16[384,768]{0,1:T(8,128)(2,1)}, u32[]{:S(2)}, u32[]{:S(2)}) collective-permute-start(bf16[384,768]{0,1:T(8,128)(2,1)} %bitcast.51), channel_id=1, source_target_pairs={{0,16},{8,24},{16,0},{24,8},{1,17},{9,25},{17,1},{25,9},{2,18},{10... | collective-permute-start | bytes 1769480 | tf_op jit(solution)/shard_map/ppermute | solution.py:349
  10.3 38.6 %collective-permute-start.8 = (bf16[384,768]{0,1:T(8,128)(2,1)}, bf16[384,768]{0,1:T(8,128)(2,1)}, u32[]{:S(2)}, u32[]{:S(2)}) collective-permute-start(bf16[384,768]{0,1:T(8,128)(2,1)} %bitcast.52), channel_id=1, source_target_pairs={{0,8},{8,0},{16,24},{24,16},{1,9},{9,1},{17,25},{25,17},{2,10},{10... | collective-permute-start | bytes 1769480 | tf_op jit(solution)/shard_map/ppermute | solution.py:349
  10.3 27.1 %collective-permute-start.4 = (bf16[384,768]{1,0:T(8,128)(2,1)}, bf16[384,768]{1,0:T(8,128)(2,1)}, u32[]{:S(2)}, u32[]{:S(2)}) collective-permute-start(bf16[384,768]{1,0:T(8,128)(2,1)} %param.18), channel_id=1, source_target_pairs={{0,16},{8,24},{16,0},{24,8},{1,17},{9,25},{17,1},{25,9},{2,18},{10... | collective-permute-start | bytes 1769480 | tf_op jit(solution)/shard_map/ppermute | solution.py:349
  10.4 30.2 %collective-permute-start.5 = (bf16[384,768]{1,0:T(8,128)(2,1)}, bf16[384,768]{1,0:T(8,128)(2,1)}, u32[]{:S(2)}, u32[]{:S(2)}) collective-permute-start(bf16[384,768]{1,0:T(8,128)(2,1)} %param.18), channel_id=1, source_target_pairs={{0,8},{8,0},{16,24},{24,16},{1,9},{9,1},{17,25},{25,17},{2,10},{10... | collective-permute-start | bytes 1769480 | tf_op jit(solution)/shard_map/ppermute | solution.py:349
  15.5 40.1 %collective-permute-start = (bf16[384,1152]{1,0:T(8,128)(2,1)}, bf16[384,1152]{1,0:T(8,128)(2,1)}, u32[]{:S(2)}, u32[]{:S(2)}) collective-permute-start(bf16[384,1152]{1,0:T(8,128)(2,1)} %get-tuple-element.124), channel_id=1, source_target_pairs={{0,16},{8,24},{16,0},{24,8},{1,17},{9,25},{17,1},{25,9},{2,18},{10... | collective-permute-start | bytes 2654216 | tf_op jit(solution)/shard_map/ppermute | solution.py:349
  37.4 19.4 %collective-permute-start.1 = (bf16[384,1152]{1,0:T(8,128)(2,1)}, bf16[384,1152]{1,0:T(8,128)(2,1)}, u32[]{:S(2)}, u32[]{:S(2)}) collective-permute-start(bf16[384,1152]{1,0:T(8,128)(2,1)} %get-tuple-element.124), channel_id=1, source_target_pairs={{0,8},{8,0},{16,24},{24,16},{1,9},{9,1},{17,25},{25,17},{2,10},{10... | collective-permute-start | bytes 2654216 | tf_op jit(solution)/shard_map/ppermute | solution.py:349
  40.2 18.0 %collective-permute-start.6 = (bf16[384,768]{1,0:T(8,128)(2,1)}, bf16[384,768]{1,0:T(8,128)(2,1)}, u32[]{:S(2)}, u32[]{:S(2)}) collective-permute-start(bf16[384,768]{1,0:T(8,128)(2,1)} %collective-permute-done.4), channel_id=1, source_target_pairs={{0,8},{8,0},{16,24},{24,16},{1,9},{9,1},{17,25},{25,17},{2,10},{10... | collective-permute-start | bytes 1769480 | tf_op jit(solution)/shard_map/ppermute | solution.py:349
  40.7 21.6 %collective-permute-start.9 = (bf16[384,768]{0,1:T(8,128)(2,1)}, bf16[384,768]{0,1:T(8,128)(2,1)}, u32[]{:S(2)}, u32[]{:S(2)}) collective-permute-start(bf16[384,768]{0,1:T(8,128)(2,1)} %collective-permute-done.7), channel_id=1, source_target_pairs={{0,8},{8,0},{16,24},{24,16},{1,9},{9,1},{17,25},{25,17},{2,10},{10... | collective-permute-start | bytes 1769480 | tf_op jit(solution)/shard_map/ppermute | solution.py:349
  251.4 321.2 %reduce-scatter.4.cloned.1.call-start = ((), (), s32[]{:S(2)}) async-start(), calls=%async_computation.3 | async-start | bytes 5308416 | tf_op jit(solution)/shard_map/reduce_scatter | solution.py:539
  259.1 313.6 %reduce-scatter.8.cloned.1.call-start = ((), (), s32[]{:S(2)}) async-start(), calls=%async_computation.5 | async-start | bytes 5308416 | tf_op jit(solution)/shard_map/reduce_scatter | solution.py:537
  259.2 21.2 %collective-permute-start.14 = (bf16[384,768]{0,1:T(8,128)(2,1)}, bf16[384,768]{0,1:T(8,128)(2,1)S(1)}, u32[]{:S(2)}, u32[]{:S(2)}) collective-permute-start(bf16[384,768]{0,1:T(8,128)(2,1)} %bitcast.53), channel_id=1, source_target_pairs={{0,1},{1,0},{2,3},{3,2},{4,5},{5,4},{6,7},{7,6},{8,9},{9,8},{10,11... | collective-permute-start | bytes 1769480 | tf_op jit(solution)/shard_map/ppermute | solution.py:349
  259.3 42.7 %collective-permute-start.15 = (bf16[384,768]{0,1:T(8,128)(2,1)}, bf16[384,768]{0,1:T(8,128)(2,1)S(1)}, u32[]{:S(2)}, u32[]{:S(2)}) collective-permute-start(bf16[384,768]{0,1:T(8,128)(2,1)} %bitcast.54), channel_id=1, source_target_pairs={{0,2},{1,3},{2,0},{3,1},{4,6},{5,7},{6,4},{7,5},{8,10},{9,11},{10,... | collective-permute-start | bytes 1769480 | tf_op jit(solution)/shard_map/ppermute | solution.py:349
  262.3 40.6 %collective-permute-start.16 = (bf16[384,768]{0,1:T(8,128)(2,1)}, bf16[384,768]{0,1:T(8,128)(2,1)S(1)}, u32[]{:S(2)}, u32[]{:S(2)}) collective-permute-start(bf16[384,768]{0,1:T(8,128)(2,1)} %bitcast.55), channel_id=1, source_target_pairs={{0,3},{1,2},{2,1},{3,0},{4,7},{5,6},{6,5},{7,4},{8,11},{9,10},{10,... | collective-permute-start | bytes 1769480 | tf_op jit(solution)/shard_map/ppermute | solution.py:349
  303.8 40.0 %collective-permute-start.17 = (bf16[384,2304]{0,1:T(8,128)(2,1)}, bf16[384,2304]{0,1:T(8,128)(2,1)}, u32[]{:S(2)}, u32[]{:S(2)}) collective-permute-start(bf16[384,2304]{0,1:T(8,128)(2,1)} %constant_dynamic-update-slice_fusion.27), channel_id=1, source_target_pairs={{0,16},{8,24},{16,0},{24,8},{1,17},{9,25},{17,1},{25,9},{2,18},{10... | collective-permute-start | bytes 5308424 | tf_op jit(solution)/shard_map/ppermute | solution.py:349
  308.8 38.1 %collective-permute-start.18 = (bf16[384,2304]{0,1:T(8,128)(2,1)}, bf16[384,2304]{0,1:T(8,128)(2,1)}, u32[]{:S(2)}, u32[]{:S(2)}) collective-permute-start(bf16[384,2304]{0,1:T(8,128)(2,1)} %constant_dynamic-update-slice_fusion.27), channel_id=1, source_target_pairs={{0,8},{8,0},{16,24},{24,16},{1,9},{9,1},{17,25},{25,17},{2,10},{10... | collective-permute-start | bytes 5308424 | tf_op jit(solution)/shard_map/ppermute | solution.py:349
  318.3 84.2 %collective-permute-start.11 = (bf16[256,768]{1,0:T(8,128)(2,1)}, bf16[256,768]{1,0:T(8,128)(2,1)}, u32[]{:S(2)}, u32[]{:S(2)}) collective-permute-start(bf16[256,768]{1,0:T(8,128)(2,1)} %get-tuple-element.118), channel_id=1, source_target_pairs={{0,1},{1,0},{2,3},{3,2},{4,5},{5,4},{6,7},{7,6},{8,9},{9,8},{10,11... | collective-permute-start | bytes 1179656 | tf_op jit(solution)/shard_map/ppermute | solution.py:349
  325.8 76.7 %collective-permute-start.12 = (bf16[256,768]{1,0:T(8,128)(2,1)}, bf16[256,768]{1,0:T(8,128)(2,1)}, u32[]{:S(2)}, u32[]{:S(2)}) collective-permute-start(bf16[256,768]{1,0:T(8,128)(2,1)} %get-tuple-element.120), channel_id=1, source_target_pairs={{0,2},{1,3},{2,0},{3,1},{4,6},{5,7},{6,4},{7,5},{8,10},{9,11},{10,... | collective-permute-start | bytes 1179656 | tf_op jit(solution)/shard_map/ppermute | solution.py:349
  326.8 75.7 %collective-permute-start.13 = (bf16[256,768]{1,0:T(8,128)(2,1)}, bf16[256,768]{1,0:T(8,128)(2,1)}, u32[]{:S(2)}, u32[]{:S(2)}) collective-permute-start(bf16[256,768]{1,0:T(8,128)(2,1)} %get-tuple-element.119), channel_id=1, source_target_pairs={{0,3},{1,2},{2,1},{3,0},{4,7},{5,6},{6,5},{7,4},{8,11},{9,10},{10,... | collective-permute-start | bytes 1179656 | tf_op jit(solution)/shard_map/ppermute | solution.py:349
  343.7 50.0 %collective-permute-start.19 = (bf16[384,2304]{0,1:T(8,128)(2,1)}, bf16[384,2304]{0,1:T(8,128)(2,1)}, u32[]{:S(2)}, u32[]{:S(2)}) collective-permute-start(bf16[384,2304]{0,1:T(8,128)(2,1)} %collective-permute-done.17), channel_id=1, source_target_pairs={{0,8},{8,0},{16,24},{24,16},{1,9},{9,1},{17,25},{25,17},{2,10},{10... | collective-permute-start | bytes 5308424 | tf_op jit(solution)/shard_map/ppermute | solution.py:349
  356.9 32.7 %collective-permute-start.28 = (bf16[256,1536]{1,0:T(8,128)(2,1)}, bf16[256,1536]{1,0:T(8,128)(2,1)}, u32[]{:S(2)}, u32[]{:S(2)}) collective-permute-start(bf16[256,1536]{1,0:T(8,128)(2,1)} %fusion.7), channel_id=1, source_target_pairs={{0,1},{3,2},{4,5},{7,6},{8,9},{11,10},{12,13},{15,14},{16,17},{19,... | collective-permute-start | bytes 2359304 | tf_op jit(solution)/shard_map/ppermute | solution.py:372
  389.6 32.7 %collective-permute-start.26 = (bf16[256,1536]{1,0:T(8,128)(2,1)}, bf16[256,1536]{1,0:T(8,128)(2,1)S(1)}, u32[]{:S(2)}, u32[]{:S(2)}) collective-permute-start(bf16[256,1536]{1,0:T(8,128)(2,1)} %fusion.7), channel_id=1, source_target_pairs={{1,2},{2,1},{5,6},{6,5},{9,10},{10,9},{13,14},{14,13},{17,18},{18,... | collective-permute-start | bytes 2359304 | tf_op jit(solution)/shard_map/ppermute | solution.py:373
  393.7 28.6 %collective-permute-start.27 = (bf16[256,1536]{1,0:T(8,128)(2,1)S(1)}, bf16[256,1536]{1,0:T(8,128)(2,1)S(1)}, u32[]{:S(2)}, u32[]{:S(2)}) collective-permute-start(bf16[256,1536]{1,0:T(8,128)(2,1)S(1)} %copy-done.20), channel_id=1, source_target_pairs={{0,1},{1,0},{2,3},{3,2},{4,5},{5,4},{6,7},{7,6},{8,9},{9,8},{10,11... | collective-permute-start | bytes 2359304 | tf_op jit(solution)/shard_map/ppermute | solution.py:349
  402.5 45.3 %collective-permute-start.29 = (bf16[256,1536]{1,0:T(8,128)(2,1)S(1)}, bf16[256,1536]{1,0:T(8,128)(2,1)S(1)}, u32[]{:S(2)}, u32[]{:S(2)}) collective-permute-start(bf16[256,1536]{1,0:T(8,128)(2,1)S(1)} %fusion.6), channel_id=1, source_target_pairs={{0,2},{1,3},{2,0},{3,1},{4,6},{5,7},{6,4},{7,5},{8,10},{9,11},{10,... | collective-permute-start | bytes 2359304 | tf_op jit(solution)/shard_map/ppermute | solution.py:349
  412.3 89.6 %collective-permute-start.20 = (bf16[256,1536]{1,0:T(8,128)(2,1)}, bf16[256,1536]{1,0:T(8,128)(2,1)}, u32[]{:S(2)}, u32[]{:S(2)}) collective-permute-start(bf16[256,1536]{1,0:T(8,128)(2,1)} %get-tuple-element.135), channel_id=1, source_target_pairs={{0,1},{1,0},{2,3},{3,2},{4,5},{5,4},{6,7},{7,6},{8,9},{9,8},{10,11... | collective-permute-start | bytes 2359304 | tf_op jit(solution)/shard_map/ppermute | solution.py:349
  414.0 88.6 %collective-permute-start.21 = (bf16[256,1536]{1,0:T(8,128)(2,1)}, bf16[256,1536]{1,0:T(8,128)(2,1)}, u32[]{:S(2)}, u32[]{:S(2)}) collective-permute-start(bf16[256,1536]{1,0:T(8,128)(2,1)} %get-tuple-element.135), channel_id=1, source_target_pairs={{0,2},{1,3},{2,0},{3,1},{4,6},{5,7},{6,4},{7,5},{8,10},{9,11},{10,... | collective-permute-start | bytes 2359304 | tf_op jit(solution)/shard_map/ppermute | solution.py:349
  496.7 39.9 %collective-permute-start.38 = (bf16[256,1536]{1,0:T(8,128)(2,1)}, bf16[256,1536]{1,0:T(8,128)(2,1)}, u32[]{:S(2)}, u32[]{:S(2)}) collective-permute-start(bf16[256,1536]{1,0:T(8,128)(2,1)} %get-tuple-element.113), channel_id=1, source_target_pairs={{0,1},{1,0},{2,3},{3,2},{4,5},{5,4},{6,7},{7,6},{8,9},{9,8},{10,11... | collective-permute-start | bytes 2359304 | tf_op jit(solution)/shard_map/ppermute | solution.py:349
  496.7 38.6 %collective-permute-start.39 = (bf16[256,1536]{1,0:T(8,128)(2,1)}, bf16[256,1536]{1,0:T(8,128)(2,1)}, u32[]{:S(2)}, u32[]{:S(2)}) collective-permute-start(bf16[256,1536]{1,0:T(8,128)(2,1)} %get-tuple-element.113), channel_id=1, source_target_pairs={{0,2},{1,3},{2,0},{3,1},{4,6},{5,7},{6,4},{7,5},{8,10},{9,11},{10,... | collective-permute-start | bytes 2359304 | tf_op jit(solution)/shard_map/ppermute | solution.py:349
  499.7 41.9 %collective-permute-start.22 = (bf16[256,1536]{1,0:T(8,128)(2,1)}, bf16[256,1536]{1,0:T(8,128)(2,1)}, u32[]{:S(2)}, u32[]{:S(2)}) collective-permute-start(bf16[256,1536]{1,0:T(8,128)(2,1)} %get-tuple-element.135), channel_id=1, source_target_pairs={{1,2},{2,1},{5,6},{6,5},{9,10},{10,9},{13,14},{14,13},{17,18},{18,... | collective-permute-start | bytes 2359304 | tf_op jit(solution)/shard_map/ppermute | solution.py:386
  501.8 50.8 %collective-permute-start.40 = (bf16[256,1536]{1,0:T(8,128)(2,1)}, bf16[256,1536]{1,0:T(8,128)(2,1)S(1)}, u32[]{:S(2)}, u32[]{:S(2)}) collective-permute-start(bf16[256,1536]{1,0:T(8,128)(2,1)} %get-tuple-element.113), channel_id=1, source_target_pairs={{1,2},{2,1},{5,6},{6,5},{9,10},{10,9},{13,14},{14,13},{17,18},{18,... | collective-permute-start | bytes 2359304 | tf_op jit(solution)/shard_map/ppermute | solution.py:386
  502.6 47.8 %collective-permute-start.23 = (bf16[256,1536]{1,0:T(8,128)(2,1)}, bf16[256,1536]{1,0:T(8,128)(2,1)S(1)}, u32[]{:S(2)}, u32[]{:S(2)}) collective-permute-start(bf16[256,1536]{1,0:T(8,128)(2,1)} %collective-permute-done.21), channel_id=1, source_target_pairs={{1,0},{2,3},{5,4},{6,7},{9,8},{10,11},{13,12},{14,15},{17,16},{18,... | collective-permute-start | bytes 2359304 | tf_op jit(solution)/shard_map/ppermute | solution.py:387
  535.3 30.9 %collective-permute-start.41 = (bf16[256,1536]{1,0:T(8,128)(2,1)}, bf16[256,1536]{1,0:T(8,128)(2,1)S(1)}, u32[]{:S(2)}, u32[]{:S(2)}) collective-permute-start(bf16[256,1536]{1,0:T(8,128)(2,1)} %collective-permute-done.39), channel_id=1, source_target_pairs={{1,0},{2,3},{5,4},{6,7},{9,8},{10,11},{13,12},{14,15},{17,16},{18,... | collective-permute-start | bytes 2359304 | tf_op jit(solution)/shard_map/ppermute | solution.py:387
  (67 other events, 797.7 us)
Sparse Core Ops, SparseCore 0:
  251.6 76.8 reduce-scatter.5
  332.5 53.7 reduce-scatter.3
  390.3 53.7 reduce-scatter.7

commit v3 on v2

--- a/solution.py
+++ b/solution.py
@@ -4,6 +4,7 @@
 import jax.numpy as jnp
 from jax import lax
 from jax.experimental import pallas as pl
+from jax.experimental.layout import Layout, with_layout_constraint
 from jax.experimental.pallas import tpu as pltpu
 from jax.sharding import PartitionSpec as P
 
@@ -16,6 +17,9 @@
 LANES = 128
 
 epsilon = 1e-05
+SHARD = "shard"
+CONTEXT = "context"
+TENSOR = "tensor"
 f32 = jnp.float32
 bf16 = jnp.bfloat16
 
@@ -31,6 +35,10 @@
 
 def dot_t(a, b):
     return lax.dot_general(a, b, (((1,), (1,)), ((), ())), preferred_element_type=f32)
+
+
+def dot_tn(a, b):
+    return lax.dot_general(a, b, (((0,), (0,)), ((), ())), preferred_element_type=f32)
 
 
 def lhs3(parts):
@@ -348,18 +356,43 @@
         pairs = [(i, i ^ m if self.paired else (i + m) % self.size) for i in range(self.size)]
         return lax.ppermute(value, self.axis, pairs)
 
-    def gather(self, value):
+    def far(self, value):
+        if self.size == 1 or not self.paired:
+            return {0: value}
+        return {0: value, self.size // 2: self.send(value, self.size // 2)}
+
+    def near(self, pieces):
+        step = self.size // 4
+        while step and self.paired:
+            pieces = {**pieces, **{m | step: self.send(piece, step) for m, piece in pieces.items()}}
+            step //= 2
+        return pieces
+
+    def join(self, pieces):
+        value = pieces[0]
+        if self.paired:
+            rows = value.shape[0]
+            full = jnp.zeros((rows * self.size,) + value.shape[1:], value.dtype)
+            for m, piece in pieces.items():
+                full = lax.dynamic_update_slice_in_dim(full, piece, self.source(m) * rows, 0)
+        else:
+            full = lax.all_gather(value, self.axis, axis=0, tiled=True)
+        return with_layout_constraint(full, Layout((0, 1)))
+
+    def reduce_rows(self, value):
         if not self.paired:
-            return lax.all_gather(value, self.axis, axis=0, tiled=True)
-        pieces, step = {0: value}, self.size // 2
-        while step:
-            pieces.update({m | step: self.send(piece, step) for m, piece in pieces.items()})
-            step //= 2
-        rows = value.shape[0]
-        full = jnp.zeros((rows * self.size,) + value.shape[1:], value.dtype)
-        for m, piece in pieces.items():
-            full = lax.dynamic_update_slice_in_dim(full, piece, self.source(m) * rows, 0)
-        return full
+            return lax.psum_scatter(value, self.axis, scatter_dimension=0, tiled=True)
+        left, step = self.size, 1
+        rows = value.shape[0] // self.size
+        while step < self.size:
+            mine = (self.me // step) % 2
+            view = value.reshape((left // 2, 2, rows) + value.shape[1:])
+            keep = lax.dynamic_index_in_dim(view, mine, 1, keepdims=False)
+            give = lax.dynamic_index_in_dim(view, 1 - mine, 1, keepdims=False)
+            got = self.send(give, step)
+            left, step = left // 2, step * 2
+            value = (keep + got).reshape((left * rows,) + value.shape[1:])
+        return value
 
     def sum_pieces(self, piece):
         if self.size != 4:
@@ -411,20 +444,19 @@
     heads = w_dt.shape[1]
     wide = inner + 2 * STATE
     inner_width = HEADS * HEAD_DIM
-    line = Ring("tensor")
+    line = Ring(TENSOR)
     ranks = line.size
     quarter = length // ranks
     rows = min(SPAN, length)
     count = length // rows
 
     w_cat = jnp.concatenate([w_x, jnp.pad(w_dt, ((0, 0), (0, LANES - heads))), w_bc], axis=1)
-    ring = Ring("shard")
+    ring, range_ring = Ring(SHARD), Ring(CONTEXT)
     w_out_t = w_out.T
-    full_cat = ring.gather(w_cat)
+    full_cat = ring.join(ring.near(ring.far(w_cat)))
     others = [line.send(w_out_t, m) for m in range(1, ranks)]
-    full_z = ring.gather(w_z)
-    full_out = ring.gather(w_out_t)
-    full_others = ring.gather(jnp.concatenate(others, axis=1))
+    far_z = ring.far(w_z)
+    far_out = ring.far(w_out_t)
 
     x_float = block_input.astype(f32)
     inverse = lax.rsqrt(jnp.mean(x_float * x_float, axis=1, keepdims=True) + epsilon)
@@ -433,10 +465,9 @@
     x_raw = proj[:, :inner].astype(bf16)
     dt_raw = proj[:, inner : inner + LANES]
     bc_raw = proj[:, inner + LANES :].astype(bf16)
-    z_part = jnp.dot(normed, full_z, preferred_element_type=f32)
 
     edge = shifted(
-        jnp.concatenate([x_raw[length - CONV + 1 :], bc_raw[length - CONV + 1 :]], axis=1), "context", 1
+        jnp.concatenate([x_raw[length - CONV + 1 :], bc_raw[length - CONV + 1 :]], axis=1), CONTEXT, 1
     ).astype(f32)
     edge = jnp.pad(edge, ((8 - CONV + 1, 0), (0, 0)))
     conv_weight = jnp.concatenate([conv_x_weight, conv_bc_weight], axis=1)
@@ -489,8 +520,12 @@
         name="front",
     )(x_raw, bc_raw, edge, conv_weight, conv_bias, step, rate_row, spread_mat, lower2)
     decay = jnp.repeat(jnp.exp(totals[0, :heads]), HEAD_DIM)[None, :]
-    s_in = chain(s_local, decay, "context", 1)
-
+    s_in = chain(s_local, decay, CONTEXT, 1)
+    totals, far_z, far_out, others = lax.optimization_barrier((totals, far_z, far_out, others))
+    full_z = ring.join(ring.near(far_z))
+    full_out = ring.join(ring.near(far_out))
+    all_others = ring.near(ring.far(jnp.concatenate(others, axis=1)))
+    z_part = dot(normed, full_z)
     ggo = jnp.dot(out_cotangent, full_out, preferred_element_type=f32)
     mixer, enter, leave, sums = pl.pallas_call(
         forward_kernel,
@@ -509,7 +544,9 @@
         compiler_params=params,
         name="forward",
     )(act, step, cum, z_part, ggo, s_in, d_row, gain_row, spread_mat)
-    sums = lax.psum(sums, "tensor")
+    parts = [line.send(sums, m) for m in range(1, ranks)]
+    for part in parts:
+        sums = sums + part
 
     gated_out, gm, grad_z, own, gate_acc = pl.pallas_call(
         functools.partial(gate_kernel, inner_width),
@@ -527,16 +564,16 @@
         compiler_params=params,
         name="gate",
     )(mixer, z_part, ggo, sums, act, cum, gain_row, spread_mat)
-    carried = chain(own, decay, "context", -1)
+    carried = chain(own, decay, CONTEXT, -1)
 
     def block(value, rank):
         return lax.dynamic_slice_in_dim(value, rank * quarter, quarter)
 
     mixed = [line.send(block(gated_out, line.target(m)), m) for m in range(1, ranks)]
-    grad_w_out = jnp.einsum("tk,td->kd", gated_out, out_cotangent, preferred_element_type=f32)
-    summed_out = lax.psum_scatter(grad_w_out, ("shard", "context"), scatter_dimension=1, tiled=True)
-    grad_w_z = jnp.einsum("td,tk->dk", normed, grad_z, preferred_element_type=f32)
-    summed_z = lax.psum_scatter(grad_w_z, ("shard", "context"), scatter_dimension=0, tiled=True)
+    grad_w_out = dot_tn(out_cotangent, gated_out)
+    grad_w_z = dot_tn(normed, grad_z)
+    summed_out, summed_z = ring.reduce_rows(grad_w_out), ring.reduce_rows(grad_w_z)
+    summed_out, summed_z = range_ring.reduce_rows(summed_out).T, range_ring.reduce_rows(summed_z)
 
     gx, gx_tail, pre_head, dbc, gstep, conv_acc, rate_acc = pl.pallas_call(
         backward_kernel,
@@ -565,13 +602,13 @@
     bc_own = block(dbc, line.me)
     for value in got:
         bc_own = bc_own + value
-    pieces = line.all_pieces(bc_own)
+    pieces = [bc_own] + [line.send(bc_own, m) for m in range(1, ranks)]
     for m in range(ranks):
         dbc = lax.dynamic_update_slice_in_dim(dbc, pieces[m], line.source(m) * quarter, 0)
     pre_bc = pre[:, inner:]
     grad_pre_bc = dbc * slope_of(pre_bc, jax.nn.sigmoid(pre_bc))
-    next_head = shifted(pre_head[: CONV - 1], "context", -1)
-    next_bc_head = shifted(grad_pre_bc[: CONV - 1], "context", -1)
+    next_head = shifted(pre_head[: CONV - 1], CONTEXT, -1)
+    next_bc_head = shifted(grad_pre_bc[: CONV - 1], CONTEXT, -1)
     after = jnp.pad(next_head, ((CONV - 1, CONV - 1), (0, 0)))
     reach = jnp.zeros((CONV - 1, inner), f32)
     for k in range(CONV):
@@ -604,20 +641,15 @@
 
     def partial_of(m):
         rank = line.target(m)
-        return jnp.einsum("tk,dk->td", block(grad_z, rank), full_z, preferred_element_type=f32) + jnp.einsum(
-            "tk,dk->td", block(g_xdt, rank), full_xdt, preferred_element_type=f32
-        )
-
+        return dot_t(block(grad_z, rank), full_z) + dot_t(block(g_xdt, rank), full_xdt)
+
+    _, all_others = lax.optimization_barrier((gx_last, all_others))
     gn = line.sum_pieces(partial_of)
-    gn = gn + jnp.einsum(
-        "tk,dk->td", block(gbc, line.me), full_cat[:, inner + LANES :], preferred_element_type=f32
-    )
-
-    out_own = jnp.einsum("tk,dk->td", block(gated_out, line.me), full_out, preferred_element_type=f32)
+    gn = gn + dot_t(block(gbc, line.me), full_cat[:, inner + LANES :])
+
+    out_own = dot_t(block(gated_out, line.me), full_out)
     if ranks > 1:
-        out_own = out_own + jnp.einsum(
-            "tk,dk->td", jnp.concatenate(mixed, axis=1), full_others, preferred_element_type=f32
-        )
+        out_own = out_own + dot_t(jnp.concatenate(mixed, axis=1), ring.join(all_others))
     block_own = (block(block_input, line.me).astype(f32) + out_own).astype(bf16)
     pieces = line.all_pieces(block_own)
     block_output = jnp.zeros((length, width), bf16)
@@ -645,8 +677,9 @@
         )
 
     g_cat = jnp.concatenate([g_xdt, gbc], axis=1)
-    grad_w_cat = jnp.einsum("td,tk->dk", normed, g_cat, preferred_element_type=f32)
-    summed_cat = lax.psum_scatter(grad_w_cat, ("shard", "context"), scatter_dimension=0, tiled=True)
+    grad_w_cat = dot_tn(normed, g_cat)
+    summed_cat = ring.reduce_rows(grad_w_cat)
+    summed_cat = range_ring.reduce_rows(summed_cat)
 
     last = jnp.pad(jnp.concatenate([grad_dt_bias[:LANES], grad_a_log]), (0, inner - 2 * LANES))[None, :]
     packed = jnp.concatenate(
@@ -661,7 +694,7 @@
     wide_lanes = packed.shape[1]
     spare = (-width) % wide_lanes
     gain_rows = jnp.pad(grad_norm_gain, (0, spare)).reshape(-1, wide_lanes)
-    packed = lax.psum(jnp.concatenate([packed, gain_rows], axis=0), ("shard", "context"))
+    packed = lax.psum(jnp.concatenate([packed, gain_rows], axis=0), (SHARD, CONTEXT))
     gain_rows = packed[8:]
     parts = [gain_rows] + [line.send(gain_rows, m) for m in range(1, ranks)]
     ordered = jnp.zeros((ranks,) + gain_rows.shape, f32)
@@ -690,39 +723,39 @@
 
 def solution(mesh):
     in_specs = (
-        P(("shard", "context"), None),
+        P((SHARD, CONTEXT), None),
         P(),
-        P("shard", "tensor"),
-        P("shard", "tensor"),
-        P("shard", None),
-        P("shard", "tensor"),
-        P(None, "tensor"),
-        P("tensor"),
+        P(SHARD, TENSOR),
+        P(SHARD, TENSOR),
+        P(SHARD, None),
+        P(SHARD, TENSOR),
+        P(None, TENSOR),
+        P(TENSOR),
         P(),
         P(),
-        P("tensor"),
-        P("tensor"),
-        P("tensor"),
-        P("tensor"),
-        P("tensor", "shard"),
-        P(("shard", "context"), None),
+        P(TENSOR),
+        P(TENSOR),
+        P(TENSOR),
+        P(TENSOR),
+        P(TENSOR, SHARD),
+        P((SHARD, CONTEXT), None),
     )
     out_specs = (
-        P(("shard", "context"), None),
-        P(("shard", "context"), None),
-        P(("shard", "context"), "tensor"),
-        P(("shard", "context"), "tensor"),
-        P(("shard", "context"), None),
-        P(("shard", "context"), "tensor"),
-        P("tensor", ("shard", "context")),
+        P((SHARD, CONTEXT), None),
+        P((SHARD, CONTEXT), None),
+        P((SHARD, CONTEXT), TENSOR),
+        P((SHARD, CONTEXT), TENSOR),
+        P((SHARD, CONTEXT), None),
+        P((SHARD, CONTEXT), TENSOR),
+        P(TENSOR, (SHARD, CONTEXT)),
         P(),
-        P(None, "tensor"),
-        P("tensor"),
+        P(None, TENSOR),
+        P(TENSOR),
         P(),
         P(),
-        P("tensor"),
-        P("tensor"),
-        P("tensor"),
-        P("tensor"),
+        P(TENSOR),
+        P(TENSOR),
+        P(TENSOR),
+        P(TENSOR),
     )
     return jax.shard_map(body, mesh=mesh, in_specs=in_specs, out_specs=out_specs, check_vma=False)

time: 590 us -> 616 us (1.044)
  starting transfers between devices: 82.4 us -> 115 us
  waiting for transfers between devices: 178 us -> 206 us
  blocking collectives: 46 us -> 26.7 us
  between operations: 14.8 us -> 2.05 us
  other arithmetic: 39.6 us -> 49.8 us
  matrix products: 69.3 us -> 59.5 us
    ppermute x32 -> x45, waiting for transfers between devices: 133 us -> 204 us  [send(): return lax.ppermute(value, self.axis, pairs)]
    ppermute x32 -> x45, starting transfers between devices: 46.7 us -> 91.3 us  [send(): return lax.ppermute(value, self.axis, pairs)]
    ppermute x3 -> x2, waiting for transfers between devices: 26.9 us -> 0.01 us  [all_pieces(): handed = lax.ppermute(across, self.axis, [(1, 0), (2, 3)])]
    dynamic_update_slice x15 -> x14, local copies, waits for them, and re-layouts: 30.3 us -> 7.29 us  [join(): lax.dynamic_update_slice_in_dim(full, piece, self.source(m) * rows, 0)]
    psum x2 -> x1, blocking collectives: 46 us -> 26.7 us  [body(): lax.psum(jnp.concatenate([packed, gain_rows], axis=0), (SHARD, CONTEXT))]
    unnamed x108 -> x146, local copies, waits for them, and re-layouts: 8.71 us -> 27.5 us
    add x0 -> x7, other arithmetic: none -> 9.88 us  [the longest x6 8.5 us: reduce_rows(): value = (keep + got).reshape((left * rows,) + value.shape[1:])]
    dot_general x15, matrix products: 58.2 us -> 48.4 us  [the longest x11 24.8 us: dot_t(): lax.dot_general(a, b, (((1,), (1,)), ((), ())), preferred_element_type=f32)]
  transfers between devices with their start and end apart: 48 -> 56, of which waited for: 19 -> 20; matrix products, arithmetic and copies ran while one was open for 29% -> 29% of each run, Pallas kernels for 0% -> 6%
where the time goes in v3:
time: 616 us; the launch traced here: 605 us
  waiting for transfers between devices  206 us (33%)
  starting transfers between devices  115 us (19%)
  local copies, waits for them, and re-layouts  82.9 us (13%)
  Pallas kernels  62.8 us (10%)
  matrix products  59.5 us (10%)
  other arithmetic  49.8 us (8%)
  blocking collectives  26.7 us (4%)
    ppermute x45, waiting for transfers between devices, send(): return lax.ppermute(value, self.axis, pairs)  204 us
    ppermute x45, starting transfers between devices, send(): return lax.ppermute(value, self.axis, pairs)  91.3 us
    unnamed x146, local copies, waits for them, and re-layouts  27.5 us
    pallas_call x1, Pallas kernels, body(): pl.pallas_call(backward_kernel, grid=(count,), in_specs=[back(inner), bac...  26.9 us
    psum x1, blocking collectives, body(): lax.psum(jnp.concatenate([packed, gain_rows], axis=0), (SHARD, CONTEXT))  26.7 us
    dot_general x11, matrix products, dot_t(): lax.dot_general(a, b, (((1,), (1,)), ((), ())), preferred_element_type=f32)  24.8 us
    dot_general x3, matrix products, dot_tn(): lax.dot_general(a, b, (((0,), (0,)), ((), ())), preferred_element_type=f32)  19.3 us
    pallas_call x1, Pallas kernels, body(): pl.pallas_call(forward_kernel, grid=(count,), in_specs=[ahead(wide), ahea...  13.4 us
  transfers between devices with their start and end apart: 56, of which 20 were waited for; matrix products, arithmetic and copies ran while one was open for 29% of the time, Pallas kernels for 6%

profile of v3, /device:TPU:0, one launch (start us, length us, event | category | flops | bytes accessed | tf_op | source)
XLA Modules:
  0.0 605.0 jit_solution(15136302010303011128)
XLA Ops:
  33.9 16.2 %collective-permute-done.7 = bf16[384,768]{1,0:T(8,128)(2,1)} collective-permute-done((bf16[384,768]{1,0:T(8,128)(2,1)}, bf16[384,768]{1,0:T(8,128)(2,1)}, u32[]{:S(2)}, u32[]{:S(2)}) %collective-permute-start.7) | collective-permute-done | bytes 589856 | tf_op jit(solution)/shard_map/ppermute | solution.py:357
  58.4 4.3 fusion.97.z_ref
  62.9 4.3 fusion.102
  75.1 11.4 %front.1 = (f32[1024,1024]{1,0:T(8,128)}, f32[1024,1024]{1,0:T(8,128)}, f32[1024,128]{1,0:T(8,128)}, f32[128,768]{1,0:T(8,128)}, f32[8,128]{1,0:T(8,128)}) custom-call(bf16[1024,768]{1,0:T(8,128)(2,1)} %slice.207.x_ref.x_raw_ref, bf16[1024,256]{1,0:T(8,128)(2,1)} %get-tuple-element.159.bc_ref, f32[8,1024]{1,0:T(8,128)} %pad.35.edge_ref, ...), custom_call_target="tpu_custom_call" | custom-call | tf_op jit(solution)/shard_map/front/pallas_call | solution.py:506
  86.5 4.1 collective-permute-start.13
  90.6 6.9 %convolution_bitcast_fusion.1.ggo_ref = f32[1024,768]{1,0:T(8,128)} fusion(bf16[1024,1536]{1,0:T(8,128)(2,1)} %param.31, bf16[1536,768]{1,0:T(8,128)(2,1)} %copy-done.10), kind=kOutput, calls=%fused_computation.35 | convolution fusion | flops 2415919104 | bytes 8650752 | tf_op jit(solution)/shard_map/dot_general | solution.py:529
  97.8 13.4 %forward.1 = (f32[1024,768]{1,0:T(8,128)}, f32[1024,768]{1,0:T(8,128)}, f32[1024,768]{1,0:T(8,128)}, f32[8,1024]{1,0:T(8,128)}) custom-call(f32[1024,1024]{1,0:T(8,128)} %get-tuple-element.47.act_ref, f32[1024,128]{1,0:T(8,128)} %compare_select_fusion.step_ref, f32[1024,128]{1,0:T(8,128)} %get-tuple-element.48.cum_ref, f32[1024,768]{1,0:T(8,128)} %fusion.97.z_ref, ...), custom_call_target="tpu_custom_call" | custom-call | tf_op jit(solution)/shard_map/forward/pallas_call | solution.py:530
  111.2 11.6 %collective-permute-start.14 = (f32[8,1024]{1,0:T(8,128)}, f32[8,1024]{1,0:T(8,128)S(1)}, u32[]{:S(2)}, u32[]{:S(2)}) collective-permute-start(f32[8,1024]{1,0:T(8,128)} %get-tuple-element.55), channel_id=1, source_target_pairs={{0,1},{1,0},{2,3},{3,2},{4,5},{5,4},{6,7},{7,6},{8,9},{9,8},{10,11... | collective-permute-start | bytes 98312 | tf_op jit(solution)/shard_map/ppermute | solution.py:357
  131.2 11.0 %gate.1 = (bf16[1024,768]{1,0:T(8,128)(2,1)}, f32[1024,768]{1,0:T(8,128)}, bf16[1024,768]{1,0:T(8,128)(2,1)}, f32[128,768]{1,0:T(8,128)}, f32[8,768]{1,0:T(8,128)}) custom-call(f32[1024,768]{1,0:T(8,128)} %get-tuple-element.54.mixer_ref, f32[1024,768]{1,0:T(8,128)} %fusion.97.z_ref, f32[1024,768]{1,0:T(8,128)} %convolution_bitcast_fusion.1.ggo_ref, ...), custom_call_target="tpu_custom_call" | custom-call | tf_op jit(solution)/shard_map/gate/pallas_call | solution.py:551
  143.5 7.5 %fusion.96 = f32[1536,768]{1,0:T(8,128)} fusion(bf16[1024,768]{1,0:T(8,128)(2,1)} %get-tuple-element.71, f32[1536]{0:T(1024)S(1)} %copy-done.44, f32[1024]{0:T(1024)S(1)} %copy-done.57, bf16[1024,1536]{1,0:T(8,128)(2,1)} %param.16), kind=kOutput, calls=%fused_computation.231 | convolution fusion | flops 2422210560 | bytes 9447424 | tf_op jit(solution)/shard_map/dot_general | solution.py:41
  157.2 4.7 convolution_bitcast_fusion
  161.9 6.6 %reshape.129 = f32[2,2,384,768]{2,1,0,3:T(2,128)} reshape(f32[1536,768]{0,1:T(8,128)} %convolution_bitcast_fusion) | data formatting | bytes 9437184 | tf_op jit(solution)/shard_map/reshape | solution.py:389
  171.9 6.3 %constant_dynamic-slice_fusion.2 = (f32[2,1,384,768]{2,1,0,3:T(1,128)}, f32[2,1,384,768]{2,1,0,3:T(1,128)}) fusion(f32[2,2,384,768]{2,1,0,3:T(2,128)S(1)} %copy-done.5, s32[]{:T(128)S(6)} %select_n.189, s32[]{:T(128)S(6)} %select_n.190), kind=kLoop, calls=%fused_computation.137 | loop fusion | bytes 9437192 | tf_op jit(solution)/shard_map/jit(dynamic_index_in_dim)/dynamic_slice | solution.py:390
  180.6 6.7 %copy.52 = f32[2,1,384,768]{3,2,0,1:T(8,128)} copy(f32[2,1,384,768]{2,1,0,3:T(1,128)} %get-tuple-element.157) | data formatting | bytes 4718592
  187.3 6.7 %copy.51 = f32[2,1,384,768]{3,2,0,1:T(8,128)} copy(f32[2,1,384,768]{2,1,0,3:T(1,128)} %get-tuple-element.156) | data formatting | bytes 4718592
  197.8 26.9 %backward.1 = (bf16[1024,768]{1,0:T(8,128)(2,1)}, f32[8,768]{1,0:T(8,128)}, f32[8,768]{1,0:T(8,128)}, f32[1024,256]{1,0:T(8,128)}, f32[1024,128]{1,0:T(8,128)}, /*index=5*/f32[8,768]{1,0:T(8,128)}, f32[8,128]{1,0:T(8,128)}) custom-call(f32[1024,768]{1,0:T(8,128)} %get-tuple-element.57.gm_ref, f32[1024,1024]{1,0:T(8,128)} %get-tuple-element.47.act_ref, ...), custom_call_target="tpu_custom_call" | custom-call | tf_op jit(solution)/shard_map/backward/pallas_call | solution.py:578
  242.9 7.6 %collective-permute-done.34 = f32[256,256]{1,0:T(8,128)S(1)} collective-permute-done((f32[256,256]{1,0:T(8,128)S(1)}, f32[256,256]{1,0:T(8,128)S(1)}, u32[]{:S(2)}, u32[]{:S(2)}) %collective-permute-start.34) | collective-permute-done | bytes 262176 | tf_op jit(solution)/shard_map/ppermute | solution.py:357
  250.6 6.1 %collective-permute-start.36 = (f32[256,256]{1,0:T(8,128)S(1)}, f32[256,256]{1,0:T(8,128)S(1)}, u32[]{:S(2)}, u32[]{:S(2)}) collective-permute-start(f32[256,256]{1,0:T(8,128)S(1)} %get-tuple-element.153), channel_id=1, source_target_pairs={{0,1},{1,0},{2,3},{3,2},{4,5},{5,4},{6,7},{7,6},{8,9},{9,8},{10,11... | collective-permute-start | bytes 786440 | tf_op jit(solution)/shard_map/ppermute | solution.py:357
  261.1 6.7 %collective-permute-done.36 = f32[256,256]{1,0:T(8,128)S(1)} collective-permute-done((f32[256,256]{1,0:T(8,128)S(1)}, f32[256,256]{1,0:T(8,128)S(1)}, u32[]{:S(2)}, u32[]{:S(2)}) %collective-permute-start.36) | collective-permute-done | bytes 262176 | tf_op jit(solution)/shard_map/ppermute | solution.py:357
  268.4 9.6 %collective-permute-done.37 = f32[256,256]{1,0:T(8,128)S(1)} collective-permute-done((f32[256,256]{1,0:T(8,128)S(1)}, f32[256,256]{1,0:T(8,128)S(1)}, u32[]{:S(2)}, u32[]{:S(2)}) %collective-permute-start.37) | collective-permute-done | bytes 262176 | tf_op jit(solution)/shard_map/ppermute | solution.py:357
  288.1 6.8 %collective-permute-start.31 = (bf16[256,1536]{1,0:T(8,128)(2,1)}, bf16[256,1536]{1,0:T(8,128)(2,1)S(1)}, u32[]{:S(2)}, u32[]{:S(2)}) collective-permute-start(bf16[256,1536]{1,0:T(8,128)(2,1)} %fusion.7), channel_id=1, source_target_pairs={{0,1},{3,2},{4,5},{7,6},{8,9},{11,10},{12,13},{15,14},{16,17},{19,... | collective-permute-start | bytes 2359304 | tf_op jit(solution)/shard_map/ppermute | solution.py:405
  297.9 7.1 %fusion.9 = f32[1536,1152]{1,0:T(8,128)S(1)} fusion(bf16[1024,256]{1,0:T(8,128)(2,1)S(1)} %fusion.38, bf16[1024,128]{1,0:T(8,128)(2,1)} %copy-done.13, bf16[1024,768]{1,0:T(8,128)(2,1)} %copy-done.3, f32[1536]{0:T(1024)} %param.17, f32[1024]{0:T(1024)} %copy-done.56, bf16[1024,1536]{1,0:T(8,128)(2,1)} %param.16), kind=kOutput, calls=%fused_computation.26 | convolution fusion | flops 3637248000 | bytes 12593152 | tf_op jit(solution)/shard_map/dot_general | solution.py:41
  326.3 15.9 %collective-permute-done.18 = bf16[256,768]{1,0:T(8,128)(2,1)S(1)} collective-permute-done((bf16[256,768]{1,0:T(8,128)(2,1)S(1)}, bf16[256,768]{1,0:T(8,128)(2,1)S(1)}, u32[]{:S(2)}, u32[]{:S(2)}) %collective-permute-start.18) | collective-permute-done | bytes 393248 | tf_op jit(solution)/shard_map/ppermute | solution.py:357
  342.2 14.4 %collective-permute-start.32 = (bf16[256,1536]{1,0:T(8,128)(2,1)S(1)}, bf16[256,1536]{1,0:T(8,128)(2,1)S(1)}, u32[]{:S(2)}, u32[]{:S(2)}) collective-permute-start(bf16[256,1536]{1,0:T(8,128)(2,1)S(1)} %fusion.6), channel_id=1, source_target_pairs={{0,2},{1,3},{2,0},{3,1},{4,6},{5,7},{6,4},{7,5},{8,10},{9,11},{10,... | collective-permute-start | bytes 2359304 | tf_op jit(solution)/shard_map/ppermute | solution.py:357
  363.4 21.5 %collective-permute-start.25 = (bf16[256,1536]{1,0:T(8,128)(2,1)}, bf16[256,1536]{1,0:T(8,128)(2,1)}, u32[]{:S(2)}, u32[]{:S(2)}) collective-permute-start(bf16[256,1536]{1,0:T(8,128)(2,1)} %get-tuple-element.177), channel_id=1, source_target_pairs={{0,1},{1,0},{2,3},{3,2},{4,5},{5,4},{6,7},{7,6},{8,9},{9,8},{10,11... | collective-permute-start | bytes 2359304 | tf_op jit(solution)/shard_map/ppermute | solution.py:357
  384.9 13.5 %collective-permute-done.32 = bf16[256,1536]{1,0:T(8,128)(2,1)S(1)} collective-permute-done((bf16[256,1536]{1,0:T(8,128)(2,1)S(1)}, bf16[256,1536]{1,0:T(8,128)(2,1)S(1)}, u32[]{:S(2)}, u32[]{:S(2)}) %collective-permute-start.32) | collective-permute-done | bytes 786464 | tf_op jit(solution)/shard_map/ppermute | solution.py:357
  404.2 26.7 %psum.7 = f32[10,1024]{1,0:T(8,128)S(1)} all-reduce(f32[10,1024]{1,0:T(8,128)S(1)} %pad_maximum_fusion.2), channel_id=1, replica_groups=mesh['shard'=4,'context'=2,'tensor'=4] {'shard','context'}, use_global_device_ids=true, to_apply=%region_13.14 | all-reduce | flops 10240 | bytes 81920 | tf_op jit(solution)/shard_map/psum | solution.py:697
  456.7 4.7 collective-permute-start.40
  466.7 24.1 %collective-permute-done.26 = bf16[256,1536]{1,0:T(8,128)(2,1)} collective-permute-done((bf16[256,1536]{1,0:T(8,128)(2,1)}, bf16[256,1536]{1,0:T(8,128)(2,1)}, u32[]{:S(2)}, u32[]{:S(2)}) %collective-permute-start.26) | collective-permute-done | bytes 786464 | tf_op jit(solution)/shard_map/ppermute | solution.py:357
  499.9 37.8 %collective-permute-done.41 = bf16[256,1536]{1,0:T(8,128)(2,1)S(1)} collective-permute-done((bf16[256,1536]{1,0:T(8,128)(2,1)S(1)}, bf16[256,1536]{1,0:T(8,128)(2,1)S(1)}, u32[]{:S(2)}, u32[]{:S(2)}) %collective-permute-start.41) | collective-permute-done | bytes 786464 | tf_op jit(solution)/shard_map/ppermute | solution.py:357
  545.3 36.3 %collective-permute-done.48 = f32[1,384,1152]{2,1,0:T(8,128)S(1)} collective-permute-done((f32[1,384,1152]{2,1,0:T(8,128)S(1)}, f32[1,384,1152]{2,1,0:T(8,128)S(1)}, u32[]{:S(2)}, u32[]{:S(2)}) %collective-permute-start.48) | collective-permute-done | bytes 1769504 | tf_op jit(solution)/shard_map/ppermute | solution.py:357
  585.2 17.3 %collective-permute-done.49 = f32[1,192,1152]{2,1,0:T(8,128)S(1)} collective-permute-done((f32[1,192,1152]{2,1,0:T(8,128)S(1)}, f32[1,192,1152]{2,1,0:T(8,128)S(1)}, u32[]{:S(2)}, u32[]{:S(2)}) %collective-permute-start.49) | collective-permute-done | bytes 884768 | tf_op jit(solution)/shard_map/ppermute | solution.py:357
  (378 shorter events, 198.4 us)
Async XLA Ops:
  2.8 28.4 %collective-permute-start.5 = (bf16[384,768]{1,0:T(8,128)(2,1)}, bf16[384,768]{1,0:T(8,128)(2,1)}, u32[]{:S(2)}, u32[]{:S(2)}) collective-permute-start(bf16[384,768]{1,0:T(8,128)(2,1)} %bitcast.108), channel_id=1, source_target_pairs={{0,16},{8,24},{16,0},{24,8},{1,17},{9,25},{17,1},{25,9},{2,18},{10... | collective-permute-start | bytes 1769480 | tf_op jit(solution)/shard_map/ppermute | solution.py:357
  5.8 28.1 %collective-permute-start.6 = (bf16[384,768]{1,0:T(8,128)(2,1)}, bf16[384,768]{1,0:T(8,128)(2,1)}, u32[]{:S(2)}, u32[]{:S(2)}) collective-permute-start(bf16[384,768]{1,0:T(8,128)(2,1)} %bitcast.109), channel_id=1, source_target_pairs={{0,1},{1,0},{2,3},{3,2},{4,5},{5,4},{6,7},{7,6},{8,9},{9,8},{10,11... | collective-permute-start | bytes 1769480 | tf_op jit(solution)/shard_map/ppermute | solution.py:357
  7.4 42.7 %collective-permute-start.7 = (bf16[384,768]{1,0:T(8,128)(2,1)}, bf16[384,768]{1,0:T(8,128)(2,1)}, u32[]{:S(2)}, u32[]{:S(2)}) collective-permute-start(bf16[384,768]{1,0:T(8,128)(2,1)} %bitcast.110), channel_id=1, source_target_pairs={{0,2},{1,3},{2,0},{3,1},{4,6},{5,7},{6,4},{7,5},{8,10},{9,11},{10,... | collective-permute-start | bytes 1769480 | tf_op jit(solution)/shard_map/ppermute | solution.py:357
  10.0 40.1 %collective-permute-start.8 = (bf16[384,768]{1,0:T(8,128)(2,1)}, bf16[384,768]{1,0:T(8,128)(2,1)}, u32[]{:S(2)}, u32[]{:S(2)}) collective-permute-start(bf16[384,768]{1,0:T(8,128)(2,1)} %bitcast.111), channel_id=1, source_target_pairs={{0,3},{1,2},{2,1},{3,0},{4,7},{5,6},{6,5},{7,4},{8,11},{9,10},{10,... | collective-permute-start | bytes 1769480 | tf_op jit(solution)/shard_map/ppermute | solution.py:357
  10.2 39.9 %collective-permute-start.4 = (bf16[384,768]{1,0:T(8,128)(2,1)}, bf16[384,768]{1,0:T(8,128)(2,1)}, u32[]{:S(2)}, u32[]{:S(2)}) collective-permute-start(bf16[384,768]{1,0:T(8,128)(2,1)} %param.18), channel_id=1, source_target_pairs={{0,16},{8,24},{16,0},{24,8},{1,17},{9,25},{17,1},{25,9},{2,18},{10... | collective-permute-start | bytes 1769480 | tf_op jit(solution)/shard_map/ppermute | solution.py:357
  31.3 23.5 %collective-permute-start = (bf16[384,1152]{1,0:T(8,128)(2,1)S(1)}, bf16[384,1152]{1,0:T(8,128)(2,1)S(1)}, u32[]{:S(2)}, u32[]{:S(2)}) collective-permute-start(bf16[384,1152]{1,0:T(8,128)(2,1)S(1)} %get-tuple-element.166), channel_id=1, source_target_pairs={{0,16},{8,24},{16,0},{24,8},{1,17},{9,25},{17,1},{25,9},{2,18},{10... | collective-permute-start | bytes 2654216 | tf_op jit(solution)/shard_map/ppermute | solution.py:357
  33.9 21.5 %collective-permute-start.1 = (bf16[384,1152]{1,0:T(8,128)(2,1)S(1)}, bf16[384,1152]{1,0:T(8,128)(2,1)S(1)}, u32[]{:S(2)}, u32[]{:S(2)}) collective-permute-start(bf16[384,1152]{1,0:T(8,128)(2,1)S(1)} %get-tuple-element.166), channel_id=1, source_target_pairs={{0,8},{8,0},{16,24},{24,16},{1,9},{9,1},{17,25},{25,17},{2,10},{10... | collective-permute-start | bytes 2654216 | tf_op jit(solution)/shard_map/ppermute | solution.py:357
  127.2 140.6 %collective-permute-start.23 = (bf16[384,2304]{1,0:T(8,128)(2,1)}, bf16[384,2304]{1,0:T(8,128)(2,1)}, u32[]{:S(2)}, u32[]{:S(2)}) collective-permute-start(bf16[384,2304]{1,0:T(8,128)(2,1)} %constant_dynamic-update-slice_fusion.28), channel_id=1, source_target_pairs={{0,16},{8,24},{16,0},{24,8},{1,17},{9,25},{17,1},{25,9},{2,18},{10... | collective-permute-start | bytes 5308424 | tf_op jit(solution)/shard_map/ppermute | solution.py:357
  127.7 186.2 %collective-permute-start.22 = (bf16[384,2304]{1,0:T(8,128)(2,1)}, bf16[384,2304]{1,0:T(8,128)(2,1)}, u32[]{:S(2)}, u32[]{:S(2)}) collective-permute-start(bf16[384,2304]{1,0:T(8,128)(2,1)} %constant_dynamic-update-slice_fusion.28), channel_id=1, source_target_pairs={{0,8},{8,0},{16,24},{24,16},{1,9},{9,1},{17,25},{25,17},{2,10},{10... | collective-permute-start | bytes 5308424 | tf_op jit(solution)/shard_map/ppermute | solution.py:357
  142.2 55.6 %collective-permute-start.20 = (f32[128,768]{1,0:T(8,128)}, f32[128,768]{1,0:T(8,128)}, u32[]{:S(2)}, u32[]{:S(2)}) collective-permute-start(f32[128,768]{1,0:T(8,128)} %get-tuple-element.61), channel_id=1, source_target_pairs={{4,0},{5,1},{6,2},{7,3},{12,8},{13,9},{14,10},{15,11},{20,16},{21,... | collective-permute-start | bytes 1179656 | tf_op jit(solution)/shard_map/ppermute | solution.py:332
  267.8 185.4 %collective-permute-start.50 = (f32[2,384,768]{2,1,0:T(8,128)}, f32[2,384,768]{2,1,0:T(8,128)}, u32[]{:S(2)}, u32[]{:S(2)}) collective-permute-start(f32[2,384,768]{2,1,0:T(8,128)} %bitcast.26), channel_id=1, source_target_pairs={{0,8},{8,0},{16,24},{24,16},{1,9},{9,1},{17,25},{25,17},{2,10},{10... | collective-permute-start | bytes 7077896 | tf_op jit(solution)/shard_map/ppermute | solution.py:357
  267.8 188.9 %collective-permute-start.44 = (f32[2,384,768]{2,1,0:T(8,128)}, f32[2,384,768]{2,1,0:T(8,128)}, u32[]{:S(2)}, u32[]{:S(2)}) collective-permute-start(f32[2,384,768]{2,1,0:T(8,128)} %dynamic-slice_bitcast_fusion.1), channel_id=1, source_target_pairs={{0,8},{8,0},{16,24},{24,16},{1,9},{9,1},{17,25},{25,17},{2,10},{10... | collective-permute-start | bytes 7077896 | tf_op jit(solution)/shard_map/ppermute | solution.py:357
  278.0 36.3 %collective-permute-start.24 = (bf16[384,2304]{1,0:T(8,128)(2,1)}, bf16[384,2304]{1,0:T(8,128)(2,1)}, u32[]{:S(2)}, u32[]{:S(2)}) collective-permute-start(bf16[384,2304]{1,0:T(8,128)(2,1)} %collective-permute-done.23), channel_id=1, source_target_pairs={{0,8},{8,0},{16,24},{24,16},{1,9},{9,1},{17,25},{25,17},{2,10},{10... | collective-permute-start | bytes 5308424 | tf_op jit(solution)/shard_map/ppermute | solution.py:357
  288.1 22.3 %collective-permute-start.31 = (bf16[256,1536]{1,0:T(8,128)(2,1)}, bf16[256,1536]{1,0:T(8,128)(2,1)S(1)}, u32[]{:S(2)}, u32[]{:S(2)}) collective-permute-start(bf16[256,1536]{1,0:T(8,128)(2,1)} %fusion.7), channel_id=1, source_target_pairs={{0,1},{3,2},{4,5},{7,6},{8,9},{11,10},{12,13},{15,14},{16,17},{19,... | collective-permute-start | bytes 2359304 | tf_op jit(solution)/shard_map/ppermute | solution.py:405
  313.9 28.3 %collective-permute-start.18 = (bf16[256,768]{1,0:T(8,128)(2,1)S(1)}, bf16[256,768]{1,0:T(8,128)(2,1)S(1)}, u32[]{:S(2)}, u32[]{:S(2)}) collective-permute-start(bf16[256,768]{1,0:T(8,128)(2,1)S(1)} %copy-done.39), channel_id=1, source_target_pairs={{0,2},{1,3},{2,0},{3,1},{4,6},{5,7},{6,4},{7,5},{8,10},{9,11},{10,... | collective-permute-start | bytes 1179656 | tf_op jit(solution)/shard_map/ppermute | solution.py:357
  314.3 27.9 %collective-permute-start.19 = (bf16[256,768]{1,0:T(8,128)(2,1)S(1)}, bf16[256,768]{1,0:T(8,128)(2,1)S(1)}, u32[]{:S(2)}, u32[]{:S(2)}) collective-permute-start(bf16[256,768]{1,0:T(8,128)(2,1)S(1)} %copy-done.38), channel_id=1, source_target_pairs={{0,3},{1,2},{2,1},{3,0},{4,7},{5,6},{6,5},{7,4},{8,11},{9,10},{10,... | collective-permute-start | bytes 1179656 | tf_op jit(solution)/shard_map/ppermute | solution.py:357
  325.4 38.0 %collective-permute-start.29 = (bf16[256,1536]{1,0:T(8,128)(2,1)S(1)}, bf16[256,1536]{1,0:T(8,128)(2,1)S(1)}, u32[]{:S(2)}, u32[]{:S(2)}) collective-permute-start(bf16[256,1536]{1,0:T(8,128)(2,1)S(1)} %copy-done.35), channel_id=1, source_target_pairs={{1,2},{2,1},{5,6},{6,5},{9,10},{10,9},{13,14},{14,13},{17,18},{18,... | collective-permute-start | bytes 2359304 | tf_op jit(solution)/shard_map/ppermute | solution.py:406
  342.2 56.2 %collective-permute-start.32 = (bf16[256,1536]{1,0:T(8,128)(2,1)S(1)}, bf16[256,1536]{1,0:T(8,128)(2,1)S(1)}, u32[]{:S(2)}, u32[]{:S(2)}) collective-permute-start(bf16[256,1536]{1,0:T(8,128)(2,1)S(1)} %fusion.6), channel_id=1, source_target_pairs={{0,2},{1,3},{2,0},{3,1},{4,6},{5,7},{6,4},{7,5},{8,10},{9,11},{10,... | collective-permute-start | bytes 2359304 | tf_op jit(solution)/shard_map/ppermute | solution.py:357
  363.4 132.5 %collective-permute-start.47 = (f32[2,384,1152]{2,1,0:T(8,128)}, f32[2,384,1152]{2,1,0:T(8,128)}, u32[]{:S(2)}, u32[]{:S(2)}) collective-permute-start(f32[2,384,1152]{2,1,0:T(8,128)} %dynamic-slice_bitcast_fusion), channel_id=1, source_target_pairs={{0,8},{8,0},{16,24},{24,16},{1,9},{9,1},{17,25},{25,17},{2,10},{10... | collective-permute-start | bytes 10616840 | tf_op jit(solution)/shard_map/ppermute | solution.py:357
  363.4 101.0 %collective-permute-start.25 = (bf16[256,1536]{1,0:T(8,128)(2,1)}, bf16[256,1536]{1,0:T(8,128)(2,1)}, u32[]{:S(2)}, u32[]{:S(2)}) collective-permute-start(bf16[256,1536]{1,0:T(8,128)(2,1)} %get-tuple-element.177), channel_id=1, source_target_pairs={{0,1},{1,0},{2,3},{3,2},{4,5},{5,4},{6,7},{7,6},{8,9},{9,8},{10,11... | collective-permute-start | bytes 2359304 | tf_op jit(solution)/shard_map/ppermute | solution.py:357
  452.5 38.2 %collective-permute-start.26 = (bf16[256,1536]{1,0:T(8,128)(2,1)}, bf16[256,1536]{1,0:T(8,128)(2,1)}, u32[]{:S(2)}, u32[]{:S(2)}) collective-permute-start(bf16[256,1536]{1,0:T(8,128)(2,1)} %get-tuple-element.177), channel_id=1, source_target_pairs={{0,2},{1,3},{2,0},{3,1},{4,6},{5,7},{6,4},{7,5},{8,10},{9,11},{10,... | collective-permute-start | bytes 2359304 | tf_op jit(solution)/shard_map/ppermute | solution.py:357
  453.2 87.3 %collective-permute-start.27 = (bf16[256,1536]{1,0:T(8,128)(2,1)}, bf16[256,1536]{1,0:T(8,128)(2,1)S(1)}, u32[]{:S(2)}, u32[]{:S(2)}) collective-permute-start(bf16[256,1536]{1,0:T(8,128)(2,1)} %get-tuple-element.177), channel_id=1, source_target_pairs={{1,2},{2,1},{5,6},{6,5},{9,10},{10,9},{13,14},{14,13},{17,18},{18,... | collective-permute-start | bytes 2359304 | tf_op jit(solution)/shard_map/ppermute | solution.py:419
  456.7 36.8 %collective-permute-start.40 = (bf16[256,1536]{1,0:T(8,128)(2,1)S(1)}, bf16[256,1536]{1,0:T(8,128)(2,1)S(1)}, u32[]{:S(2)}, u32[]{:S(2)}) collective-permute-start(bf16[256,1536]{1,0:T(8,128)(2,1)S(1)} %copy-done.33), channel_id=1, source_target_pairs={{0,1},{1,0},{2,3},{3,2},{4,5},{5,4},{6,7},{7,6},{8,9},{9,8},{10,11... | collective-permute-start | bytes 2359304 | tf_op jit(solution)/shard_map/ppermute | solution.py:357
  464.5 73.2 %collective-permute-start.41 = (bf16[256,1536]{1,0:T(8,128)(2,1)S(1)}, bf16[256,1536]{1,0:T(8,128)(2,1)S(1)}, u32[]{:S(2)}, u32[]{:S(2)}) collective-permute-start(bf16[256,1536]{1,0:T(8,128)(2,1)S(1)} %copy-done.33), channel_id=1, source_target_pairs={{0,2},{1,3},{2,0},{3,1},{4,6},{5,7},{6,4},{7,5},{8,10},{9,11},{10,... | collective-permute-start | bytes 2359304 | tf_op jit(solution)/shard_map/ppermute | solution.py:357
  490.8 52.0 %collective-permute-start.51 = (f32[1,384,768]{2,1,0:T(8,128)S(1)}, f32[1,384,768]{2,1,0:T(8,128)S(1)}, u32[]{:S(2)}, u32[]{:S(2)}) collective-permute-start(f32[1,384,768]{2,1,0:T(8,128)S(1)} %constant_dynamic-slice_fusion), channel_id=1, source_target_pairs={{0,16},{8,24},{16,0},{24,8},{1,17},{9,25},{17,1},{25,9},{2,18},{10... | collective-permute-start | bytes 3538952 | tf_op jit(solution)/shard_map/ppermute | solution.py:357
  493.5 51.4 %collective-permute-start.45 = (f32[1,384,768]{2,1,0:T(8,128)S(1)}, f32[1,384,768]{2,1,0:T(8,128)S(1)}, u32[]{:S(2)}, u32[]{:S(2)}) collective-permute-start(f32[1,384,768]{2,1,0:T(8,128)S(1)} %constant_dynamic-slice_fusion.4), channel_id=1, source_target_pairs={{0,16},{8,24},{16,0},{24,8},{1,17},{9,25},{17,1},{25,9},{2,18},{10... | collective-permute-start | bytes 3538952 | tf_op jit(solution)/shard_map/ppermute | solution.py:357
  495.9 45.3 %collective-permute-start.28 = (bf16[256,1536]{1,0:T(8,128)(2,1)}, bf16[256,1536]{1,0:T(8,128)(2,1)S(1)}, u32[]{:S(2)}, u32[]{:S(2)}) collective-permute-start(bf16[256,1536]{1,0:T(8,128)(2,1)} %collective-permute-done.26), channel_id=1, source_target_pairs={{1,0},{2,3},{5,4},{6,7},{9,8},{10,11},{13,12},{14,15},{17,16},{18,... | collective-permute-start | bytes 2359304 | tf_op jit(solution)/shard_map/ppermute | solution.py:420
  537.7 43.9 %collective-permute-start.48 = (f32[1,384,1152]{2,1,0:T(8,128)S(1)}, f32[1,384,1152]{2,1,0:T(8,128)S(1)}, u32[]{:S(2)}, u32[]{:S(2)}) collective-permute-start(f32[1,384,1152]{2,1,0:T(8,128)S(1)} %constant_dynamic-slice_fusion.3), channel_id=1, source_target_pairs={{0,16},{8,24},{16,0},{24,8},{1,17},{9,25},{17,1},{25,9},{2,18},{10... | collective-permute-start | bytes 5308424 | tf_op jit(solution)/shard_map/ppermute | solution.py:357
  540.5 41.5 %collective-permute-start.42 = (bf16[256,1536]{1,0:T(8,128)(2,1)S(1)}, bf16[256,1536]{1,0:T(8,128)(2,1)S(1)}, u32[]{:S(2)}, u32[]{:S(2)}) collective-permute-start(bf16[256,1536]{1,0:T(8,128)(2,1)S(1)} %copy-done.33), channel_id=1, source_target_pairs={{1,2},{2,1},{5,6},{6,5},{9,10},{10,9},{13,14},{14,13},{17,18},{18,... | collective-permute-start | bytes 2359304 | tf_op jit(solution)/shard_map/ppermute | solution.py:419
  541.2 40.8 %collective-permute-start.43 = (bf16[256,1536]{1,0:T(8,128)(2,1)S(1)}, bf16[256,1536]{1,0:T(8,128)(2,1)S(1)}, u32[]{:S(2)}, u32[]{:S(2)}) collective-permute-start(bf16[256,1536]{1,0:T(8,128)(2,1)S(1)} %collective-permute-done.41), channel_id=1, source_target_pairs={{1,0},{2,3},{5,4},{6,7},{9,8},{10,11},{13,12},{14,15},{17,16},{18,... | collective-permute-start | bytes 2359304 | tf_op jit(solution)/shard_map/ppermute | solution.py:420
  543.0 40.5 %collective-permute-start.52 = (f32[1,192,768]{2,1,0:T(8,128)S(1)}, f32[1,192,768]{2,1,0:T(8,128)S(1)}, u32[]{:S(2)}, u32[]{:S(2)}) collective-permute-start(f32[1,192,768]{2,1,0:T(8,128)S(1)} %dynamic-slice_bitcast_fusion.3), channel_id=1, source_target_pairs={{0,4},{4,0},{1,5},{5,1},{2,6},{6,2},{3,7},{7,3},{8,12},{12,8},{9,1... | collective-permute-start | bytes 1769480 | tf_op jit(solution)/shard_map/ppermute | solution.py:357
  545.1 39.3 %collective-permute-start.46 = (f32[1,192,768]{2,1,0:T(8,128)S(1)}, f32[1,192,768]{2,1,0:T(8,128)S(1)}, u32[]{:S(2)}, u32[]{:S(2)}) collective-permute-start(f32[1,192,768]{2,1,0:T(8,128)S(1)} %dynamic-slice_bitcast_fusion.4), channel_id=1, source_target_pairs={{0,4},{4,0},{1,5},{5,1},{2,6},{6,2},{3,7},{7,3},{8,12},{12,8},{9,1... | collective-permute-start | bytes 1769480 | tf_op jit(solution)/shard_map/ppermute | solution.py:357
  (93 other events, 1201.6 us)

commit v4 on v3

--- a/solution.py
+++ b/solution.py
@@ -382,17 +382,15 @@
     def reduce_rows(self, value):
         if not self.paired:
             return lax.psum_scatter(value, self.axis, scatter_dimension=0, tiled=True)
-        left, step = self.size, 1
-        rows = value.shape[0] // self.size
+        rows, step = value.shape[0] // self.size, 1
+        value = with_layout_constraint(value, Layout((0, 1)))
+        parts = {m: lax.dynamic_slice_in_dim(value, self.target(m) * rows, rows) for m in range(self.size)}
         while step < self.size:
-            mine = (self.me // step) % 2
-            view = value.reshape((left // 2, 2, rows) + value.shape[1:])
-            keep = lax.dynamic_index_in_dim(view, mine, 1, keepdims=False)
-            give = lax.dynamic_index_in_dim(view, 1 - mine, 1, keepdims=False)
-            got = self.send(give, step)
-            left, step = left // 2, step * 2
-            value = (keep + got).reshape((left * rows,) + value.shape[1:])
-        return value
+            parts = {
+                m: part + self.send(parts[m | step], step) for m, part in parts.items() if not m & step
+            }
+            step *= 2
+        return parts[0]
 
     def sum_pieces(self, piece):
         if self.size != 4:
@@ -636,12 +634,16 @@
     g_dt = g_dt.astype(bf16)
     grad_a_log = rate_acc[0] * rate_row[0]
 
+    gx, late_z = lax.optimization_barrier((gx, grad_z))
     g_xdt = jnp.concatenate([gx, g_dt], axis=1)
+    grad_w_xdt = dot_tn(normed, g_xdt)
+    summed_xdt = ring.reduce_rows(grad_w_xdt)
+    summed_xdt = range_ring.reduce_rows(summed_xdt)
     full_xdt = full_cat[:, : inner + LANES]
 
     def partial_of(m):
         rank = line.target(m)
-        return dot_t(block(grad_z, rank), full_z) + dot_t(block(g_xdt, rank), full_xdt)
+        return dot_t(block(late_z, rank), full_z) + dot_t(block(g_xdt, rank), full_xdt)
 
     _, all_others = lax.optimization_barrier((gx_last, all_others))
     gn = line.sum_pieces(partial_of)
@@ -666,20 +668,10 @@
     delta = delta.astype(bf16)
     grad_norm_gain = jnp.sum(gn * x_own * inv_own, axis=0)
     pieces = line.all_pieces(delta)
-    input_grad = jnp.zeros((length, width), f32)
-    for m in range(ranks):
-        rank = line.source(m)
-        input_grad = lax.dynamic_update_slice_in_dim(
-            input_grad,
-            block(out_cotangent, rank).astype(f32) + pieces[m].astype(f32),
-            rank * quarter,
-            0,
-        )
-
-    g_cat = jnp.concatenate([g_xdt, gbc], axis=1)
-    grad_w_cat = dot_tn(normed, g_cat)
-    summed_cat = ring.reduce_rows(grad_w_cat)
-    summed_cat = range_ring.reduce_rows(summed_cat)
+    back_pieces = pieces
+
+    summed_bc = ring.reduce_rows(dot_tn(normed, gbc))
+    summed_bc = range_ring.reduce_rows(summed_bc)
 
     last = jnp.pad(jnp.concatenate([grad_dt_bias[:LANES], grad_a_log]), (0, inner - 2 * LANES))[None, :]
     packed = jnp.concatenate(
@@ -701,13 +693,24 @@
     for m in range(ranks):
         ordered = lax.dynamic_update_slice_in_dim(ordered, parts[m][None], line.source(m), 0)
     sum_norm_gain = jnp.sum(ordered, axis=0).reshape(-1)[:width]
+    if ranks > 1:
+        packed, back_pieces[1] = lax.optimization_barrier((packed, back_pieces[1]))
+    input_grad = jnp.zeros((length, width), f32)
+    for m in range(ranks):
+        rank = line.source(m)
+        input_grad = lax.dynamic_update_slice_in_dim(
+            input_grad,
+            block(out_cotangent, rank).astype(f32) + back_pieces[m].astype(f32),
+            rank * quarter,
+            0,
+        )
     return (
         block_output,
         input_grad,
         summed_z,
-        summed_cat[:, :inner],
-        summed_cat[:, inner + LANES :],
-        summed_cat[:, inner : inner + heads],
+        summed_xdt[:, :inner],
+        summed_bc,
+        summed_xdt[:, inner : inner + heads],
         summed_out,
         sum_norm_gain,
         packed[:CONV, :inner],

time: 616 us -> 550 us (0.89)
  local copies, waits for them, and re-layouts: 82.9 us -> 50.9 us
  starting transfers between devices: 115 us -> 92.8 us
  waiting for transfers between devices: 206 us -> 190 us
  other arithmetic: 49.8 us -> 61.8 us
    ppermute x45 -> x52, waiting for transfers between devices: 204 us -> 173 us  [send(): return lax.ppermute(value, self.axis, pairs)]
    ppermute x45 -> x52, starting transfers between devices: 91.3 us -> 73.2 us  [send(): return lax.ppermute(value, self.axis, pairs)]
    ppermute x2, waiting for transfers between devices: 0.01 us -> 15 us  [all_pieces(): handed = lax.ppermute(across, self.axis, [(1, 0), (2, 3)])]
    unnamed x146 -> x156, local copies, waits for them, and re-layouts: 27.5 us -> 14.9 us
    dynamic_slice x0 -> x4, other arithmetic: none -> 7.82 us  [reduce_rows(): lax.dynamic_slice_in_dim(value, self.target(m) * rows, rows)]
    reshape x1 -> x0, local copies, waits for them, and re-layouts: 6.62 us -> none  [reduce_rows(): view = value.reshape((left // 2, 2, rows) + value.shape[1:])]
    dot_general x3 -> x4, matrix products: 19.3 us -> 15.4 us  [dot_tn(): lax.dot_general(a, b, (((0,), (0,)), ((), ())), preferred_element_type=f32)]
  transfers between devices with their start and end apart: 56 -> 63, of which waited for: 20 -> 22; matrix products, arithmetic and copies ran while one was open for 29% -> 28% of each run, Pallas kernels for 6% -> 7%
where the time goes in v4:
time: 550 us; the launch traced here: 540 us
  waiting for transfers between devices  190 us (35%)
  starting transfers between devices  92.8 us (17%)
  Pallas kernels  62.8 us (11%)
  other arithmetic  61.8 us (11%)
  matrix products  54.9 us (10%)
  local copies, waits for them, and re-layouts  50.9 us (9%)
  blocking collectives  24.8 us (5%)
    ppermute x52, waiting for transfers between devices, send(): return lax.ppermute(value, self.axis, pairs)  173 us
    ppermute x52, starting transfers between devices, send(): return lax.ppermute(value, self.axis, pairs)  73.2 us
    pallas_call x1, Pallas kernels, body(): pl.pallas_call(backward_kernel, grid=(count,), in_specs=[back(inner), bac...  26.9 us
    psum x1, blocking collectives, body(): lax.psum(jnp.concatenate([packed, gain_rows], axis=0), (SHARD, CONTEXT))  24.8 us
    dot_general x11, matrix products, dot_t(): lax.dot_general(a, b, (((1,), (1,)), ((), ())), preferred_element_type=f32)  24 us
    dot_general x4, matrix products, dot_tn(): lax.dot_general(a, b, (((0,), (0,)), ((), ())), preferred_element_type=f32)  15.4 us
    ppermute x2, waiting for transfers between devices, all_pieces(): handed = lax.ppermute(across, self.axis, [(1, 0), (2, 3)])  15 us
    unnamed x156, local copies, waits for them, and re-layouts  14.9 us
  transfers between devices with their start and end apart: 63, of which 22 were waited for; matrix products, arithmetic and copies ran while one was open for 28% of the time, Pallas kernels for 7%

profile of v4, /device:TPU:0, one launch (start us, length us, event | category | flops | bytes accessed | tf_op | source)
XLA Modules:
  0.0 539.7 jit_solution(1053919825183902871)
XLA Ops:
  22.7 3.5 convert_element_type.98
  33.8 16.3 %collective-permute-done.7 = bf16[384,768]{1,0:T(8,128)(2,1)} collective-permute-done((bf16[384,768]{1,0:T(8,128)(2,1)}, bf16[384,768]{1,0:T(8,128)(2,1)}, u32[]{:S(2)}, u32[]{:S(2)}) %collective-permute-start.7) | collective-permute-done | bytes 589856 | tf_op jit(solution)/shard_map/ppermute | solution.py:357
  58.4 4.3 fusion.91.z_ref
  62.9 4.3 fusion.96
  68.7 3.4 collective-permute-start.3
  75.2 11.4 %front.1 = (f32[1024,1024]{1,0:T(8,128)}, f32[1024,1024]{1,0:T(8,128)}, f32[1024,128]{1,0:T(8,128)}, f32[128,768]{1,0:T(8,128)}, f32[8,128]{1,0:T(8,128)}) custom-call(bf16[1024,768]{1,0:T(8,128)(2,1)} %slice.203.x_ref.x_raw_ref, bf16[1024,256]{1,0:T(8,128)(2,1)} %get-tuple-element.155.bc_ref, f32[8,1024]{1,0:T(8,128)} %pad.35.edge_ref, ...), custom_call_target="tpu_custom_call" | custom-call | tf_op jit(solution)/shard_map/front/pallas_call | solution.py:504
  86.6 4.1 collective-permute-start.13
  90.7 6.8 %convolution_bitcast_fusion.1.ggo_ref = f32[1024,768]{1,0:T(8,128)} fusion(bf16[1024,1536]{1,0:T(8,128)(2,1)} %param.31, bf16[1536,768]{1,0:T(8,128)(2,1)} %copy-done.8), kind=kOutput, calls=%fused_computation.25 | convolution fusion | flops 2415919104 | bytes 8650752 | tf_op jit(solution)/shard_map/dot_general | solution.py:527
  97.9 13.5 %forward.1 = (f32[1024,768]{1,0:T(8,128)}, f32[1024,768]{1,0:T(8,128)}, f32[1024,768]{1,0:T(8,128)}, f32[8,1024]{1,0:T(8,128)}) custom-call(f32[1024,1024]{1,0:T(8,128)} %get-tuple-element.51.act_ref, f32[1024,128]{1,0:T(8,128)} %compare_select_fusion.step_ref, f32[1024,128]{1,0:T(8,128)} %get-tuple-element.52.cum_ref, f32[1024,768]{1,0:T(8,128)} %fusion.91.z_ref, ...), custom_call_target="tpu_custom_call" | custom-call | tf_op jit(solution)/shard_map/forward/pallas_call | solution.py:528
  111.3 11.6 %collective-permute-start.14 = (f32[8,1024]{1,0:T(8,128)}, f32[8,1024]{1,0:T(8,128)S(1)}, u32[]{:S(2)}, u32[]{:S(2)}) collective-permute-start(f32[8,1024]{1,0:T(8,128)} %get-tuple-element.59), channel_id=1, source_target_pairs={{0,1},{1,0},{2,3},{3,2},{4,5},{5,4},{6,7},{7,6},{8,9},{9,8},{10,11... | collective-permute-start | bytes 98312 | tf_op jit(solution)/shard_map/ppermute | solution.py:357
  131.3 11.0 %gate.1 = (bf16[1024,768]{1,0:T(8,128)(2,1)}, f32[1024,768]{1,0:T(8,128)}, bf16[1024,768]{1,0:T(8,128)(2,1)}, f32[128,768]{1,0:T(8,128)}, f32[8,768]{1,0:T(8,128)}) custom-call(f32[1024,768]{1,0:T(8,128)} %get-tuple-element.58.mixer_ref, f32[1024,768]{1,0:T(8,128)} %fusion.91.z_ref, f32[1024,768]{1,0:T(8,128)} %convolution_bitcast_fusion.1.ggo_ref, ...), custom_call_target="tpu_custom_call" | custom-call | tf_op jit(solution)/shard_map/gate/pallas_call | solution.py:549
  145.0 5.2 convolution_bitcast_fusion
  160.0 26.9 %backward.1 = (bf16[1024,768]{1,0:T(8,128)(2,1)}, f32[8,768]{1,0:T(8,128)}, f32[8,768]{1,0:T(8,128)}, f32[1024,256]{1,0:T(8,128)}, f32[1024,128]{1,0:T(8,128)}, /*index=5*/f32[8,768]{1,0:T(8,128)}, f32[8,128]{1,0:T(8,128)}) custom-call(f32[1024,768]{1,0:T(8,128)} %get-tuple-element.61.gm_ref, f32[1024,1024]{1,0:T(8,128)} %get-tuple-element.51.act_ref, ...), custom_call_target="tpu_custom_call" | custom-call | tf_op jit(solution)/shard_map/backward/pallas_call | solution.py:576
  203.1 3.6 fusion.9
  214.3 4.8 collective-permute-start.36
  223.5 6.5 %collective-permute-done.36 = f32[256,256]{1,0:T(8,128)S(1)} collective-permute-done((f32[256,256]{1,0:T(8,128)S(1)}, f32[256,256]{1,0:T(8,128)S(1)}, u32[]{:S(2)}, u32[]{:S(2)}) %collective-permute-start.36) | collective-permute-done | bytes 262176 | tf_op jit(solution)/shard_map/ppermute | solution.py:357
  230.0 10.3 %collective-permute-done.37 = f32[256,256]{1,0:T(8,128)S(1)} collective-permute-done((f32[256,256]{1,0:T(8,128)S(1)}, f32[256,256]{1,0:T(8,128)S(1)}, u32[]{:S(2)}, u32[]{:S(2)}) %collective-permute-start.37) | collective-permute-done | bytes 262176 | tf_op jit(solution)/shard_map/ppermute | solution.py:357
  255.2 3.8 fusion.89
  273.6 4.4 collective-permute-done.54
  294.8 13.0 %collective-permute-done.18 = bf16[256,768]{1,0:T(8,128)(2,1)S(1)} collective-permute-done((bf16[256,768]{1,0:T(8,128)(2,1)S(1)}, bf16[256,768]{1,0:T(8,128)(2,1)S(1)}, u32[]{:S(2)}, u32[]{:S(2)}) %collective-permute-start.18) | collective-permute-done | bytes 393248 | tf_op jit(solution)/shard_map/ppermute | solution.py:357
  309.2 8.3 %collective-permute-start.32 = (bf16[256,1536]{1,0:T(8,128)(2,1)S(1)}, bf16[256,1536]{1,0:T(8,128)(2,1)S(1)}, u32[]{:S(2)}, u32[]{:S(2)}) collective-permute-start(bf16[256,1536]{1,0:T(8,128)(2,1)S(1)} %fusion.6), channel_id=1, source_target_pairs={{0,2},{1,3},{2,0},{3,1},{4,6},{5,7},{6,4},{7,5},{8,10},{9,11},{10,... | collective-permute-start | bytes 2359304 | tf_op jit(solution)/shard_map/ppermute | solution.py:357
  325.8 39.8 %collective-permute-done.32 = bf16[256,1536]{1,0:T(8,128)(2,1)S(1)} collective-permute-done((bf16[256,1536]{1,0:T(8,128)(2,1)S(1)}, bf16[256,1536]{1,0:T(8,128)(2,1)S(1)}, u32[]{:S(2)}, u32[]{:S(2)}) %collective-permute-start.32) | collective-permute-done | bytes 786464 | tf_op jit(solution)/shard_map/ppermute | solution.py:357
  366.8 3.8 multiply_reduce_fusion.1
  371.4 24.8 %psum.7 = f32[10,1024]{1,0:T(8,128)S(1)} all-reduce(f32[10,1024]{1,0:T(8,128)S(1)} %pad_maximum_fusion.4), channel_id=1, replica_groups=mesh['shard'=4,'context'=2,'tensor'=4] {'shard','context'}, use_global_device_ids=true, to_apply=%region_13.14 | all-reduce | flops 10240 | bytes 81920 | tf_op jit(solution)/shard_map/psum | solution.py:689
  397.0 3.5 broadcast_in_dim.68
  424.9 25.7 %collective-permute-done.25 = bf16[256,1536]{1,0:T(8,128)(2,1)S(1)} collective-permute-done((bf16[256,1536]{1,0:T(8,128)(2,1)}, bf16[256,1536]{1,0:T(8,128)(2,1)S(1)}, u32[]{:S(2)}, u32[]{:S(2)}) %collective-permute-start.25) | collective-permute-done | bytes 786464 | tf_op jit(solution)/shard_map/ppermute | solution.py:357
  451.6 5.4 %collective-permute-done.26 = bf16[256,1536]{1,0:T(8,128)(2,1)S(1)} collective-permute-done((bf16[256,1536]{1,0:T(8,128)(2,1)}, bf16[256,1536]{1,0:T(8,128)(2,1)S(1)}, u32[]{:S(2)}, u32[]{:S(2)}) %collective-permute-start.26) | collective-permute-done | bytes 786464 | tf_op jit(solution)/shard_map/ppermute | solution.py:357
  459.5 23.9 %collective-permute-done.40 = bf16[256,1536]{1,0:T(8,128)(2,1)S(1)} collective-permute-done((bf16[256,1536]{1,0:T(8,128)(2,1)S(1)}, bf16[256,1536]{1,0:T(8,128)(2,1)S(1)}, u32[]{:S(2)}, u32[]{:S(2)}) %collective-permute-start.40) | collective-permute-done | bytes 786464 | tf_op jit(solution)/shard_map/ppermute | solution.py:357
  485.4 5.3 collective-permute-done.41
  496.3 3.7 collective-permute-done.59
  503.2 7.8 %collective-permute-done.47 = f32[192,768]{1,0:T(8,128)} collective-permute-done((f32[192,768]{1,0:T(8,128)}, f32[192,768]{1,0:T(8,128)}, u32[]{:S(2)}, u32[]{:S(2)}) %collective-permute-start.47) | collective-permute-done | bytes 589856 | tf_op jit(solution)/shard_map/ppermute | solution.py:357
  522.4 12.9 %collective-permute-done.43 = bf16[256,1536]{1,0:T(8,128)(2,1)S(1)} collective-permute-done((bf16[256,1536]{1,0:T(8,128)(2,1)S(1)}, bf16[256,1536]{1,0:T(8,128)(2,1)S(1)}, u32[]{:S(2)}, u32[]{:S(2)}) %collective-permute-start.43) | collective-permute-done | bytes 786464 | tf_op jit(solution)/shard_map/ppermute | solution.py:418
  (405 shorter events, 204.1 us)
Async XLA Ops:
  2.8 28.3 %collective-permute-start.5 = (bf16[384,768]{1,0:T(8,128)(2,1)}, bf16[384,768]{1,0:T(8,128)(2,1)}, u32[]{:S(2)}, u32[]{:S(2)}) collective-permute-start(bf16[384,768]{1,0:T(8,128)(2,1)} %bitcast.61), channel_id=1, source_target_pairs={{0,16},{8,24},{16,0},{24,8},{1,17},{9,25},{17,1},{25,9},{2,18},{10... | collective-permute-start | bytes 1769480 | tf_op jit(solution)/shard_map/ppermute | solution.py:357
  5.8 28.0 %collective-permute-start.6 = (bf16[384,768]{1,0:T(8,128)(2,1)}, bf16[384,768]{1,0:T(8,128)(2,1)}, u32[]{:S(2)}, u32[]{:S(2)}) collective-permute-start(bf16[384,768]{1,0:T(8,128)(2,1)} %bitcast.62), channel_id=1, source_target_pairs={{0,1},{1,0},{2,3},{3,2},{4,5},{5,4},{6,7},{7,6},{8,9},{9,8},{10,11... | collective-permute-start | bytes 1769480 | tf_op jit(solution)/shard_map/ppermute | solution.py:357
  7.4 42.7 %collective-permute-start.7 = (bf16[384,768]{1,0:T(8,128)(2,1)}, bf16[384,768]{1,0:T(8,128)(2,1)}, u32[]{:S(2)}, u32[]{:S(2)}) collective-permute-start(bf16[384,768]{1,0:T(8,128)(2,1)} %bitcast.63), channel_id=1, source_target_pairs={{0,2},{1,3},{2,0},{3,1},{4,6},{5,7},{6,4},{7,5},{8,10},{9,11},{10,... | collective-permute-start | bytes 1769480 | tf_op jit(solution)/shard_map/ppermute | solution.py:357
  10.0 40.1 %collective-permute-start.8 = (bf16[384,768]{1,0:T(8,128)(2,1)}, bf16[384,768]{1,0:T(8,128)(2,1)}, u32[]{:S(2)}, u32[]{:S(2)}) collective-permute-start(bf16[384,768]{1,0:T(8,128)(2,1)} %bitcast.64), channel_id=1, source_target_pairs={{0,3},{1,2},{2,1},{3,0},{4,7},{5,6},{6,5},{7,4},{8,11},{9,10},{10,... | collective-permute-start | bytes 1769480 | tf_op jit(solution)/shard_map/ppermute | solution.py:357
  10.2 39.9 %collective-permute-start.4 = (bf16[384,768]{1,0:T(8,128)(2,1)}, bf16[384,768]{1,0:T(8,128)(2,1)}, u32[]{:S(2)}, u32[]{:S(2)}) collective-permute-start(bf16[384,768]{1,0:T(8,128)(2,1)} %param.18), channel_id=1, source_target_pairs={{0,16},{8,24},{16,0},{24,8},{1,17},{9,25},{17,1},{25,9},{2,18},{10... | collective-permute-start | bytes 1769480 | tf_op jit(solution)/shard_map/ppermute | solution.py:357
  31.2 23.6 %collective-permute-start = (bf16[384,1152]{1,0:T(8,128)(2,1)S(1)}, bf16[384,1152]{1,0:T(8,128)(2,1)S(1)}, u32[]{:S(2)}, u32[]{:S(2)}) collective-permute-start(bf16[384,1152]{1,0:T(8,128)(2,1)S(1)} %get-tuple-element.164), channel_id=1, source_target_pairs={{0,16},{8,24},{16,0},{24,8},{1,17},{9,25},{17,1},{25,9},{2,18},{10... | collective-permute-start | bytes 2654216 | tf_op jit(solution)/shard_map/ppermute | solution.py:357
  127.3 135.2 %collective-permute-start.23 = (bf16[384,2304]{1,0:T(8,128)(2,1)}, bf16[384,2304]{1,0:T(8,128)(2,1)}, u32[]{:S(2)}, u32[]{:S(2)}) collective-permute-start(bf16[384,2304]{1,0:T(8,128)(2,1)} %constant_dynamic-update-slice_fusion.28), channel_id=1, source_target_pairs={{0,16},{8,24},{16,0},{24,8},{1,17},{9,25},{17,1},{25,9},{2,18},{10... | collective-permute-start | bytes 5308424 | tf_op jit(solution)/shard_map/ppermute | solution.py:357
  151.4 107.7 %collective-permute-start.57 = (f32[384,768]{1,0:T(8,128)}, f32[384,768]{1,0:T(8,128)}, u32[]{:S(2)}, u32[]{:S(2)}) collective-permute-start(f32[384,768]{1,0:T(8,128)} %constant_dynamic-slice_fusion.1), channel_id=1, source_target_pairs={{0,8},{8,0},{16,24},{24,16},{1,9},{9,1},{17,25},{25,17},{2,10},{10... | collective-permute-start | bytes 3538952 | tf_op jit(solution)/shard_map/ppermute | solution.py:357
  219.6 23.0 %collective-permute-start.38 = (f32[256,256]{1,0:T(8,128)S(1)}, f32[256,256]{1,0:T(8,128)S(1)}, u32[]{:S(2)}, u32[]{:S(2)}) collective-permute-start(f32[256,256]{1,0:T(8,128)S(1)} %get-tuple-element.145), channel_id=1, source_target_pairs={{0,3},{1,2},{2,1},{3,0},{4,7},{5,6},{6,5},{7,4},{8,11},{9,10},{10,... | collective-permute-start | bytes 786440 | tf_op jit(solution)/shard_map/ppermute | solution.py:357
  230.0 32.8 %collective-permute-start.45 = (f32[384,768]{1,0:T(8,128)}, f32[384,768]{1,0:T(8,128)}, u32[]{:S(2)}, u32[]{:S(2)}) collective-permute-start(f32[384,768]{1,0:T(8,128)} %constant_dynamic-slice_fusion.10), channel_id=1, source_target_pairs={{0,8},{8,0},{16,24},{24,16},{1,9},{9,1},{17,25},{25,17},{2,10},{10... | collective-permute-start | bytes 3538952 | tf_op jit(solution)/shard_map/ppermute | solution.py:357
  240.4 26.2 %collective-permute-start.31 = (bf16[256,1536]{1,0:T(8,128)(2,1)}, bf16[256,1536]{1,0:T(8,128)(2,1)}, u32[]{:S(2)}, u32[]{:S(2)}) collective-permute-start(bf16[256,1536]{1,0:T(8,128)(2,1)} %fusion.7), channel_id=1, source_target_pairs={{0,1},{3,2},{4,5},{7,6},{8,9},{11,10},{12,13},{15,14},{16,17},{19,... | collective-permute-start | bytes 2359304 | tf_op jit(solution)/shard_map/ppermute | solution.py:403
  252.0 28.9 %collective-permute-start.49 = (f32[384,896]{1,0:T(8,128)}, f32[384,896]{1,0:T(8,128)S(1)}, u32[]{:S(2)}, u32[]{:S(2)}) collective-permute-start(f32[384,896]{1,0:T(8,128)} %constant_dynamic-slice_fusion.7), channel_id=1, source_target_pairs={{0,8},{8,0},{16,24},{24,16},{1,9},{9,1},{17,25},{25,17},{2,10},{10... | collective-permute-start | bytes 4128776 | tf_op jit(solution)/shard_map/ppermute | solution.py:357
  262.6 27.5 %collective-permute-start.22 = (bf16[384,2304]{1,0:T(8,128)(2,1)S(1)}, bf16[384,2304]{1,0:T(8,128)(2,1)S(1)}, u32[]{:S(2)}, u32[]{:S(2)}) collective-permute-start(bf16[384,2304]{1,0:T(8,128)(2,1)S(1)} %copy-done.23), channel_id=1, source_target_pairs={{0,8},{8,0},{16,24},{24,16},{1,9},{9,1},{17,25},{25,17},{2,10},{10... | collective-permute-start | bytes 5308424 | tf_op jit(solution)/shard_map/ppermute | solution.py:357
  262.8 28.0 %collective-permute-start.24 = (bf16[384,2304]{1,0:T(8,128)(2,1)}, bf16[384,2304]{1,0:T(8,128)(2,1)S(1)}, u32[]{:S(2)}, u32[]{:S(2)}) collective-permute-start(bf16[384,2304]{1,0:T(8,128)(2,1)} %collective-permute-done.23), channel_id=1, source_target_pairs={{0,8},{8,0},{16,24},{24,16},{1,9},{9,1},{17,25},{25,17},{2,10},{10... | collective-permute-start | bytes 5308424 | tf_op jit(solution)/shard_map/ppermute | solution.py:357
  270.8 24.0 %collective-permute-start.17 = (bf16[256,768]{1,0:T(8,128)(2,1)S(1)}, bf16[256,768]{1,0:T(8,128)(2,1)S(1)}, u32[]{:S(2)}, u32[]{:S(2)}) collective-permute-start(bf16[256,768]{1,0:T(8,128)(2,1)S(1)} %copy-done.38), channel_id=1, source_target_pairs={{0,1},{1,0},{2,3},{3,2},{4,5},{5,4},{6,7},{7,6},{8,9},{9,8},{10,11... | collective-permute-start | bytes 1179656 | tf_op jit(solution)/shard_map/ppermute | solution.py:357
  278.0 29.8 %collective-permute-start.18 = (bf16[256,768]{1,0:T(8,128)(2,1)S(1)}, bf16[256,768]{1,0:T(8,128)(2,1)S(1)}, u32[]{:S(2)}, u32[]{:S(2)}) collective-permute-start(bf16[256,768]{1,0:T(8,128)(2,1)S(1)} %copy-done.37), channel_id=1, source_target_pairs={{0,2},{1,3},{2,0},{3,1},{4,6},{5,7},{6,4},{7,5},{8,10},{9,11},{10,... | collective-permute-start | bytes 1179656 | tf_op jit(solution)/shard_map/ppermute | solution.py:357
  287.0 22.1 %collective-permute-start.19 = (bf16[256,768]{1,0:T(8,128)(2,1)S(1)}, bf16[256,768]{1,0:T(8,128)(2,1)S(1)}, u32[]{:S(2)}, u32[]{:S(2)}) collective-permute-start(bf16[256,768]{1,0:T(8,128)(2,1)S(1)} %copy-done.36), channel_id=1, source_target_pairs={{0,3},{1,2},{2,1},{3,0},{4,7},{5,6},{6,5},{7,4},{8,11},{9,10},{10,... | collective-permute-start | bytes 1179656 | tf_op jit(solution)/shard_map/ppermute | solution.py:357
  290.1 34.3 %collective-permute-start.29 = (bf16[256,1536]{1,0:T(8,128)(2,1)}, bf16[256,1536]{1,0:T(8,128)(2,1)S(1)}, u32[]{:S(2)}, u32[]{:S(2)}) collective-permute-start(bf16[256,1536]{1,0:T(8,128)(2,1)} %fusion.7), channel_id=1, source_target_pairs={{1,2},{2,1},{5,6},{6,5},{9,10},{10,9},{13,14},{14,13},{17,18},{18,... | collective-permute-start | bytes 2359304 | tf_op jit(solution)/shard_map/ppermute | solution.py:404
  290.8 33.5 %collective-permute-start.30 = (bf16[256,1536]{1,0:T(8,128)(2,1)S(1)}, bf16[256,1536]{1,0:T(8,128)(2,1)S(1)}, u32[]{:S(2)}, u32[]{:S(2)}) collective-permute-start(bf16[256,1536]{1,0:T(8,128)(2,1)S(1)} %copy-done.31), channel_id=1, source_target_pairs={{0,1},{1,0},{2,3},{3,2},{4,5},{5,4},{6,7},{7,6},{8,9},{9,8},{10,11... | collective-permute-start | bytes 2359304 | tf_op jit(solution)/shard_map/ppermute | solution.py:357
  294.8 119.8 %collective-permute-start.56 = (f32[384,768]{1,0:T(8,128)}, f32[384,768]{1,0:T(8,128)}, u32[]{:S(2)}, u32[]{:S(2)}) collective-permute-start(f32[384,768]{1,0:T(8,128)} %get-tuple-element.150), channel_id=1, source_target_pairs={{0,8},{8,0},{16,24},{24,16},{1,9},{9,1},{17,25},{25,17},{2,10},{10... | collective-permute-start | bytes 3538952 | tf_op jit(solution)/shard_map/ppermute | solution.py:357
  307.8 108.2 %collective-permute-start.58 = (f32[384,768]{1,0:T(8,128)}, f32[384,768]{1,0:T(8,128)}, u32[]{:S(2)}, u32[]{:S(2)}) collective-permute-start(f32[384,768]{1,0:T(8,128)} %get-tuple-element.151), channel_id=1, source_target_pairs={{0,16},{8,24},{16,0},{24,8},{1,17},{9,25},{17,1},{25,9},{2,18},{10... | collective-permute-start | bytes 3538952 | tf_op jit(solution)/shard_map/ppermute | solution.py:357
  309.2 56.3 %collective-permute-start.32 = (bf16[256,1536]{1,0:T(8,128)(2,1)S(1)}, bf16[256,1536]{1,0:T(8,128)(2,1)S(1)}, u32[]{:S(2)}, u32[]{:S(2)}) collective-permute-start(bf16[256,1536]{1,0:T(8,128)(2,1)S(1)} %fusion.6), channel_id=1, source_target_pairs={{0,2},{1,3},{2,0},{3,1},{4,6},{5,7},{6,4},{7,5},{8,10},{9,11},{10,... | collective-permute-start | bytes 2359304 | tf_op jit(solution)/shard_map/ppermute | solution.py:357
  324.4 94.1 %collective-permute-start.44 = (f32[384,768]{1,0:T(8,128)}, f32[384,768]{1,0:T(8,128)}, u32[]{:S(2)}, u32[]{:S(2)}) collective-permute-start(f32[384,768]{1,0:T(8,128)} %get-tuple-element.152), channel_id=1, source_target_pairs={{0,8},{8,0},{16,24},{24,16},{1,9},{9,1},{17,25},{25,17},{2,10},{10... | collective-permute-start | bytes 3538952 | tf_op jit(solution)/shard_map/ppermute | solution.py:357
  324.4 96.3 %collective-permute-start.46 = (f32[384,768]{1,0:T(8,128)}, f32[384,768]{1,0:T(8,128)}, u32[]{:S(2)}, u32[]{:S(2)}) collective-permute-start(f32[384,768]{1,0:T(8,128)} %get-tuple-element.153), channel_id=1, source_target_pairs={{0,16},{8,24},{16,0},{24,8},{1,17},{9,25},{17,1},{25,9},{2,18},{10... | collective-permute-start | bytes 3538952 | tf_op jit(solution)/shard_map/ppermute | solution.py:357
  413.9 99.8 %collective-permute-start.48 = (f32[384,896]{1,0:T(8,128)}, f32[384,896]{1,0:T(8,128)}, u32[]{:S(2)}, u32[]{:S(2)}) collective-permute-start(f32[384,896]{1,0:T(8,128)} %get-tuple-element.148), channel_id=1, source_target_pairs={{0,8},{8,0},{16,24},{24,16},{1,9},{9,1},{17,25},{25,17},{2,10},{10... | collective-permute-start | bytes 4128776 | tf_op jit(solution)/shard_map/ppermute | solution.py:357
  414.5 100.5 %collective-permute-start.50 = (f32[384,896]{1,0:T(8,128)}, f32[384,896]{1,0:T(8,128)}, u32[]{:S(2)}, u32[]{:S(2)}) collective-permute-start(f32[384,896]{1,0:T(8,128)} %get-tuple-element.149), channel_id=1, source_target_pairs={{0,16},{8,24},{16,0},{24,8},{1,17},{9,25},{17,1},{25,9},{2,18},{10... | collective-permute-start | bytes 4128776 | tf_op jit(solution)/shard_map/ppermute | solution.py:357
  416.1 34.5 %collective-permute-start.25 = (bf16[256,1536]{1,0:T(8,128)(2,1)}, bf16[256,1536]{1,0:T(8,128)(2,1)S(1)}, u32[]{:S(2)}, u32[]{:S(2)}) collective-permute-start(bf16[256,1536]{1,0:T(8,128)(2,1)} %get-tuple-element.175), channel_id=1, source_target_pairs={{0,1},{1,0},{2,3},{3,2},{4,5},{5,4},{6,7},{7,6},{8,9},{9,8},{10,11... | collective-permute-start | bytes 2359304 | tf_op jit(solution)/shard_map/ppermute | solution.py:357
  418.5 38.6 %collective-permute-start.26 = (bf16[256,1536]{1,0:T(8,128)(2,1)}, bf16[256,1536]{1,0:T(8,128)(2,1)S(1)}, u32[]{:S(2)}, u32[]{:S(2)}) collective-permute-start(bf16[256,1536]{1,0:T(8,128)(2,1)} %get-tuple-element.175), channel_id=1, source_target_pairs={{0,2},{1,3},{2,0},{3,1},{4,6},{5,7},{6,4},{7,5},{8,10},{9,11},{10,... | collective-permute-start | bytes 2359304 | tf_op jit(solution)/shard_map/ppermute | solution.py:357
  420.7 62.7 %collective-permute-start.40 = (bf16[256,1536]{1,0:T(8,128)(2,1)S(1)}, bf16[256,1536]{1,0:T(8,128)(2,1)S(1)}, u32[]{:S(2)}, u32[]{:S(2)}) collective-permute-start(bf16[256,1536]{1,0:T(8,128)(2,1)S(1)} %get-tuple-element.143), channel_id=1, source_target_pairs={{0,1},{1,0},{2,3},{3,2},{4,5},{5,4},{6,7},{7,6},{8,9},{9,8},{10,11... | collective-permute-start | bytes 2359304 | tf_op jit(solution)/shard_map/ppermute | solution.py:357
  450.5 40.2 %collective-permute-start.41 = (bf16[256,1536]{1,0:T(8,128)(2,1)S(1)}, bf16[256,1536]{1,0:T(8,128)(2,1)S(1)}, u32[]{:S(2)}, u32[]{:S(2)}) collective-permute-start(bf16[256,1536]{1,0:T(8,128)(2,1)S(1)} %get-tuple-element.143), channel_id=1, source_target_pairs={{0,2},{1,3},{2,0},{3,1},{4,6},{5,7},{6,4},{7,5},{8,10},{9,11},{10,... | collective-permute-start | bytes 2359304 | tf_op jit(solution)/shard_map/ppermute | solution.py:357
  457.1 61.0 %collective-permute-start.27 = (bf16[256,1536]{1,0:T(8,128)(2,1)}, bf16[256,1536]{1,0:T(8,128)(2,1)}, u32[]{:S(2)}, u32[]{:S(2)}) collective-permute-start(bf16[256,1536]{1,0:T(8,128)(2,1)} %get-tuple-element.175), channel_id=1, source_target_pairs={{1,2},{2,1},{5,6},{6,5},{9,10},{10,9},{13,14},{14,13},{17,18},{18,... | collective-permute-start | bytes 2359304 | tf_op jit(solution)/shard_map/ppermute | solution.py:417
  513.7 21.6 %collective-permute-start.43 = (bf16[256,1536]{1,0:T(8,128)(2,1)S(1)}, bf16[256,1536]{1,0:T(8,128)(2,1)S(1)}, u32[]{:S(2)}, u32[]{:S(2)}) collective-permute-start(bf16[256,1536]{1,0:T(8,128)(2,1)S(1)} %copy-done.33), channel_id=1, source_target_pairs={{1,0},{2,3},{5,4},{6,7},{9,8},{10,11},{13,12},{14,15},{17,16},{18,... | collective-permute-start | bytes 2359304 | tf_op jit(solution)/shard_map/ppermute | solution.py:418
  (106 other events, 1266.4 us)

commit v5 on v4

--- a/solution.py
+++ b/solution.py
@@ -412,11 +412,23 @@
     def all_pieces(self, own):
         if self.size != 4:
             return [own] + [self.send(own, m) for m in range(1, self.size)]
-        across = self.send(own, 2)
-        near = self.send(own, 1)
-        middle = lax.ppermute(own, self.axis, [(1, 2), (2, 1)])
-        handed = lax.ppermute(across, self.axis, [(1, 0), (2, 3)])
-        return [own, near, across, middle + handed]
+        right, left = [(i, i + 1) for i in range(3)], [(i + 1, i) for i in range(3)]
+        before = lax.ppermute(own, self.axis, right)
+        after = lax.ppermute(own, self.axis, left)
+        across = lax.ppermute(before, self.axis, right[1:]) + lax.ppermute(after, self.axis, left[:2])
+        ends = lax.ppermute(across, self.axis, [(2, 3), (1, 0)])
+        near = jnp.where(self.me % 2 == 1, before, after)
+        far = jnp.where(self.me == 1, after, jnp.where(self.me == 2, before, ends))
+        return [own, near, across, far]
+
+    def total(self, value):
+        if not self.paired:
+            return lax.psum(value, self.axis)
+        step = 1
+        while step < self.size:
+            value = value + self.send(value, step)
+            step *= 2
+        return value
 
 
 def body(
@@ -519,10 +531,9 @@
     )(x_raw, bc_raw, edge, conv_weight, conv_bias, step, rate_row, spread_mat, lower2)
     decay = jnp.repeat(jnp.exp(totals[0, :heads]), HEAD_DIM)[None, :]
     s_in = chain(s_local, decay, CONTEXT, 1)
-    totals, far_z, far_out, others = lax.optimization_barrier((totals, far_z, far_out, others))
+    totals, far_z, far_out = lax.optimization_barrier((totals, far_z, far_out))
     full_z = ring.join(ring.near(far_z))
     full_out = ring.join(ring.near(far_out))
-    all_others = ring.near(ring.far(jnp.concatenate(others, axis=1)))
     z_part = dot(normed, full_z)
     ggo = jnp.dot(out_cotangent, full_out, preferred_element_type=f32)
     mixer, enter, leave, sums = pl.pallas_call(
@@ -542,6 +553,8 @@
         compiler_params=params,
         name="forward",
     )(act, step, cum, z_part, ggo, s_in, d_row, gain_row, spread_mat)
+    mixer, others = lax.optimization_barrier((mixer, others))
+    all_others = ring.near(ring.far(jnp.concatenate(others, axis=1)))
     parts = [line.send(sums, m) for m in range(1, ranks)]
     for part in parts:
         sums = sums + part
@@ -569,10 +582,6 @@
 
     mixed = [line.send(block(gated_out, line.target(m)), m) for m in range(1, ranks)]
     grad_w_out = dot_tn(out_cotangent, gated_out)
-    grad_w_z = dot_tn(normed, grad_z)
-    summed_out, summed_z = ring.reduce_rows(grad_w_out), ring.reduce_rows(grad_w_z)
-    summed_out, summed_z = range_ring.reduce_rows(summed_out).T, range_ring.reduce_rows(summed_z)
-
     gx, gx_tail, pre_head, dbc, gstep, conv_acc, rate_acc = pl.pallas_call(
         backward_kernel,
         grid=(count,),
@@ -600,7 +609,7 @@
     bc_own = block(dbc, line.me)
     for value in got:
         bc_own = bc_own + value
-    pieces = [bc_own] + [line.send(bc_own, m) for m in range(1, ranks)]
+    pieces = line.all_pieces(bc_own)
     for m in range(ranks):
         dbc = lax.dynamic_update_slice_in_dim(dbc, pieces[m], line.source(m) * quarter, 0)
     pre_bc = pre[:, inner:]
@@ -635,6 +644,9 @@
     grad_a_log = rate_acc[0] * rate_row[0]
 
     gx, late_z = lax.optimization_barrier((gx, grad_z))
+    grad_w_z = dot_tn(normed, late_z)
+    summed_out, summed_z = ring.reduce_rows(grad_w_out), ring.reduce_rows(grad_w_z)
+    summed_out, summed_z = range_ring.reduce_rows(summed_out).T, range_ring.reduce_rows(summed_z)
     g_xdt = jnp.concatenate([gx, g_dt], axis=1)
     grad_w_xdt = dot_tn(normed, g_xdt)
     summed_xdt = ring.reduce_rows(grad_w_xdt)
@@ -660,12 +672,12 @@
             block_output, pieces[m], line.source(m) * quarter, 0
         )
 
-    x_own, inv_own = block(x_float, line.me), block(inverse, line.me)
+    x_own, inv_own = block(block_input, line.me).astype(f32), block(inverse, line.me)
     scaled = norm_gain * gn
     delta = inv_own * scaled - x_own * (inv_own * inv_own * inv_own) * jnp.mean(
         scaled * x_own, axis=1, keepdims=True
     )
-    delta = delta.astype(bf16)
+    delta = lax.optimization_barrier(delta.astype(bf16))
     grad_norm_gain = jnp.sum(gn * x_own * inv_own, axis=0)
     pieces = line.all_pieces(delta)
     back_pieces = pieces
@@ -686,15 +698,14 @@
     wide_lanes = packed.shape[1]
     spare = (-width) % wide_lanes
     gain_rows = jnp.pad(grad_norm_gain, (0, spare)).reshape(-1, wide_lanes)
-    packed = lax.psum(jnp.concatenate([packed, gain_rows], axis=0), (SHARD, CONTEXT))
+    packed = ring.total(jnp.concatenate([packed, gain_rows], axis=0))
+    packed = range_ring.total(packed)
     gain_rows = packed[8:]
     parts = [gain_rows] + [line.send(gain_rows, m) for m in range(1, ranks)]
     ordered = jnp.zeros((ranks,) + gain_rows.shape, f32)
     for m in range(ranks):
         ordered = lax.dynamic_update_slice_in_dim(ordered, parts[m][None], line.source(m), 0)
     sum_norm_gain = jnp.sum(ordered, axis=0).reshape(-1)[:width]
-    if ranks > 1:
-        packed, back_pieces[1] = lax.optimization_barrier((packed, back_pieces[1]))
     input_grad = jnp.zeros((length, width), f32)
     for m in range(ranks):
         rank = line.source(m)

time: 550 us -> 556 us (1.011)
  blocking collectives: 24.8 us -> 0 us
  waiting for transfers between devices: 190 us -> 211 us
  local copies, waits for them, and re-layouts: 50.9 us -> 57.7 us
    ppermute x4 -> x15, waiting for transfers between devices: 15 us -> 95.6 us  [the longest x3 38.5 us: all_pieces(): ends = lax.ppermute(across, self.axis, [(2, 3), (1, 0)])]
    ppermute x52 -> x48, waiting for transfers between devices: 173 us -> 114 us  [send(): return lax.ppermute(value, self.axis, pairs)]
    psum x1 -> x0, blocking collectives: 24.8 us -> none  [body(): lax.psum(jnp.concatenate([packed, gain_rows], axis=0), (SHARD, CONTEXT))]
    ppermute x4 -> x15, starting transfers between devices: 4.81 us -> 25.6 us  [the longest x3 11.3 us: all_pieces(): before = lax.ppermute(own, self.axis, right)]
    ppermute x52 -> x48, starting transfers between devices: 73.2 us -> 53 us  [send(): return lax.ppermute(value, self.axis, pairs)]
    dynamic_update_slice x14, local copies, waits for them, and re-layouts: 4.23 us -> 12.1 us  [join(): lax.dynamic_update_slice_in_dim(full, piece, self.source(m) * rows, 0)]
    unnamed x156 -> x144, local copies, waits for them, and re-layouts: 14.9 us -> 15.4 us
  transfers between devices with their start and end apart: 63 -> 70, of which waited for: 22 -> 25; matrix products, arithmetic and copies ran while one was open for 28% -> 30% of each run, Pallas kernels for 7% -> 9%
where the time goes in v5:
time: 556 us; the launch traced here: 545 us
  waiting for transfers between devices  211 us (38%)
  starting transfers between devices  93.1 us (17%)
  other arithmetic  65.7 us (12%)
  Pallas kernels  62.8 us (11%)
  local copies, waits for them, and re-layouts  57.7 us (10%)
  matrix products  53 us (10%)
    ppermute x48, waiting for transfers between devices, send(): return lax.ppermute(value, self.axis, pairs)  114 us
    ppermute x48, starting transfers between devices, send(): return lax.ppermute(value, self.axis, pairs)  53 us
    ppermute x3, waiting for transfers between devices, all_pieces(): ends = lax.ppermute(across, self.axis, [(2, 3), (1, 0)])  38.5 us
    pallas_call x1, Pallas kernels, body(): pl.pallas_call(backward_kernel, grid=(count,), in_specs=[back(inner), bac...  26.9 us
    ppermute x3, waiting for transfers between devices, all_pieces(): lax.ppermute(after, self.axis, left[:2])  22.8 us
    dot_general x11, matrix products, dot_t(): lax.dot_general(a, b, (((1,), (1,)), ((), ())), preferred_element_type=f32)  21.9 us
    ppermute x3, waiting for transfers between devices, all_pieces(): after = lax.ppermute(own, self.axis, left)  17.7 us
    ppermute x3, waiting for transfers between devices, all_pieces(): before = lax.ppermute(own, self.axis, right)  16.6 us
  transfers between devices with their start and end apart: 70, of which 25 were waited for; matrix products, arithmetic and copies ran while one was open for 30% of the time, Pallas kernels for 9%

profile of v5, /device:TPU:0, one launch (start us, length us, event | category | flops | bytes accessed | tf_op | source)
XLA Modules:
  0.0 545.5 jit_solution(15143811446638047862)
XLA Ops:
  32.9 7.8 %collective-permute-done.5 = bf16[384,768]{1,0:T(8,128)(2,1)} collective-permute-done((bf16[384,768]{1,0:T(8,128)(2,1)}, bf16[384,768]{1,0:T(8,128)(2,1)}, u32[]{:S(2)}, u32[]{:S(2)}) %collective-permute-start.5) | collective-permute-done | bytes 589856 | tf_op jit(solution)/shard_map/ppermute | solution.py:357
  40.7 11.8 %collective-permute-done.4 = bf16[384,768]{1,0:T(8,128)(2,1)} collective-permute-done((bf16[384,768]{1,0:T(8,128)(2,1)}, bf16[384,768]{1,0:T(8,128)(2,1)}, u32[]{:S(2)}, u32[]{:S(2)}) %collective-permute-start.4) | collective-permute-done | bytes 589856 | tf_op jit(solution)/shard_map/ppermute | solution.py:357
  63.9 4.3 fusion.104.z_ref
  68.4 4.3 fusion.111
  80.5 11.4 %front.1 = (f32[1024,1024]{1,0:T(8,128)}, f32[1024,1024]{1,0:T(8,128)}, f32[1024,128]{1,0:T(8,128)}, f32[128,768]{1,0:T(8,128)}, f32[8,128]{1,0:T(8,128)}) custom-call(bf16[1024,768]{1,0:T(8,128)(2,1)} %slice.203.x_ref.x_raw_ref, bf16[1024,256]{1,0:T(8,128)(2,1)} %get-tuple-element.157.bc_ref, f32[8,1024]{1,0:T(8,128)} %pad.35.edge_ref, ...), custom_call_target="tpu_custom_call" | custom-call | tf_op jit(solution)/shard_map/front/pallas_call | solution.py:516
  91.9 4.1 collective-permute-start.10
  96.0 6.9 %convolution_bitcast_fusion.1.ggo_ref = f32[1024,768]{1,0:T(8,128)} fusion(bf16[1024,1536]{1,0:T(8,128)(2,1)} %param.31, bf16[1536,768]{1,0:T(8,128)(2,1)} %copy-done.6), kind=kOutput, calls=%fused_computation.31 | convolution fusion | flops 2415919104 | bytes 8650752 | tf_op jit(solution)/shard_map/dot_general | solution.py:538
  104.2 13.5 %forward.1 = (f32[1024,768]{1,0:T(8,128)}, f32[1024,768]{1,0:T(8,128)}, f32[1024,768]{1,0:T(8,128)}, f32[8,1024]{1,0:T(8,128)}) custom-call(f32[1024,1024]{1,0:T(8,128)} %get-tuple-element.50.act_ref, f32[1024,128]{1,0:T(8,128)} %compare_select_fusion.step_ref, f32[1024,128]{1,0:T(8,128)} %get-tuple-element.51.cum_ref, f32[1024,768]{1,0:T(8,128)} %fusion.104.z_ref, ...), custom_call_target="tpu_custom_call" | custom-call | tf_op jit(solution)/shard_map/forward/pallas_call | solution.py:539
  129.2 11.0 %gate.1 = (bf16[1024,768]{1,0:T(8,128)(2,1)}, f32[1024,768]{1,0:T(8,128)}, bf16[1024,768]{1,0:T(8,128)(2,1)}, f32[128,768]{1,0:T(8,128)}, f32[8,768]{1,0:T(8,128)}) custom-call(f32[1024,768]{1,0:T(8,128)} %get-tuple-element.58.mixer_ref, f32[1024,768]{1,0:T(8,128)} %fusion.104.z_ref, f32[1024,768]{1,0:T(8,128)} %convolution_bitcast_fusion.1.ggo_ref, ...), custom_call_target="tpu_custom_call" | custom-call | tf_op jit(solution)/shard_map/gate/pallas_call | solution.py:562
  141.5 5.0 convolution_bitcast_fusion
  152.1 26.9 %backward.1 = (bf16[1024,768]{1,0:T(8,128)(2,1)}, f32[8,768]{1,0:T(8,128)}, f32[8,768]{1,0:T(8,128)}, f32[1024,256]{1,0:T(8,128)}, f32[1024,128]{1,0:T(8,128)}, /*index=5*/f32[8,768]{1,0:T(8,128)}, f32[8,128]{1,0:T(8,128)}) custom-call(f32[1024,768]{1,0:T(8,128)} %get-tuple-element.61.gm_ref, f32[1024,1024]{1,0:T(8,128)} %get-tuple-element.50.act_ref, ...), custom_call_target="tpu_custom_call" | custom-call | tf_op jit(solution)/shard_map/backward/pallas_call | solution.py:585
  217.6 11.8 %collective-permute-done.37 = f32[256,256]{1,0:T(8,128)S(1)} collective-permute-done((f32[256,256]{1,0:T(8,128)S(1)}, f32[256,256]{1,0:T(8,128)S(1)}, u32[]{:S(2)}, u32[]{:S(2)}) %collective-permute-start.37) | collective-permute-done | bytes 262176 | tf_op jit(solution)/shard_map/ppermute | solution.py:416
  232.5 8.7 %collective-permute-start.31 = (bf16[256,1536]{1,0:T(8,128)(2,1)}, bf16[256,1536]{1,0:T(8,128)(2,1)}, u32[]{:S(2)}, u32[]{:S(2)}) collective-permute-start(bf16[256,1536]{1,0:T(8,128)(2,1)} %fusion.11), channel_id=1, source_target_pairs={{0,1},{1,0},{2,3},{3,2},{4,5},{5,4},{6,7},{7,6},{8,9},{9,8},{10,11... | collective-permute-start | bytes 2359304 | tf_op jit(solution)/shard_map/ppermute | solution.py:357
  241.2 5.2 collective-permute-done.40
  251.3 14.0 %collective-permute-done.41 = f32[256,256]{1,0:T(8,128)S(1)} collective-permute-done((f32[256,256]{1,0:T(8,128)S(1)}, f32[256,256]{1,0:T(8,128)S(1)}, u32[]{:S(2)}, u32[]{:S(2)}) %collective-permute-start.41) | collective-permute-done | bytes 262176 | tf_op jit(solution)/shard_map/ppermute | solution.py:419
  277.8 4.0 fusion.99
  291.9 19.1 %collective-permute-done.33 = bf16[256,1536]{1,0:T(8,128)(2,1)S(1)} collective-permute-done((bf16[256,1536]{1,0:T(8,128)(2,1)}, bf16[256,1536]{1,0:T(8,128)(2,1)S(1)}, u32[]{:S(2)}, u32[]{:S(2)}) %collective-permute-start.33) | collective-permute-done | bytes 786464 | tf_op jit(solution)/shard_map/ppermute | solution.py:357
  323.7 29.2 %collective-permute-done.65 = f32[10,1024]{1,0:T(8,128)S(1)} collective-permute-done((f32[10,1024]{1,0:T(8,128)S(1)}, f32[10,1024]{1,0:T(8,128)S(1)}, u32[]{:S(2)}, u32[]{:S(2)}) %collective-permute-start.65) | collective-permute-done | bytes 40992 | tf_op jit(solution)/shard_map/ppermute | solution.py:357
  375.8 4.5 collective-permute-done.58
  381.9 7.9 %collective-permute-done.69 = f32[2,1024]{1,0:T(2,128)S(1)} collective-permute-done((f32[2,1024]{1,0:T(2,128)S(1)}, f32[2,1024]{1,0:T(2,128)S(1)}, u32[]{:S(2)}, u32[]{:S(2)}) %collective-permute-start.69) | collective-permute-done | bytes 8224 | tf_op jit(solution)/shard_map/ppermute | solution.py:357
  392.2 6.4 %collective-permute-done.59 = f32[192,256]{1,0:T(8,128)S(1)} collective-permute-done((f32[192,256]{1,0:T(8,128)S(1)}, f32[192,256]{1,0:T(8,128)S(1)}, u32[]{:S(2)}, u32[]{:S(2)}) %collective-permute-start.59) | collective-permute-done | bytes 196640 | tf_op jit(solution)/shard_map/ppermute | solution.py:357
  403.3 8.4 %collective-permute-done.44 = bf16[256,1536]{1,0:T(8,128)(2,1)} collective-permute-done((bf16[256,1536]{1,0:T(8,128)(2,1)S(1)}, bf16[256,1536]{1,0:T(8,128)(2,1)}, u32[]{:S(2)}, u32[]{:S(2)}) %collective-permute-start.44) | collective-permute-done | bytes 786464 | tf_op jit(solution)/shard_map/ppermute | solution.py:417
  417.2 10.8 %collective-permute-done.50 = f32[384,768]{1,0:T(8,128)S(1)} collective-permute-done((f32[384,768]{1,0:T(8,128)}, f32[384,768]{1,0:T(8,128)S(1)}, u32[]{:S(2)}, u32[]{:S(2)}) %collective-permute-start.50) | collective-permute-done | bytes 1179680 | tf_op jit(solution)/shard_map/ppermute | solution.py:357
  428.0 5.7 %collective-permute-start.19 = (bf16[256,768]{1,0:T(8,128)(2,1)S(1)}, bf16[256,768]{1,0:T(8,128)(2,1)S(1)}, u32[]{:S(2)}, u32[]{:S(2)}) collective-permute-start(bf16[256,768]{1,0:T(8,128)(2,1)S(1)} %copy-done.30), channel_id=1, source_target_pairs={{0,3},{1,2},{2,1},{3,0},{4,7},{5,6},{6,5},{7,4},{8,11},{9,10},{10,... | collective-permute-start | bytes 1179656 | tf_op jit(solution)/shard_map/ppermute | solution.py:357
  453.6 4.9 collective-permute-done.63
  458.8 5.2 collective-permute-start.25
  464.0 3.8 collective-permute-done.54
  474.2 4.8 collective-permute-done.25
  479.7 9.3 %collective-permute-done.26 = bf16[256,1536]{1,0:T(8,128)(2,1)S(1)} collective-permute-done((bf16[256,1536]{1,0:T(8,128)(2,1)S(1)}, bf16[256,1536]{1,0:T(8,128)(2,1)S(1)}, u32[]{:S(2)}, u32[]{:S(2)}) %collective-permute-start.26) | collective-permute-done | bytes 786464 | tf_op jit(solution)/shard_map/ppermute | solution.py:417
  493.7 17.6 %collective-permute-done.28 = bf16[256,1536]{1,0:T(8,128)(2,1)S(1)} collective-permute-done((bf16[256,1536]{1,0:T(8,128)(2,1)S(1)}, bf16[256,1536]{1,0:T(8,128)(2,1)S(1)}, u32[]{:S(2)}, u32[]{:S(2)}) %collective-permute-start.28) | collective-permute-done | bytes 786464 | tf_op jit(solution)/shard_map/ppermute | solution.py:418
  515.6 12.6 %collective-permute-done.47 = bf16[256,1536]{1,0:T(8,128)(2,1)} collective-permute-done((bf16[256,1536]{1,0:T(8,128)(2,1)}, bf16[256,1536]{1,0:T(8,128)(2,1)}, u32[]{:S(2)}, u32[]{:S(2)}) %collective-permute-start.47) | collective-permute-done | bytes 786464 | tf_op jit(solution)/shard_map/ppermute | solution.py:419
  531.2 11.8 %collective-permute-done.29 = bf16[256,1536]{1,0:T(8,128)(2,1)} collective-permute-done((bf16[256,1536]{1,0:T(8,128)(2,1)}, bf16[256,1536]{1,0:T(8,128)(2,1)}, u32[]{:S(2)}, u32[]{:S(2)}) %collective-permute-start.29) | collective-permute-done | bytes 786464 | tf_op jit(solution)/shard_map/ppermute | solution.py:419
  (409 shorter events, 230.5 us)
Async XLA Ops:
  4.3 51.6 %collective-permute-start = (bf16[384,1152]{1,0:T(8,128)(2,1)}, bf16[384,1152]{1,0:T(8,128)(2,1)}, u32[]{:S(2)}, u32[]{:S(2)}) collective-permute-start(bf16[384,1152]{1,0:T(8,128)(2,1)} %get-tuple-element.166), channel_id=1, source_target_pairs={{0,16},{8,24},{16,0},{24,8},{1,17},{9,25},{17,1},{25,9},{2,18},{10... | collective-permute-start | bytes 2654216 | tf_op jit(solution)/shard_map/ppermute | solution.py:357
  7.3 50.0 %collective-permute-start.1 = (bf16[384,1152]{1,0:T(8,128)(2,1)}, bf16[384,1152]{1,0:T(8,128)(2,1)}, u32[]{:S(2)}, u32[]{:S(2)}) collective-permute-start(bf16[384,1152]{1,0:T(8,128)(2,1)} %get-tuple-element.166), channel_id=1, source_target_pairs={{0,8},{8,0},{16,24},{24,16},{1,9},{9,1},{17,25},{25,17},{2,10},{10... | collective-permute-start | bytes 2654216 | tf_op jit(solution)/shard_map/ppermute | solution.py:357
  9.4 31.3 %collective-permute-start.5 = (bf16[384,768]{1,0:T(8,128)(2,1)}, bf16[384,768]{1,0:T(8,128)(2,1)}, u32[]{:S(2)}, u32[]{:S(2)}) collective-permute-start(bf16[384,768]{1,0:T(8,128)(2,1)} %bitcast.2), channel_id=1, source_target_pairs={{0,16},{8,24},{16,0},{24,8},{1,17},{9,25},{17,1},{25,9},{2,18},{10... | collective-permute-start | bytes 1769480 | tf_op jit(solution)/shard_map/ppermute | solution.py:357
  9.4 111.2 %collective-permute-start.11 = (bf16[384,768]{1,0:T(8,128)(2,1)}, bf16[384,768]{1,0:T(8,128)(2,1)}, u32[]{:S(2)}, u32[]{:S(2)}) collective-permute-start(bf16[384,768]{1,0:T(8,128)(2,1)} %bitcast.2), channel_id=1, source_target_pairs={{0,1},{1,0},{2,3},{3,2},{4,5},{5,4},{6,7},{7,6},{8,9},{9,8},{10,11... | collective-permute-start | bytes 1769480 | tf_op jit(solution)/shard_map/ppermute | solution.py:357
  11.5 41.0 %collective-permute-start.4 = (bf16[384,768]{1,0:T(8,128)(2,1)}, bf16[384,768]{1,0:T(8,128)(2,1)}, u32[]{:S(2)}, u32[]{:S(2)}) collective-permute-start(bf16[384,768]{1,0:T(8,128)(2,1)} %param.18), channel_id=1, source_target_pairs={{0,16},{8,24},{16,0},{24,8},{1,17},{9,25},{17,1},{25,9},{2,18},{10... | collective-permute-start | bytes 1769480 | tf_op jit(solution)/shard_map/ppermute | solution.py:357
  59.2 63.4 %collective-permute-start.12 = (bf16[384,768]{1,0:T(8,128)(2,1)}, bf16[384,768]{1,0:T(8,128)(2,1)}, u32[]{:S(2)}, u32[]{:S(2)}) collective-permute-start(bf16[384,768]{1,0:T(8,128)(2,1)} %bitcast.2), channel_id=1, source_target_pairs={{0,2},{1,3},{2,0},{3,1},{4,6},{5,7},{6,4},{7,5},{8,10},{9,11},{10,... | collective-permute-start | bytes 1769480 | tf_op jit(solution)/shard_map/ppermute | solution.py:357
  62.1 60.5 %collective-permute-start.13 = (bf16[384,768]{1,0:T(8,128)(2,1)}, bf16[384,768]{1,0:T(8,128)(2,1)}, u32[]{:S(2)}, u32[]{:S(2)}) collective-permute-start(bf16[384,768]{1,0:T(8,128)(2,1)} %bitcast.2), channel_id=1, source_target_pairs={{0,3},{1,2},{2,1},{3,0},{4,7},{5,6},{6,5},{7,4},{8,11},{9,10},{10,... | collective-permute-start | bytes 1769480 | tf_op jit(solution)/shard_map/ppermute | solution.py:357
  149.2 97.3 %collective-permute-start.61 = (f32[384,768]{1,0:T(8,128)}, f32[384,768]{1,0:T(8,128)}, u32[]{:S(2)}, u32[]{:S(2)}) collective-permute-start(f32[384,768]{1,0:T(8,128)} %constant_dynamic-slice_fusion.1), channel_id=1, source_target_pairs={{0,8},{8,0},{16,24},{24,16},{1,9},{9,1},{17,25},{25,17},{2,10},{10... | collective-permute-start | bytes 3538952 | tf_op jit(solution)/shard_map/ppermute | solution.py:357
  183.5 25.9 %collective-permute-start.34 = (f32[256,256]{1,0:T(8,128)S(1)}, f32[256,256]{1,0:T(8,128)S(1)}, u32[]{:S(2)}, u32[]{:S(2)}) collective-permute-start(f32[256,256]{1,0:T(8,128)S(1)} %get-tuple-element.163), channel_id=1, source_target_pairs={{0,1},{1,0},{2,3},{3,2},{4,5},{5,4},{6,7},{7,6},{8,9},{9,8},{10,11... | collective-permute-start | bytes 786440 | tf_op jit(solution)/shard_map/ppermute | solution.py:357
  183.6 27.4 %collective-permute-start.35 = (f32[256,256]{1,0:T(8,128)S(1)}, f32[256,256]{1,0:T(8,128)S(1)}, u32[]{:S(2)}, u32[]{:S(2)}) collective-permute-start(f32[256,256]{1,0:T(8,128)S(1)} %get-tuple-element.165), channel_id=1, source_target_pairs={{0,2},{1,3},{2,0},{3,1},{4,6},{5,7},{6,4},{7,5},{8,10},{9,11},{10,... | collective-permute-start | bytes 786440 | tf_op jit(solution)/shard_map/ppermute | solution.py:357
  206.0 62.9 %collective-permute-start.32 = (bf16[256,1536]{1,0:T(8,128)(2,1)}, bf16[256,1536]{1,0:T(8,128)(2,1)S(1)}, u32[]{:S(2)}, u32[]{:S(2)}) collective-permute-start(bf16[256,1536]{1,0:T(8,128)(2,1)} %fusion.10), channel_id=1, source_target_pairs={{0,1},{3,2},{4,5},{7,6},{8,9},{11,10},{12,13},{15,14},{16,17},{19,... | collective-permute-start | bytes 2359304 | tf_op jit(solution)/shard_map/ppermute | solution.py:403
  209.4 82.3 %collective-permute-start.30 = (bf16[256,1536]{1,0:T(8,128)(2,1)}, bf16[256,1536]{1,0:T(8,128)(2,1)}, u32[]{:S(2)}, u32[]{:S(2)}) collective-permute-start(bf16[256,1536]{1,0:T(8,128)(2,1)} %fusion.10), channel_id=1, source_target_pairs={{1,2},{2,1},{5,6},{6,5},{9,10},{10,9},{13,14},{14,13},{17,18},{18,... | collective-permute-start | bytes 2359304 | tf_op jit(solution)/shard_map/ppermute | solution.py:404
  232.5 58.7 %collective-permute-start.31 = (bf16[256,1536]{1,0:T(8,128)(2,1)}, bf16[256,1536]{1,0:T(8,128)(2,1)}, u32[]{:S(2)}, u32[]{:S(2)}) collective-permute-start(bf16[256,1536]{1,0:T(8,128)(2,1)} %fusion.11), channel_id=1, source_target_pairs={{0,1},{1,0},{2,3},{3,2},{4,5},{5,4},{6,7},{7,6},{8,9},{9,8},{10,11... | collective-permute-start | bytes 2359304 | tf_op jit(solution)/shard_map/ppermute | solution.py:357
  246.4 38.9 %collective-permute-start.53 = (f32[384,896]{1,0:T(8,128)}, f32[384,896]{1,0:T(8,128)}, u32[]{:S(2)}, u32[]{:S(2)}) collective-permute-start(f32[384,896]{1,0:T(8,128)} %constant_dynamic-slice_fusion.7), channel_id=1, source_target_pairs={{0,8},{8,0},{16,24},{24,16},{1,9},{9,1},{17,25},{25,17},{2,10},{10... | collective-permute-start | bytes 4128776 | tf_op jit(solution)/shard_map/ppermute | solution.py:357
  274.8 36.2 %collective-permute-start.33 = (bf16[256,1536]{1,0:T(8,128)(2,1)}, bf16[256,1536]{1,0:T(8,128)(2,1)S(1)}, u32[]{:S(2)}, u32[]{:S(2)}) collective-permute-start(bf16[256,1536]{1,0:T(8,128)(2,1)} %fusion.9), channel_id=1, source_target_pairs={{0,2},{1,3},{2,0},{3,1},{4,6},{5,7},{6,4},{7,5},{8,10},{9,11},{10,... | collective-permute-start | bytes 2359304 | tf_op jit(solution)/shard_map/ppermute | solution.py:357
  285.4 96.4 %collective-permute-start.23 = (bf16[384,2304]{1,0:T(8,128)(2,1)}, bf16[384,2304]{1,0:T(8,128)(2,1)}, u32[]{:S(2)}, u32[]{:S(2)}) collective-permute-start(bf16[384,2304]{1,0:T(8,128)(2,1)} %constant_dynamic-update-slice_fusion.25), channel_id=1, source_target_pairs={{0,16},{8,24},{16,0},{24,8},{1,17},{9,25},{17,1},{25,9},{2,18},{10... | collective-permute-start | bytes 5308424 | tf_op jit(solution)/shard_map/ppermute | solution.py:357
  290.2 99.6 %collective-permute-start.60 = (f32[384,768]{1,0:T(8,128)}, f32[384,768]{1,0:T(8,128)}, u32[]{:S(2)}, u32[]{:S(2)}) collective-permute-start(f32[384,768]{1,0:T(8,128)} %get-tuple-element.152), channel_id=1, source_target_pairs={{0,8},{8,0},{16,24},{24,16},{1,9},{9,1},{17,25},{25,17},{2,10},{10... | collective-permute-start | bytes 3538952 | tf_op jit(solution)/shard_map/ppermute | solution.py:357
  291.2 100.0 %collective-permute-start.62 = (f32[384,768]{1,0:T(8,128)}, f32[384,768]{1,0:T(8,128)}, u32[]{:S(2)}, u32[]{:S(2)}) collective-permute-start(f32[384,768]{1,0:T(8,128)} %get-tuple-element.153), channel_id=1, source_target_pairs={{0,16},{8,24},{16,0},{24,8},{1,17},{9,25},{17,1},{25,9},{2,18},{10... | collective-permute-start | bytes 3538952 | tf_op jit(solution)/shard_map/ppermute | solution.py:357
  291.7 81.3 %collective-permute-start.56 = (f32[384,256]{1,0:T(8,128)}, f32[384,256]{1,0:T(8,128)}, u32[]{:S(2)}, u32[]{:S(2)}) collective-permute-start(f32[384,256]{1,0:T(8,128)} %get-tuple-element.158), channel_id=1, source_target_pairs={{0,8},{8,0},{16,24},{24,16},{1,9},{9,1},{17,25},{25,17},{2,10},{10... | collective-permute-start | bytes 1179656 | tf_op jit(solution)/shard_map/ppermute | solution.py:357
  320.0 32.8 %collective-permute-start.65 = (f32[10,1024]{1,0:T(8,128)S(1)}, f32[10,1024]{1,0:T(8,128)S(1)}, u32[]{:S(2)}, u32[]{:S(2)}) collective-permute-start(f32[10,1024]{1,0:T(8,128)S(1)} %fusion.98), channel_id=1, source_target_pairs={{0,16},{8,24},{16,0},{24,8},{1,17},{9,25},{17,1},{25,9},{2,18},{10... | collective-permute-start | bytes 122888 | tf_op jit(solution)/shard_map/ppermute | solution.py:357
  373.0 26.3 %collective-permute-start.43 = (bf16[256,1536]{1,0:T(8,128)(2,1)S(1)}, bf16[256,1536]{1,0:T(8,128)(2,1)}, u32[]{:S(2)}, u32[]{:S(2)}) collective-permute-start(bf16[256,1536]{1,0:T(8,128)(2,1)S(1)} %fusion.21), channel_id=1, source_target_pairs={{0,1},{1,2},{2,3},{4,5},{5,6},{6,7},{8,9},{9,10},{10,11},{12,13},{... | collective-permute-start | bytes 2359304 | tf_op jit(solution)/shard_map/ppermute | solution.py:416
  381.8 53.4 %collective-permute-start.22 = (bf16[384,2304]{1,0:T(8,128)(2,1)}, bf16[384,2304]{1,0:T(8,128)(2,1)}, u32[]{:S(2)}, u32[]{:S(2)}) collective-permute-start(bf16[384,2304]{1,0:T(8,128)(2,1)} %constant_dynamic-update-slice_fusion.25), channel_id=1, source_target_pairs={{0,8},{8,0},{16,24},{24,16},{1,9},{9,1},{17,25},{25,17},{2,10},{10... | collective-permute-start | bytes 5308424 | tf_op jit(solution)/shard_map/ppermute | solution.py:357
  389.8 45.5 %collective-permute-start.24 = (bf16[384,2304]{1,0:T(8,128)(2,1)}, bf16[384,2304]{1,0:T(8,128)(2,1)}, u32[]{:S(2)}, u32[]{:S(2)}) collective-permute-start(bf16[384,2304]{1,0:T(8,128)(2,1)} %collective-permute-done.23), channel_id=1, source_target_pairs={{0,8},{8,0},{16,24},{24,16},{1,9},{9,1},{17,25},{25,17},{2,10},{10... | collective-permute-start | bytes 5308424 | tf_op jit(solution)/shard_map/ppermute | solution.py:357
  399.3 28.6 %collective-permute-start.50 = (f32[384,768]{1,0:T(8,128)}, f32[384,768]{1,0:T(8,128)S(1)}, u32[]{:S(2)}, u32[]{:S(2)}) collective-permute-start(f32[384,768]{1,0:T(8,128)} %get-tuple-element.155), channel_id=1, source_target_pairs={{0,16},{8,24},{16,0},{24,8},{1,17},{9,25},{17,1},{25,9},{2,18},{10... | collective-permute-start | bytes 3538952 | tf_op jit(solution)/shard_map/ppermute | solution.py:357
  411.7 31.3 %collective-permute-start.17 = (bf16[256,768]{1,0:T(8,128)(2,1)S(1)}, bf16[256,768]{1,0:T(8,128)(2,1)S(1)}, u32[]{:S(2)}, u32[]{:S(2)}) collective-permute-start(bf16[256,768]{1,0:T(8,128)(2,1)S(1)} %copy-done.32), channel_id=1, source_target_pairs={{0,1},{1,0},{2,3},{3,2},{4,5},{5,4},{6,7},{7,6},{8,9},{9,8},{10,11... | collective-permute-start | bytes 1179656 | tf_op jit(solution)/shard_map/ppermute | solution.py:357
  416.0 29.7 %collective-permute-start.18 = (bf16[256,768]{1,0:T(8,128)(2,1)S(1)}, bf16[256,768]{1,0:T(8,128)(2,1)S(1)}, u32[]{:S(2)}, u32[]{:S(2)}) collective-permute-start(bf16[256,768]{1,0:T(8,128)(2,1)S(1)} %copy-done.31), channel_id=1, source_target_pairs={{0,2},{1,3},{2,0},{3,1},{4,6},{5,7},{6,4},{7,5},{8,10},{9,11},{10,... | collective-permute-start | bytes 1179656 | tf_op jit(solution)/shard_map/ppermute | solution.py:357
  435.3 32.6 %collective-permute-start.54 = (f32[384,896]{1,0:T(8,128)S(1)}, f32[384,896]{1,0:T(8,128)S(1)}, u32[]{:S(2)}, u32[]{:S(2)}) collective-permute-start(f32[384,896]{1,0:T(8,128)S(1)} %copy-done.25), channel_id=1, source_target_pairs={{0,16},{8,24},{16,0},{24,8},{1,17},{9,25},{17,1},{25,9},{2,18},{10... | collective-permute-start | bytes 4128776 | tf_op jit(solution)/shard_map/ppermute | solution.py:357
  445.7 44.5 %collective-permute-start.45 = (bf16[256,1536]{1,0:T(8,128)(2,1)}, bf16[256,1536]{1,0:T(8,128)(2,1)S(1)}, u32[]{:S(2)}, u32[]{:S(2)}) collective-permute-start(bf16[256,1536]{1,0:T(8,128)(2,1)} %collective-permute-done.43), channel_id=1, source_target_pairs={{1,2},{2,3},{5,6},{6,7},{9,10},{10,11},{13,14},{14,15},{17,18},{18... | collective-permute-start | bytes 2359304 | tf_op jit(solution)/shard_map/ppermute | solution.py:418
  446.5 43.8 %collective-permute-start.46 = (bf16[256,1536]{1,0:T(8,128)(2,1)}, bf16[256,1536]{1,0:T(8,128)(2,1)S(1)}, u32[]{:S(2)}, u32[]{:S(2)}) collective-permute-start(bf16[256,1536]{1,0:T(8,128)(2,1)} %collective-permute-done.44), channel_id=1, source_target_pairs={{1,0},{2,1},{5,4},{6,5},{9,8},{10,9},{13,12},{14,13},{17,16},{18,1... | collective-permute-start | bytes 2359304 | tf_op jit(solution)/shard_map/ppermute | solution.py:418
  473.0 40.7 %collective-permute-start.55 = (f32[192,896]{1,0:T(8,128)S(1)}, f32[192,896]{1,0:T(8,128)S(1)}, u32[]{:S(2)}, u32[]{:S(2)}) collective-permute-start(f32[192,896]{1,0:T(8,128)S(1)} %constant_dynamic-slice_fusion.6), channel_id=1, source_target_pairs={{0,4},{4,0},{1,5},{5,1},{2,6},{6,2},{3,7},{7,3},{8,12},{12,8},{9,1... | collective-permute-start | bytes 2064392 | tf_op jit(solution)/shard_map/ppermute | solution.py:357
  492.1 36.1 %collective-permute-start.47 = (bf16[256,1536]{1,0:T(8,128)(2,1)}, bf16[256,1536]{1,0:T(8,128)(2,1)}, u32[]{:S(2)}, u32[]{:S(2)}) collective-permute-start(bf16[256,1536]{1,0:T(8,128)(2,1)} %get-tuple-element.141), channel_id=1, source_target_pairs={{2,3},{1,0},{6,7},{5,4},{10,11},{9,8},{14,15},{13,12},{18,19},{17,... | collective-permute-start | bytes 2359304 | tf_op jit(solution)/shard_map/ppermute | solution.py:419
  512.4 30.6 %collective-permute-start.29 = (bf16[256,1536]{1,0:T(8,128)(2,1)}, bf16[256,1536]{1,0:T(8,128)(2,1)}, u32[]{:S(2)}, u32[]{:S(2)}) collective-permute-start(bf16[256,1536]{1,0:T(8,128)(2,1)} %get-tuple-element.149), channel_id=1, source_target_pairs={{2,3},{1,0},{6,7},{5,4},{10,11},{9,8},{14,15},{13,12},{18,19},{17,... | collective-permute-start | bytes 2359304 | tf_op jit(solution)/shard_map/ppermute | solution.py:419
  (107 other events, 1275.9 us)

commit v6 on v5

--- a/solution.py
+++ b/solution.py
@@ -409,17 +409,24 @@
             total = total + value.astype(f32)
         return total
 
-    def all_pieces(self, own):
+    def all_pieces(self, own, parts=1):
+        rows = own.shape[0] // parts
+        cuts = [own[p * rows : (p + 1) * rows] for p in range(parts)]
         if self.size != 4:
-            return [own] + [self.send(own, m) for m in range(1, self.size)]
-        right, left = [(i, i + 1) for i in range(3)], [(i + 1, i) for i in range(3)]
-        before = lax.ppermute(own, self.axis, right)
-        after = lax.ppermute(own, self.axis, left)
-        across = lax.ppermute(before, self.axis, right[1:]) + lax.ppermute(after, self.axis, left[:2])
-        ends = lax.ppermute(across, self.axis, [(2, 3), (1, 0)])
-        near = jnp.where(self.me % 2 == 1, before, after)
-        far = jnp.where(self.me == 1, after, jnp.where(self.me == 2, before, ends))
-        return [own, near, across, far]
+            return [
+                (m, p * rows, self.send(cut, m) if m else cut) for m in range(self.size) for p, cut in enumerate(cuts)
+            ]
+        direct = []
+        for cut in cuts:
+            middle = lax.ppermute(cut, self.axis, [(1, 2), (2, 1)])
+            cross = lax.ppermute(cut, self.axis, [(0, 2), (3, 1)])
+            direct.append((self.send(cut, 1), middle, cross))
+        found = [(0, p * rows, cut) for p, cut in enumerate(cuts)]
+        for p, (near, middle, cross) in enumerate(direct):
+            first = lax.ppermute(middle, self.axis, [(1, 0), (2, 3)])
+            second = lax.ppermute(cross, self.axis, [(1, 0), (2, 3)])
+            found += [(1, p * rows, near), (2, p * rows, cross + first), (3, p * rows, middle + second)]
+        return found
 
     def total(self, value):
         if not self.paired:
@@ -609,7 +616,7 @@
     bc_own = block(dbc, line.me)
     for value in got:
         bc_own = bc_own + value
-    pieces = line.all_pieces(bc_own)
+    pieces = [bc_own] + [line.send(bc_own, m) for m in range(1, ranks)]
     for m in range(ranks):
         dbc = lax.dynamic_update_slice_in_dim(dbc, pieces[m], line.source(m) * quarter, 0)
     pre_bc = pre[:, inner:]
@@ -667,9 +674,9 @@
     block_own = (block(block_input, line.me).astype(f32) + out_own).astype(bf16)
     pieces = line.all_pieces(block_own)
     block_output = jnp.zeros((length, width), bf16)
-    for m in range(ranks):
+    for m, first, piece in pieces:
         block_output = lax.dynamic_update_slice_in_dim(
-            block_output, pieces[m], line.source(m) * quarter, 0
+            block_output, piece, line.source(m) * quarter + first, 0
         )
 
     x_own, inv_own = block(block_input, line.me).astype(f32), block(inverse, line.me)
@@ -679,7 +686,7 @@
     )
     delta = lax.optimization_barrier(delta.astype(bf16))
     grad_norm_gain = jnp.sum(gn * x_own * inv_own, axis=0)
-    pieces = line.all_pieces(delta)
+    pieces = line.all_pieces(delta, 2)
     back_pieces = pieces
 
     summed_bc = ring.reduce_rows(dot_tn(normed, gbc))
@@ -698,8 +705,8 @@
     wide_lanes = packed.shape[1]
     spare = (-width) % wide_lanes
     gain_rows = jnp.pad(grad_norm_gain, (0, spare)).reshape(-1, wide_lanes)
-    packed = ring.total(jnp.concatenate([packed, gain_rows], axis=0))
-    packed = range_ring.total(packed)
+    packed = range_ring.total(jnp.concatenate([packed, gain_rows], axis=0))
+    packed = ring.total(packed)
     gain_rows = packed[8:]
     parts = [gain_rows] + [line.send(gain_rows, m) for m in range(1, ranks)]
     ordered = jnp.zeros((ranks,) + gain_rows.shape, f32)
@@ -707,13 +714,11 @@
         ordered = lax.dynamic_update_slice_in_dim(ordered, parts[m][None], line.source(m), 0)
     sum_norm_gain = jnp.sum(ordered, axis=0).reshape(-1)[:width]
     input_grad = jnp.zeros((length, width), f32)
-    for m in range(ranks):
-        rank = line.source(m)
+    for m, first, piece in back_pieces:
+        first = line.source(m) * quarter + first
+        kept = lax.dynamic_slice_in_dim(out_cotangent, first, piece.shape[0])
         input_grad = lax.dynamic_update_slice_in_dim(
-            input_grad,
-            block(out_cotangent, rank).astype(f32) + back_pieces[m].astype(f32),
-            rank * quarter,
-            0,
+            input_grad, kept.astype(f32) + piece.astype(f32), first, 0
         )
     return (
         block_output,

time: 556 us -> 541 us (0.973)
  waiting for transfers between devices: 211 us -> 189 us
  starting transfers between devices: 93.1 us -> 106 us
    ppermute x15 -> x12, waiting for transfers between devices: 95.6 us -> 80.1 us  [the longest x3 32 us: all_pieces(): second = lax.ppermute(cross, self.axis, [(1, 0), (2, 3)])]
    ppermute x48 -> x54, starting transfers between devices: 53 us -> 68.3 us  [send(): return lax.ppermute(value, self.axis, pairs)]
    ppermute x48 -> x54, waiting for transfers between devices: 114 us -> 105 us  [send(): return lax.ppermute(value, self.axis, pairs)]
    ppermute x15 -> x12, starting transfers between devices: 25.6 us -> 22.7 us  [the longest x3 11.4 us: all_pieces(): cross = lax.ppermute(cut, self.axis, [(0, 2), (3, 1)])]
    dynamic_update_slice x7 -> x10, other arithmetic: 13.6 us -> 14.6 us  [the longest x8 9.98 us: body(): lax.dynamic_update_slice_in_dim(input_grad, kept.astype(f32) + piece.asty...]
    unnamed x144 -> x146, local copies, waits for them, and re-layouts: 15.4 us -> 14.5 us
  transfers between devices with their start and end apart: 70 -> 73, of which waited for: 25 -> 23; matrix products, arithmetic and copies ran while one was open for 30% -> 30% of each run, Pallas kernels for 9% -> 12%
where the time goes in v6:
time: 541 us; the launch traced here: 531 us
  waiting for transfers between devices  189 us (35%)
  starting transfers between devices  106 us (20%)
  Pallas kernels  62.8 us (12%)
  other arithmetic  62.5 us (12%)
  local copies, waits for them, and re-layouts  57 us (11%)
  matrix products  51.3 us (9%)
    ppermute x54, waiting for transfers between devices, send(): return lax.ppermute(value, self.axis, pairs)  105 us
    ppermute x54, starting transfers between devices, send(): return lax.ppermute(value, self.axis, pairs)  68.3 us
    ppermute x3, waiting for transfers between devices, all_pieces(): second = lax.ppermute(cross, self.axis, [(1, 0), (2, 3)])  32 us
    ppermute x3, waiting for transfers between devices, all_pieces(): cross = lax.ppermute(cut, self.axis, [(0, 2), (3, 1)])  31.4 us
    pallas_call x1, Pallas kernels, body(): pl.pallas_call(backward_kernel, grid=(count,), in_specs=[back(inner), bac...  26.9 us
    dot_general x11, matrix products, dot_t(): lax.dot_general(a, b, (((1,), (1,)), ((), ())), preferred_element_type=f32)  23 us
    ppermute x3, waiting for transfers between devices, all_pieces(): first = lax.ppermute(middle, self.axis, [(1, 0), (2, 3)])  16.7 us
    unnamed x146, local copies, waits for them, and re-layouts  14.5 us
  transfers between devices with their start and end apart: 73, of which 23 were waited for; matrix products, arithmetic and copies ran while one was open for 30% of the time, Pallas kernels for 12%

profile of v6, /device:TPU:0, one launch (start us, length us, event | category | flops | bytes accessed | tf_op | source)
XLA Modules:
  0.0 530.9 jit_solution(5464706405810177168)
XLA Ops:
  32.9 7.8 %collective-permute-done.5 = bf16[384,768]{1,0:T(8,128)(2,1)} collective-permute-done((bf16[384,768]{1,0:T(8,128)(2,1)}, bf16[384,768]{1,0:T(8,128)(2,1)}, u32[]{:S(2)}, u32[]{:S(2)}) %collective-permute-start.5) | collective-permute-done | bytes 589856 | tf_op jit(solution)/shard_map/ppermute | solution.py:357
  40.7 11.8 %collective-permute-done.4 = bf16[384,768]{1,0:T(8,128)(2,1)} collective-permute-done((bf16[384,768]{1,0:T(8,128)(2,1)}, bf16[384,768]{1,0:T(8,128)(2,1)}, u32[]{:S(2)}, u32[]{:S(2)}) %collective-permute-start.4) | collective-permute-done | bytes 589856 | tf_op jit(solution)/shard_map/ppermute | solution.py:357
  63.9 4.3 fusion.104.z_ref
  68.4 4.3 fusion.112
  80.6 11.4 %front.1 = (f32[1024,1024]{1,0:T(8,128)}, f32[1024,1024]{1,0:T(8,128)}, f32[1024,128]{1,0:T(8,128)}, f32[128,768]{1,0:T(8,128)}, f32[8,128]{1,0:T(8,128)}) custom-call(bf16[1024,768]{1,0:T(8,128)(2,1)} %slice.211.x_ref.x_raw_ref, bf16[1024,256]{1,0:T(8,128)(2,1)} %get-tuple-element.151.bc_ref, f32[8,1024]{1,0:T(8,128)} %pad.35.edge_ref, ...), custom_call_target="tpu_custom_call" | custom-call | tf_op jit(solution)/shard_map/front/pallas_call | solution.py:523
  92.0 4.1 collective-permute-start.10
  96.1 6.8 %convolution_bitcast_fusion.1.ggo_ref = f32[1024,768]{1,0:T(8,128)} fusion(bf16[1024,1536]{1,0:T(8,128)(2,1)} %param.31, bf16[1536,768]{1,0:T(8,128)(2,1)} %copy-done.6), kind=kOutput, calls=%fused_computation.31 | convolution fusion | flops 2415919104 | bytes 8650752 | tf_op jit(solution)/shard_map/dot_general | solution.py:545
  104.1 13.4 %forward.1 = (f32[1024,768]{1,0:T(8,128)}, f32[1024,768]{1,0:T(8,128)}, f32[1024,768]{1,0:T(8,128)}, f32[8,1024]{1,0:T(8,128)}) custom-call(f32[1024,1024]{1,0:T(8,128)} %get-tuple-element.50.act_ref, f32[1024,128]{1,0:T(8,128)} %compare_select_fusion.step_ref, f32[1024,128]{1,0:T(8,128)} %get-tuple-element.51.cum_ref, f32[1024,768]{1,0:T(8,128)} %fusion.104.z_ref, ...), custom_call_target="tpu_custom_call" | custom-call | tf_op jit(solution)/shard_map/forward/pallas_call | solution.py:546
  130.5 11.0 %gate.1 = (bf16[1024,768]{1,0:T(8,128)(2,1)}, f32[1024,768]{1,0:T(8,128)}, bf16[1024,768]{1,0:T(8,128)(2,1)}, f32[128,768]{1,0:T(8,128)}, f32[8,768]{1,0:T(8,128)}) custom-call(f32[1024,768]{1,0:T(8,128)} %get-tuple-element.58.mixer_ref, f32[1024,768]{1,0:T(8,128)} %fusion.104.z_ref, f32[1024,768]{1,0:T(8,128)} %convolution_bitcast_fusion.1.ggo_ref, ...), custom_call_target="tpu_custom_call" | custom-call | tf_op jit(solution)/shard_map/gate/pallas_call | solution.py:569
  142.9 5.0 convolution_bitcast_fusion
  153.2 26.9 %backward.1 = (bf16[1024,768]{1,0:T(8,128)(2,1)}, f32[8,768]{1,0:T(8,128)}, f32[8,768]{1,0:T(8,128)}, f32[1024,256]{1,0:T(8,128)}, f32[1024,128]{1,0:T(8,128)}, /*index=5*/f32[8,768]{1,0:T(8,128)}, f32[8,128]{1,0:T(8,128)}) custom-call(f32[1024,768]{1,0:T(8,128)} %get-tuple-element.61.gm_ref, f32[1024,1024]{1,0:T(8,128)} %get-tuple-element.50.act_ref, ...), custom_call_target="tpu_custom_call" | custom-call | tf_op jit(solution)/shard_map/backward/pallas_call | solution.py:592
  216.2 5.1 collective-permute-done.37
  223.8 9.0 %collective-permute-done.38 = f32[256,256]{1,0:T(8,128)S(1)} collective-permute-done((f32[256,256]{1,0:T(8,128)S(1)}, f32[256,256]{1,0:T(8,128)S(1)}, u32[]{:S(2)}, u32[]{:S(2)}) %collective-permute-start.38) | collective-permute-done | bytes 262176 | tf_op jit(solution)/shard_map/ppermute | solution.py:357
  247.8 3.7 constant_dynamic-slice_fusion.2
  260.4 5.7 %collective-permute-start.31 = (bf16[256,1536]{1,0:T(8,128)(2,1)S(1)}, bf16[256,1536]{1,0:T(8,128)(2,1)S(1)}, u32[]{:S(2)}, u32[]{:S(2)}) collective-permute-start(bf16[256,1536]{1,0:T(8,128)(2,1)S(1)} %copy-done.27), channel_id=1, source_target_pairs={{0,1},{1,0},{2,3},{3,2},{4,5},{5,4},{6,7},{7,6},{8,9},{9,8},{10,11... | collective-permute-start | bytes 2359304 | tf_op jit(solution)/shard_map/ppermute | solution.py:357
  270.1 4.3 collective-permute-done.62
  275.0 13.7 %collective-permute-done.31 = bf16[256,1536]{1,0:T(8,128)(2,1)S(1)} collective-permute-done((bf16[256,1536]{1,0:T(8,128)(2,1)S(1)}, bf16[256,1536]{1,0:T(8,128)(2,1)S(1)}, u32[]{:S(2)}, u32[]{:S(2)}) %collective-permute-start.31) | collective-permute-done | bytes 786464 | tf_op jit(solution)/shard_map/ppermute | solution.py:357
  290.2 25.2 %collective-permute-done.33 = bf16[256,1536]{1,0:T(8,128)(2,1)S(1)} collective-permute-done((bf16[256,1536]{1,0:T(8,128)(2,1)S(1)}, bf16[256,1536]{1,0:T(8,128)(2,1)S(1)}, u32[]{:S(2)}, u32[]{:S(2)}) %collective-permute-start.33) | collective-permute-done | bytes 786464 | tf_op jit(solution)/shard_map/ppermute | solution.py:357
  345.3 4.0 collective-permute-done.72
  354.7 4.8 collective-permute-done.41
  366.9 7.0 %collective-permute-start.17 = (bf16[256,768]{1,0:T(8,128)(2,1)S(1)}, bf16[256,768]{1,0:T(8,128)(2,1)S(1)}, u32[]{:S(2)}, u32[]{:S(2)}) collective-permute-start(bf16[256,768]{1,0:T(8,128)(2,1)S(1)} %copy-done.33), channel_id=1, source_target_pairs={{0,1},{1,0},{2,3},{3,2},{4,5},{5,4},{6,7},{7,6},{8,9},{9,8},{10,11... | collective-permute-start | bytes 1179656 | tf_op jit(solution)/shard_map/ppermute | solution.py:357
  374.0 7.9 %collective-permute-done.44 = bf16[128,1536]{1,0:T(8,128)(2,1)S(1)} collective-permute-done((bf16[128,1536]{1,0:T(8,128)(2,1)S(1)}, bf16[128,1536]{1,0:T(8,128)(2,1)S(1)}, u32[]{:S(2)}, u32[]{:S(2)}) %collective-permute-start.44) | collective-permute-done | bytes 393248 | tf_op jit(solution)/shard_map/ppermute | solution.py:426
  386.5 17.3 %collective-permute-done.45 = bf16[128,1536]{1,0:T(8,128)(2,1)S(1)} collective-permute-done((bf16[128,1536]{1,0:T(8,128)(2,1)S(1)}, bf16[128,1536]{1,0:T(8,128)(2,1)S(1)}, u32[]{:S(2)}, u32[]{:S(2)}) %collective-permute-start.45) | collective-permute-done | bytes 393248 | tf_op jit(solution)/shard_map/ppermute | solution.py:427
  405.6 4.1 collective-permute-start.47
  412.2 5.4 %collective-permute-done.47 = bf16[128,1536]{1,0:T(8,128)(2,1)S(1)} collective-permute-done((bf16[128,1536]{1,0:T(8,128)(2,1)}, bf16[128,1536]{1,0:T(8,128)(2,1)S(1)}, u32[]{:S(2)}, u32[]{:S(2)}) %collective-permute-start.47) | collective-permute-done | bytes 393248 | tf_op jit(solution)/shard_map/ppermute | solution.py:422
  417.6 9.1 %collective-permute-start.18 = (bf16[256,768]{1,0:T(8,128)(2,1)S(1)}, bf16[256,768]{1,0:T(8,128)(2,1)S(1)}, u32[]{:S(2)}, u32[]{:S(2)}) collective-permute-start(bf16[256,768]{1,0:T(8,128)(2,1)S(1)} %copy-done.32), channel_id=1, source_target_pairs={{0,2},{1,3},{2,0},{3,1},{4,6},{5,7},{6,4},{7,5},{8,10},{9,11},{10,... | collective-permute-start | bytes 1179656 | tf_op jit(solution)/shard_map/ppermute | solution.py:357
  426.7 8.7 %collective-permute-done.49 = bf16[128,1536]{1,0:T(8,128)(2,1)S(1)} collective-permute-done((bf16[128,1536]{1,0:T(8,128)(2,1)S(1)}, bf16[128,1536]{1,0:T(8,128)(2,1)S(1)}, u32[]{:S(2)}, u32[]{:S(2)}) %collective-permute-start.49) | collective-permute-done | bytes 393248 | tf_op jit(solution)/shard_map/ppermute | solution.py:426
  443.2 10.4 %collective-permute-done.18 = bf16[256,768]{1,0:T(8,128)(2,1)S(1)} collective-permute-done((bf16[256,768]{1,0:T(8,128)(2,1)S(1)}, bf16[256,768]{1,0:T(8,128)(2,1)S(1)}, u32[]{:S(2)}, u32[]{:S(2)}) %collective-permute-start.18) | collective-permute-done | bytes 393248 | tf_op jit(solution)/shard_map/ppermute | solution.py:357
  464.8 4.8 collective-permute-done.57
  474.2 5.1 collective-permute-start.26
  483.4 23.0 %collective-permute-done.26 = bf16[256,1536]{1,0:T(8,128)(2,1)} collective-permute-done((bf16[256,1536]{1,0:T(8,128)(2,1)}, bf16[256,1536]{1,0:T(8,128)(2,1)}, u32[]{:S(2)}, u32[]{:S(2)}) %collective-permute-start.26) | collective-permute-done | bytes 786464 | tf_op jit(solution)/shard_map/ppermute | solution.py:422
  513.8 14.7 %collective-permute-done.29 = bf16[256,1536]{1,0:T(8,128)(2,1)S(1)} collective-permute-done((bf16[256,1536]{1,0:T(8,128)(2,1)}, bf16[256,1536]{1,0:T(8,128)(2,1)S(1)}, u32[]{:S(2)}, u32[]{:S(2)}) %collective-permute-start.29) | collective-permute-done | bytes 786464 | tf_op jit(solution)/shard_map/ppermute | solution.py:427
  (420 shorter events, 228.8 us)
Async XLA Ops:
  4.3 51.6 %collective-permute-start = (bf16[384,1152]{1,0:T(8,128)(2,1)}, bf16[384,1152]{1,0:T(8,128)(2,1)}, u32[]{:S(2)}, u32[]{:S(2)}) collective-permute-start(bf16[384,1152]{1,0:T(8,128)(2,1)} %get-tuple-element.160), channel_id=1, source_target_pairs={{0,16},{8,24},{16,0},{24,8},{1,17},{9,25},{17,1},{25,9},{2,18},{10... | collective-permute-start | bytes 2654216 | tf_op jit(solution)/shard_map/ppermute | solution.py:357
  7.3 50.0 %collective-permute-start.1 = (bf16[384,1152]{1,0:T(8,128)(2,1)}, bf16[384,1152]{1,0:T(8,128)(2,1)}, u32[]{:S(2)}, u32[]{:S(2)}) collective-permute-start(bf16[384,1152]{1,0:T(8,128)(2,1)} %get-tuple-element.160), channel_id=1, source_target_pairs={{0,8},{8,0},{16,24},{24,16},{1,9},{9,1},{17,25},{25,17},{2,10},{10... | collective-permute-start | bytes 2654216 | tf_op jit(solution)/shard_map/ppermute | solution.py:357
  9.4 31.3 %collective-permute-start.5 = (bf16[384,768]{1,0:T(8,128)(2,1)}, bf16[384,768]{1,0:T(8,128)(2,1)}, u32[]{:S(2)}, u32[]{:S(2)}) collective-permute-start(bf16[384,768]{1,0:T(8,128)(2,1)} %bitcast.2), channel_id=1, source_target_pairs={{0,16},{8,24},{16,0},{24,8},{1,17},{9,25},{17,1},{25,9},{2,18},{10... | collective-permute-start | bytes 1769480 | tf_op jit(solution)/shard_map/ppermute | solution.py:357
  9.4 111.1 %collective-permute-start.11 = (bf16[384,768]{1,0:T(8,128)(2,1)}, bf16[384,768]{1,0:T(8,128)(2,1)}, u32[]{:S(2)}, u32[]{:S(2)}) collective-permute-start(bf16[384,768]{1,0:T(8,128)(2,1)} %bitcast.2), channel_id=1, source_target_pairs={{0,1},{1,0},{2,3},{3,2},{4,5},{5,4},{6,7},{7,6},{8,9},{9,8},{10,11... | collective-permute-start | bytes 1769480 | tf_op jit(solution)/shard_map/ppermute | solution.py:357
  11.5 41.0 %collective-permute-start.4 = (bf16[384,768]{1,0:T(8,128)(2,1)}, bf16[384,768]{1,0:T(8,128)(2,1)}, u32[]{:S(2)}, u32[]{:S(2)}) collective-permute-start(bf16[384,768]{1,0:T(8,128)(2,1)} %param.18), channel_id=1, source_target_pairs={{0,16},{8,24},{16,0},{24,8},{1,17},{9,25},{17,1},{25,9},{2,18},{10... | collective-permute-start | bytes 1769480 | tf_op jit(solution)/shard_map/ppermute | solution.py:357
  59.2 63.3 %collective-permute-start.12 = (bf16[384,768]{1,0:T(8,128)(2,1)}, bf16[384,768]{1,0:T(8,128)(2,1)}, u32[]{:S(2)}, u32[]{:S(2)}) collective-permute-start(bf16[384,768]{1,0:T(8,128)(2,1)} %bitcast.2), channel_id=1, source_target_pairs={{0,2},{1,3},{2,0},{3,1},{4,6},{5,7},{6,4},{7,5},{8,10},{9,11},{10,... | collective-permute-start | bytes 1769480 | tf_op jit(solution)/shard_map/ppermute | solution.py:357
  62.1 60.4 %collective-permute-start.13 = (bf16[384,768]{1,0:T(8,128)(2,1)}, bf16[384,768]{1,0:T(8,128)(2,1)}, u32[]{:S(2)}, u32[]{:S(2)}) collective-permute-start(bf16[384,768]{1,0:T(8,128)(2,1)} %bitcast.2), channel_id=1, source_target_pairs={{0,3},{1,2},{2,1},{3,0},{4,7},{5,6},{6,5},{7,4},{8,11},{9,10},{10,... | collective-permute-start | bytes 1769480 | tf_op jit(solution)/shard_map/ppermute | solution.py:357
  128.4 235.6 %collective-permute-start.23 = (bf16[384,2304]{1,0:T(8,128)(2,1)}, bf16[384,2304]{1,0:T(8,128)(2,1)}, u32[]{:S(2)}, u32[]{:S(2)}) collective-permute-start(bf16[384,2304]{1,0:T(8,128)(2,1)} %constant_dynamic-update-slice_fusion.27), channel_id=1, source_target_pairs={{0,16},{8,24},{16,0},{24,8},{1,17},{9,25},{17,1},{25,9},{2,18},{10... | collective-permute-start | bytes 5308424 | tf_op jit(solution)/shard_map/ppermute | solution.py:357
  150.5 96.7 %collective-permute-start.64 = (f32[384,768]{1,0:T(8,128)}, f32[384,768]{1,0:T(8,128)}, u32[]{:S(2)}, u32[]{:S(2)}) collective-permute-start(f32[384,768]{1,0:T(8,128)} %constant_dynamic-slice_fusion.1), channel_id=1, source_target_pairs={{0,8},{8,0},{16,24},{24,16},{1,9},{9,1},{17,25},{25,17},{2,10},{10... | collective-permute-start | bytes 3538952 | tf_op jit(solution)/shard_map/ppermute | solution.py:357
  184.6 24.5 %collective-permute-start.34 = (f32[256,256]{1,0:T(8,128)S(1)}, f32[256,256]{1,0:T(8,128)S(1)}, u32[]{:S(2)}, u32[]{:S(2)}) collective-permute-start(f32[256,256]{1,0:T(8,128)S(1)} %get-tuple-element.157), channel_id=1, source_target_pairs={{0,1},{1,0},{2,3},{3,2},{4,5},{5,4},{6,7},{7,6},{8,9},{9,8},{10,11... | collective-permute-start | bytes 786440 | tf_op jit(solution)/shard_map/ppermute | solution.py:357
  184.8 24.3 %collective-permute-start.35 = (f32[256,256]{1,0:T(8,128)S(1)}, f32[256,256]{1,0:T(8,128)S(1)}, u32[]{:S(2)}, u32[]{:S(2)}) collective-permute-start(f32[256,256]{1,0:T(8,128)S(1)} %get-tuple-element.159), channel_id=1, source_target_pairs={{0,2},{1,3},{2,0},{3,1},{4,6},{5,7},{6,4},{7,5},{8,10},{9,11},{10,... | collective-permute-start | bytes 786440 | tf_op jit(solution)/shard_map/ppermute | solution.py:357
  221.2 31.6 %collective-permute-start.32 = (bf16[256,1536]{1,0:T(8,128)(2,1)}, bf16[256,1536]{1,0:T(8,128)(2,1)}, u32[]{:S(2)}, u32[]{:S(2)}) collective-permute-start(bf16[256,1536]{1,0:T(8,128)(2,1)} %fusion.10), channel_id=1, source_target_pairs={{0,1},{3,2},{4,5},{7,6},{8,9},{11,10},{12,13},{15,14},{16,17},{19,... | collective-permute-start | bytes 2359304 | tf_op jit(solution)/shard_map/ppermute | solution.py:403
  255.8 34.4 %collective-permute-start.30 = (bf16[256,1536]{1,0:T(8,128)(2,1)}, bf16[256,1536]{1,0:T(8,128)(2,1)S(1)}, u32[]{:S(2)}, u32[]{:S(2)}) collective-permute-start(bf16[256,1536]{1,0:T(8,128)(2,1)} %fusion.10), channel_id=1, source_target_pairs={{1,2},{2,1},{5,6},{6,5},{9,10},{10,9},{13,14},{14,13},{17,18},{18,... | collective-permute-start | bytes 2359304 | tf_op jit(solution)/shard_map/ppermute | solution.py:404
  260.4 28.3 %collective-permute-start.31 = (bf16[256,1536]{1,0:T(8,128)(2,1)S(1)}, bf16[256,1536]{1,0:T(8,128)(2,1)S(1)}, u32[]{:S(2)}, u32[]{:S(2)}) collective-permute-start(bf16[256,1536]{1,0:T(8,128)(2,1)S(1)} %copy-done.27), channel_id=1, source_target_pairs={{0,1},{1,0},{2,3},{3,2},{4,5},{5,4},{6,7},{7,6},{8,9},{9,8},{10,11... | collective-permute-start | bytes 2359304 | tf_op jit(solution)/shard_map/ppermute | solution.py:357
  266.1 49.3 %collective-permute-start.33 = (bf16[256,1536]{1,0:T(8,128)(2,1)S(1)}, bf16[256,1536]{1,0:T(8,128)(2,1)S(1)}, u32[]{:S(2)}, u32[]{:S(2)}) collective-permute-start(bf16[256,1536]{1,0:T(8,128)(2,1)S(1)} %fusion.9), channel_id=1, source_target_pairs={{0,2},{1,3},{2,0},{3,1},{4,6},{5,7},{6,4},{7,5},{8,10},{9,11},{10,... | collective-permute-start | bytes 2359304 | tf_op jit(solution)/shard_map/ppermute | solution.py:357
  274.3 77.1 %collective-permute-start.63 = (f32[384,768]{1,0:T(8,128)}, f32[384,768]{1,0:T(8,128)}, u32[]{:S(2)}, u32[]{:S(2)}) collective-permute-start(f32[384,768]{1,0:T(8,128)} %get-tuple-element.146), channel_id=1, source_target_pairs={{0,8},{8,0},{16,24},{24,16},{1,9},{9,1},{17,25},{25,17},{2,10},{10... | collective-permute-start | bytes 3538952 | tf_op jit(solution)/shard_map/ppermute | solution.py:357
  288.7 62.9 %collective-permute-start.65 = (f32[384,768]{1,0:T(8,128)}, f32[384,768]{1,0:T(8,128)}, u32[]{:S(2)}, u32[]{:S(2)}) collective-permute-start(f32[384,768]{1,0:T(8,128)} %get-tuple-element.147), channel_id=1, source_target_pairs={{0,16},{8,24},{16,0},{24,8},{1,17},{9,25},{17,1},{25,9},{2,18},{10... | collective-permute-start | bytes 3538952 | tf_op jit(solution)/shard_map/ppermute | solution.py:357
  290.2 92.7 %collective-permute-start.51 = (f32[384,768]{1,0:T(8,128)}, f32[384,768]{1,0:T(8,128)}, u32[]{:S(2)}, u32[]{:S(2)}) collective-permute-start(f32[384,768]{1,0:T(8,128)} %get-tuple-element.148), channel_id=1, source_target_pairs={{0,8},{8,0},{16,24},{24,16},{1,9},{9,1},{17,25},{25,17},{2,10},{10... | collective-permute-start | bytes 3538952 | tf_op jit(solution)/shard_map/ppermute | solution.py:357
  349.3 33.7 %collective-permute-start.53 = (f32[384,768]{1,0:T(8,128)}, f32[384,768]{1,0:T(8,128)}, u32[]{:S(2)}, u32[]{:S(2)}) collective-permute-start(f32[384,768]{1,0:T(8,128)} %get-tuple-element.149), channel_id=1, source_target_pairs={{0,16},{8,24},{16,0},{24,8},{1,17},{9,25},{17,1},{25,9},{2,18},{10... | collective-permute-start | bytes 3538952 | tf_op jit(solution)/shard_map/ppermute | solution.py:357
  364.0 73.0 %collective-permute-start.22 = (bf16[384,2304]{1,0:T(8,128)(2,1)}, bf16[384,2304]{1,0:T(8,128)(2,1)S(1)}, u32[]{:S(2)}, u32[]{:S(2)}) collective-permute-start(bf16[384,2304]{1,0:T(8,128)(2,1)} %constant_dynamic-update-slice_fusion.27), channel_id=1, source_target_pairs={{0,8},{8,0},{16,24},{24,16},{1,9},{9,1},{17,25},{25,17},{2,10},{10... | collective-permute-start | bytes 5308424 | tf_op jit(solution)/shard_map/ppermute | solution.py:357
  366.9 74.8 %collective-permute-start.17 = (bf16[256,768]{1,0:T(8,128)(2,1)S(1)}, bf16[256,768]{1,0:T(8,128)(2,1)S(1)}, u32[]{:S(2)}, u32[]{:S(2)}) collective-permute-start(bf16[256,768]{1,0:T(8,128)(2,1)S(1)} %copy-done.33), channel_id=1, source_target_pairs={{0,1},{1,0},{2,3},{3,2},{4,5},{5,4},{6,7},{7,6},{8,9},{9,8},{10,11... | collective-permute-start | bytes 1179656 | tf_op jit(solution)/shard_map/ppermute | solution.py:357
  381.9 55.1 %collective-permute-start.24 = (bf16[384,2304]{1,0:T(8,128)(2,1)}, bf16[384,2304]{1,0:T(8,128)(2,1)S(1)}, u32[]{:S(2)}, u32[]{:S(2)}) collective-permute-start(bf16[384,2304]{1,0:T(8,128)(2,1)} %collective-permute-done.23), channel_id=1, source_target_pairs={{0,8},{8,0},{16,24},{24,16},{1,9},{9,1},{17,25},{25,17},{2,10},{10... | collective-permute-start | bytes 5308424 | tf_op jit(solution)/shard_map/ppermute | solution.py:357
  409.7 25.7 %collective-permute-start.49 = (bf16[128,1536]{1,0:T(8,128)(2,1)S(1)}, bf16[128,1536]{1,0:T(8,128)(2,1)S(1)}, u32[]{:S(2)}, u32[]{:S(2)}) collective-permute-start(bf16[128,1536]{1,0:T(8,128)(2,1)S(1)} %collective-permute-done.48), channel_id=1, source_target_pairs={{1,0},{2,3},{5,4},{6,7},{9,8},{10,11},{13,12},{14,15},{17,16},{18,... | collective-permute-start | bytes 1179656 | tf_op jit(solution)/shard_map/ppermute | solution.py:426
  417.6 35.9 %collective-permute-start.18 = (bf16[256,768]{1,0:T(8,128)(2,1)S(1)}, bf16[256,768]{1,0:T(8,128)(2,1)S(1)}, u32[]{:S(2)}, u32[]{:S(2)}) collective-permute-start(bf16[256,768]{1,0:T(8,128)(2,1)S(1)} %copy-done.32), channel_id=1, source_target_pairs={{0,2},{1,3},{2,0},{3,1},{4,6},{5,7},{6,4},{7,5},{8,10},{9,11},{10,... | collective-permute-start | bytes 1179656 | tf_op jit(solution)/shard_map/ppermute | solution.py:357
  437.0 25.9 %collective-permute-start.55 = (f32[384,896]{1,0:T(8,128)S(1)}, f32[384,896]{1,0:T(8,128)S(1)}, u32[]{:S(2)}, u32[]{:S(2)}) collective-permute-start(f32[384,896]{1,0:T(8,128)S(1)} %copy-done.25), channel_id=1, source_target_pairs={{0,8},{8,0},{16,24},{24,16},{1,9},{9,1},{17,25},{25,17},{2,10},{10... | collective-permute-start | bytes 4128776 | tf_op jit(solution)/shard_map/ppermute | solution.py:357
  437.0 32.6 %collective-permute-start.57 = (f32[384,896]{1,0:T(8,128)S(1)}, f32[384,896]{1,0:T(8,128)S(1)}, u32[]{:S(2)}, u32[]{:S(2)}) collective-permute-start(f32[384,896]{1,0:T(8,128)S(1)} %copy-done.24), channel_id=1, source_target_pairs={{0,16},{8,24},{16,0},{24,8},{1,17},{9,25},{17,1},{25,9},{2,18},{10... | collective-permute-start | bytes 4128776 | tf_op jit(solution)/shard_map/ppermute | solution.py:357
  441.8 32.4 %collective-permute-start.66 = (f32[192,768]{1,0:T(8,128)S(1)}, f32[192,768]{1,0:T(8,128)S(1)}, u32[]{:S(2)}, u32[]{:S(2)}) collective-permute-start(f32[192,768]{1,0:T(8,128)S(1)} %constant_dynamic-slice_fusion), channel_id=1, source_target_pairs={{0,4},{4,0},{1,5},{5,1},{2,6},{6,2},{3,7},{7,3},{8,12},{12,8},{9,1... | collective-permute-start | bytes 1769480 | tf_op jit(solution)/shard_map/ppermute | solution.py:357
  454.8 27.6 %collective-permute-start.54 = (f32[192,768]{1,0:T(8,128)S(1)}, f32[192,768]{1,0:T(8,128)S(1)}, u32[]{:S(2)}, u32[]{:S(2)}) collective-permute-start(f32[192,768]{1,0:T(8,128)S(1)} %constant_dynamic-slice_fusion.9), channel_id=1, source_target_pairs={{0,4},{4,0},{1,5},{5,1},{2,6},{6,2},{3,7},{7,3},{8,12},{12,8},{9,1... | collective-permute-start | bytes 1769480 | tf_op jit(solution)/shard_map/ppermute | solution.py:357
  471.2 36.5 %collective-permute-start.58 = (f32[192,896]{1,0:T(8,128)S(1)}, f32[192,896]{1,0:T(8,128)S(1)}, u32[]{:S(2)}, u32[]{:S(2)}) collective-permute-start(f32[192,896]{1,0:T(8,128)S(1)} %constant_dynamic-slice_fusion.6), channel_id=1, source_target_pairs={{0,4},{4,0},{1,5},{5,1},{2,6},{6,2},{3,7},{7,3},{8,12},{12,8},{9,1... | collective-permute-start | bytes 2064392 | tf_op jit(solution)/shard_map/ppermute | solution.py:357
  472.6 36.7 %collective-permute-start.25 = (bf16[256,1536]{1,0:T(8,128)(2,1)}, bf16[256,1536]{1,0:T(8,128)(2,1)}, u32[]{:S(2)}, u32[]{:S(2)}) collective-permute-start(bf16[256,1536]{1,0:T(8,128)(2,1)} %get-tuple-element.173), channel_id=1, source_target_pairs={{0,1},{1,0},{2,3},{3,2},{4,5},{5,4},{6,7},{7,6},{8,9},{9,8},{10,11... | collective-permute-start | bytes 2359304 | tf_op jit(solution)/shard_map/ppermute | solution.py:357
  474.2 32.2 %collective-permute-start.26 = (bf16[256,1536]{1,0:T(8,128)(2,1)}, bf16[256,1536]{1,0:T(8,128)(2,1)}, u32[]{:S(2)}, u32[]{:S(2)}) collective-permute-start(bf16[256,1536]{1,0:T(8,128)(2,1)} %get-tuple-element.173), channel_id=1, source_target_pairs={{0,2},{3,1},{4,6},{7,5},{8,10},{11,9},{12,14},{15,13},{16,18},{19,... | collective-permute-start | bytes 2359304 | tf_op jit(solution)/shard_map/ppermute | solution.py:422
  480.3 31.1 %collective-permute-start.28 = (bf16[256,1536]{1,0:T(8,128)(2,1)}, bf16[256,1536]{1,0:T(8,128)(2,1)}, u32[]{:S(2)}, u32[]{:S(2)}) collective-permute-start(bf16[256,1536]{1,0:T(8,128)(2,1)} %collective-permute-done.27), channel_id=1, source_target_pairs={{1,0},{2,3},{5,4},{6,7},{9,8},{10,11},{13,12},{14,15},{17,16},{18,... | collective-permute-start | bytes 2359304 | tf_op jit(solution)/shard_map/ppermute | solution.py:426
  (111 other events, 1314.5 us)

commit v7 on v6

--- a/solution.py
+++ b/solution.py
@@ -705,14 +705,13 @@
     wide_lanes = packed.shape[1]
     spare = (-width) % wide_lanes
     gain_rows = jnp.pad(grad_norm_gain, (0, spare)).reshape(-1, wide_lanes)
-    packed = range_ring.total(jnp.concatenate([packed, gain_rows], axis=0))
-    packed = ring.total(packed)
-    gain_rows = packed[8:]
     parts = [gain_rows] + [line.send(gain_rows, m) for m in range(1, ranks)]
     ordered = jnp.zeros((ranks,) + gain_rows.shape, f32)
     for m in range(ranks):
         ordered = lax.dynamic_update_slice_in_dim(ordered, parts[m][None], line.source(m), 0)
-    sum_norm_gain = jnp.sum(ordered, axis=0).reshape(-1)[:width]
+    packed = range_ring.total(jnp.concatenate([packed, jnp.sum(ordered, axis=0)], axis=0))
+    packed = ring.total(packed)
+    sum_norm_gain = packed[8:].reshape(-1)[:width]
     input_grad = jnp.zeros((length, width), f32)
     for m, first, piece in back_pieces:
         first = line.source(m) * quarter + first

time: 541 us -> 548 us (1.013)
  waiting for transfers between devices: 189 us -> 200 us
    ppermute x54, waiting for transfers between devices: 105 us -> 118 us  [send(): return lax.ppermute(value, self.axis, pairs)]
    unnamed x146 -> x151, local copies, waits for them, and re-layouts: 14.5 us -> 14.4 us
  transfers between devices with their start and end apart: 73 -> 73, of which waited for: 23 -> 21; matrix products, arithmetic and copies ran while one was open for 30% -> 30% of each run, Pallas kernels for 12% -> 12%
where the time goes in v7:
time: 548 us; the launch traced here: 538 us
  waiting for transfers between devices  200 us (36%)
  starting transfers between devices  102 us (19%)
  Pallas kernels  62.8 us (11%)
  other arithmetic  61.5 us (11%)
  local copies, waits for them, and re-layouts  57.5 us (10%)
  matrix products  51.5 us (9%)
    ppermute x54, waiting for transfers between devices, send(): return lax.ppermute(value, self.axis, pairs)  118 us
    ppermute x54, starting transfers between devices, send(): return lax.ppermute(value, self.axis, pairs)  65.5 us
    ppermute x3, waiting for transfers between devices, all_pieces(): cross = lax.ppermute(cut, self.axis, [(0, 2), (3, 1)])  32.9 us
    ppermute x3, waiting for transfers between devices, all_pieces(): second = lax.ppermute(cross, self.axis, [(1, 0), (2, 3)])  29.7 us
    pallas_call x1, Pallas kernels, body(): pl.pallas_call(backward_kernel, grid=(count,), in_specs=[back(inner), bac...  26.9 us
    dot_general x11, matrix products, dot_t(): lax.dot_general(a, b, (((1,), (1,)), ((), ())), preferred_element_type=f32)  23.1 us
    ppermute x3, waiting for transfers between devices, all_pieces(): first = lax.ppermute(middle, self.axis, [(1, 0), (2, 3)])  15.8 us
    unnamed x151, local copies, waits for them, and re-layouts  14.4 us
  transfers between devices with their start and end apart: 73, of which 21 were waited for; matrix products, arithmetic and copies ran while one was open for 30% of the time, Pallas kernels for 12%

profile of v7, /device:TPU:0, one launch (start us, length us, event | category | flops | bytes accessed | tf_op | source)
XLA Modules:
  0.0 538.1 jit_solution(13680889711544996346)
XLA Ops:
  33.0 7.8 %collective-permute-done.5 = bf16[384,768]{1,0:T(8,128)(2,1)} collective-permute-done((bf16[384,768]{1,0:T(8,128)(2,1)}, bf16[384,768]{1,0:T(8,128)(2,1)}, u32[]{:S(2)}, u32[]{:S(2)}) %collective-permute-start.5) | collective-permute-done | bytes 589856 | tf_op jit(solution)/shard_map/ppermute | solution.py:357
  40.7 11.8 %collective-permute-done.4 = bf16[384,768]{1,0:T(8,128)(2,1)} collective-permute-done((bf16[384,768]{1,0:T(8,128)(2,1)}, bf16[384,768]{1,0:T(8,128)(2,1)}, u32[]{:S(2)}, u32[]{:S(2)}) %collective-permute-start.4) | collective-permute-done | bytes 589856 | tf_op jit(solution)/shard_map/ppermute | solution.py:357
  63.9 4.3 fusion.104.z_ref
  68.4 4.3 fusion.112
  80.6 11.4 %front.1 = (f32[1024,1024]{1,0:T(8,128)}, f32[1024,1024]{1,0:T(8,128)}, f32[1024,128]{1,0:T(8,128)}, f32[128,768]{1,0:T(8,128)}, f32[8,128]{1,0:T(8,128)}) custom-call(bf16[1024,768]{1,0:T(8,128)(2,1)} %slice.211.x_ref.x_raw_ref, bf16[1024,256]{1,0:T(8,128)(2,1)} %get-tuple-element.167.bc_ref, f32[8,1024]{1,0:T(8,128)} %pad.35.edge_ref, ...), custom_call_target="tpu_custom_call" | custom-call | tf_op jit(solution)/shard_map/front/pallas_call | solution.py:523
  92.0 4.0 collective-permute-start.10
  96.1 7.0 %convolution_bitcast_fusion.1.ggo_ref = f32[1024,768]{1,0:T(8,128)} fusion(bf16[1024,1536]{1,0:T(8,128)(2,1)} %param.31, bf16[1536,768]{1,0:T(8,128)(2,1)} %copy-done.6), kind=kOutput, calls=%fused_computation.31 | convolution fusion | flops 2415919104 | bytes 8650752 | tf_op jit(solution)/shard_map/dot_general | solution.py:545
  104.2 13.5 %forward.1 = (f32[1024,768]{1,0:T(8,128)}, f32[1024,768]{1,0:T(8,128)}, f32[1024,768]{1,0:T(8,128)}, f32[8,1024]{1,0:T(8,128)}) custom-call(f32[1024,1024]{1,0:T(8,128)} %get-tuple-element.50.act_ref, f32[1024,128]{1,0:T(8,128)} %compare_select_fusion.step_ref, f32[1024,128]{1,0:T(8,128)} %get-tuple-element.51.cum_ref, f32[1024,768]{1,0:T(8,128)} %fusion.104.z_ref, ...), custom_call_target="tpu_custom_call" | custom-call | tf_op jit(solution)/shard_map/forward/pallas_call | solution.py:546
  130.8 11.0 %gate.1 = (bf16[1024,768]{1,0:T(8,128)(2,1)}, f32[1024,768]{1,0:T(8,128)}, bf16[1024,768]{1,0:T(8,128)(2,1)}, f32[128,768]{1,0:T(8,128)}, f32[8,768]{1,0:T(8,128)}) custom-call(f32[1024,768]{1,0:T(8,128)} %get-tuple-element.58.mixer_ref, f32[1024,768]{1,0:T(8,128)} %fusion.104.z_ref, f32[1024,768]{1,0:T(8,128)} %convolution_bitcast_fusion.1.ggo_ref, ...), custom_call_target="tpu_custom_call" | custom-call | tf_op jit(solution)/shard_map/gate/pallas_call | solution.py:569
  143.1 5.0 convolution_bitcast_fusion
  153.5 26.9 %backward.1 = (bf16[1024,768]{1,0:T(8,128)(2,1)}, f32[8,768]{1,0:T(8,128)}, f32[8,768]{1,0:T(8,128)}, f32[1024,256]{1,0:T(8,128)}, f32[1024,128]{1,0:T(8,128)}, /*index=5*/f32[8,768]{1,0:T(8,128)}, f32[8,128]{1,0:T(8,128)}) custom-call(f32[1024,768]{1,0:T(8,128)} %get-tuple-element.61.gm_ref, f32[1024,1024]{1,0:T(8,128)} %get-tuple-element.50.act_ref, ...), custom_call_target="tpu_custom_call" | custom-call | tf_op jit(solution)/shard_map/backward/pallas_call | solution.py:592
  216.4 5.1 collective-permute-done.37
  224.1 9.0 %collective-permute-done.38 = f32[256,256]{1,0:T(8,128)S(1)} collective-permute-done((f32[256,256]{1,0:T(8,128)S(1)}, f32[256,256]{1,0:T(8,128)S(1)}, u32[]{:S(2)}, u32[]{:S(2)}) %collective-permute-start.38) | collective-permute-done | bytes 262176 | tf_op jit(solution)/shard_map/ppermute | solution.py:357
  248.0 3.7 constant_dynamic-slice_fusion.2
  260.5 5.8 %collective-permute-start.31 = (bf16[256,1536]{1,0:T(8,128)(2,1)S(1)}, bf16[256,1536]{1,0:T(8,128)(2,1)S(1)}, u32[]{:S(2)}, u32[]{:S(2)}) collective-permute-start(bf16[256,1536]{1,0:T(8,128)(2,1)S(1)} %copy-done.28), channel_id=1, source_target_pairs={{0,1},{1,0},{2,3},{3,2},{4,5},{5,4},{6,7},{7,6},{8,9},{9,8},{10,11... | collective-permute-start | bytes 2359304 | tf_op jit(solution)/shard_map/ppermute | solution.py:357
  270.2 4.3 collective-permute-done.62
  275.3 13.5 %collective-permute-done.31 = bf16[256,1536]{1,0:T(8,128)(2,1)S(1)} collective-permute-done((bf16[256,1536]{1,0:T(8,128)(2,1)S(1)}, bf16[256,1536]{1,0:T(8,128)(2,1)S(1)}, u32[]{:S(2)}, u32[]{:S(2)}) %collective-permute-start.31) | collective-permute-done | bytes 786464 | tf_op jit(solution)/shard_map/ppermute | solution.py:357
  288.7 26.9 %collective-permute-done.33 = bf16[256,1536]{1,0:T(8,128)(2,1)S(1)} collective-permute-done((bf16[256,1536]{1,0:T(8,128)(2,1)S(1)}, bf16[256,1536]{1,0:T(8,128)(2,1)S(1)}, u32[]{:S(2)}, u32[]{:S(2)}) %collective-permute-start.33) | collective-permute-done | bytes 786464 | tf_op jit(solution)/shard_map/ppermute | solution.py:357
  342.6 13.0 %collective-permute-done.72 = f32[10,1024]{1,0:T(8,128)S(1)} collective-permute-done((f32[10,1024]{1,0:T(8,128)S(1)}, f32[10,1024]{1,0:T(8,128)S(1)}, u32[]{:S(2)}, u32[]{:S(2)}) %collective-permute-start.72) | collective-permute-done | bytes 40992 | tf_op jit(solution)/shard_map/ppermute | solution.py:357
  364.2 5.7 %collective-permute-done.41 = bf16[128,1536]{1,0:T(8,128)(2,1)S(1)} collective-permute-done((bf16[128,1536]{1,0:T(8,128)(2,1)}, bf16[128,1536]{1,0:T(8,128)(2,1)S(1)}, u32[]{:S(2)}, u32[]{:S(2)}) %collective-permute-start.41) | collective-permute-done | bytes 393248 | tf_op jit(solution)/shard_map/ppermute | solution.py:357
  374.7 3.7 collective-permute-done.42
  378.4 6.0 %collective-permute-start.17 = (bf16[256,768]{1,0:T(8,128)(2,1)S(1)}, bf16[256,768]{1,0:T(8,128)(2,1)S(1)}, u32[]{:S(2)}, u32[]{:S(2)}) collective-permute-start(bf16[256,768]{1,0:T(8,128)(2,1)S(1)} %copy-done.34), channel_id=1, source_target_pairs={{0,1},{1,0},{2,3},{3,2},{4,5},{5,4},{6,7},{7,6},{8,9},{9,8},{10,11... | collective-permute-start | bytes 1179656 | tf_op jit(solution)/shard_map/ppermute | solution.py:357
  384.3 7.9 %collective-permute-done.44 = bf16[128,1536]{1,0:T(8,128)(2,1)S(1)} collective-permute-done((bf16[128,1536]{1,0:T(8,128)(2,1)S(1)}, bf16[128,1536]{1,0:T(8,128)(2,1)S(1)}, u32[]{:S(2)}, u32[]{:S(2)}) %collective-permute-start.44) | collective-permute-done | bytes 393248 | tf_op jit(solution)/shard_map/ppermute | solution.py:426
  396.9 17.3 %collective-permute-done.45 = bf16[128,1536]{1,0:T(8,128)(2,1)S(1)} collective-permute-done((bf16[128,1536]{1,0:T(8,128)(2,1)S(1)}, bf16[128,1536]{1,0:T(8,128)(2,1)S(1)}, u32[]{:S(2)}, u32[]{:S(2)}) %collective-permute-start.45) | collective-permute-done | bytes 393248 | tf_op jit(solution)/shard_map/ppermute | solution.py:427
  415.9 4.1 collective-permute-start.47
  422.6 4.9 collective-permute-done.47
  427.5 9.5 %collective-permute-start.18 = (bf16[256,768]{1,0:T(8,128)(2,1)S(1)}, bf16[256,768]{1,0:T(8,128)(2,1)S(1)}, u32[]{:S(2)}, u32[]{:S(2)}) collective-permute-start(bf16[256,768]{1,0:T(8,128)(2,1)S(1)} %copy-done.33), channel_id=1, source_target_pairs={{0,2},{1,3},{2,0},{3,1},{4,6},{5,7},{6,4},{7,5},{8,10},{9,11},{10,... | collective-permute-start | bytes 1179656 | tf_op jit(solution)/shard_map/ppermute | solution.py:357
  437.0 7.9 %collective-permute-done.49 = bf16[128,1536]{1,0:T(8,128)(2,1)S(1)} collective-permute-done((bf16[128,1536]{1,0:T(8,128)(2,1)S(1)}, bf16[128,1536]{1,0:T(8,128)(2,1)S(1)}, u32[]{:S(2)}, u32[]{:S(2)}) %collective-permute-start.49) | collective-permute-done | bytes 393248 | tf_op jit(solution)/shard_map/ppermute | solution.py:426
  452.3 11.0 %collective-permute-done.18 = bf16[256,768]{1,0:T(8,128)(2,1)S(1)} collective-permute-done((bf16[256,768]{1,0:T(8,128)(2,1)S(1)}, bf16[256,768]{1,0:T(8,128)(2,1)S(1)}, u32[]{:S(2)}, u32[]{:S(2)}) %collective-permute-start.18) | collective-permute-done | bytes 393248 | tf_op jit(solution)/shard_map/ppermute | solution.py:357
  473.3 6.7 %collective-permute-done.57 = f32[384,896]{1,0:T(8,128)S(1)} collective-permute-done((f32[384,896]{1,0:T(8,128)S(1)}, f32[384,896]{1,0:T(8,128)S(1)}, u32[]{:S(2)}, u32[]{:S(2)}) %collective-permute-start.57) | collective-permute-done | bytes 1376288 | tf_op jit(solution)/shard_map/ppermute | solution.py:357
  491.6 24.3 %collective-permute-done.26 = bf16[256,1536]{1,0:T(8,128)(2,1)} collective-permute-done((bf16[256,1536]{1,0:T(8,128)(2,1)}, bf16[256,1536]{1,0:T(8,128)(2,1)}, u32[]{:S(2)}, u32[]{:S(2)}) %collective-permute-start.26) | collective-permute-done | bytes 786464 | tf_op jit(solution)/shard_map/ppermute | solution.py:422
  523.3 12.4 %collective-permute-done.29 = bf16[256,1536]{1,0:T(8,128)(2,1)S(1)} collective-permute-done((bf16[256,1536]{1,0:T(8,128)(2,1)}, bf16[256,1536]{1,0:T(8,128)(2,1)S(1)}, u32[]{:S(2)}, u32[]{:S(2)}) %collective-permute-start.29) | collective-permute-done | bytes 786464 | tf_op jit(solution)/shard_map/ppermute | solution.py:427
  (427 shorter events, 226.2 us)
Async XLA Ops:
  4.3 51.6 %collective-permute-start = (bf16[384,1152]{1,0:T(8,128)(2,1)}, bf16[384,1152]{1,0:T(8,128)(2,1)}, u32[]{:S(2)}, u32[]{:S(2)}) collective-permute-start(bf16[384,1152]{1,0:T(8,128)(2,1)} %get-tuple-element.176), channel_id=1, source_target_pairs={{0,16},{8,24},{16,0},{24,8},{1,17},{9,25},{17,1},{25,9},{2,18},{10... | collective-permute-start | bytes 2654216 | tf_op jit(solution)/shard_map/ppermute | solution.py:357
  7.3 50.0 %collective-permute-start.1 = (bf16[384,1152]{1,0:T(8,128)(2,1)}, bf16[384,1152]{1,0:T(8,128)(2,1)}, u32[]{:S(2)}, u32[]{:S(2)}) collective-permute-start(bf16[384,1152]{1,0:T(8,128)(2,1)} %get-tuple-element.176), channel_id=1, source_target_pairs={{0,8},{8,0},{16,24},{24,16},{1,9},{9,1},{17,25},{25,17},{2,10},{10... | collective-permute-start | bytes 2654216 | tf_op jit(solution)/shard_map/ppermute | solution.py:357
  9.4 31.3 %collective-permute-start.5 = (bf16[384,768]{1,0:T(8,128)(2,1)}, bf16[384,768]{1,0:T(8,128)(2,1)}, u32[]{:S(2)}, u32[]{:S(2)}) collective-permute-start(bf16[384,768]{1,0:T(8,128)(2,1)} %bitcast.2), channel_id=1, source_target_pairs={{0,16},{8,24},{16,0},{24,8},{1,17},{9,25},{17,1},{25,9},{2,18},{10... | collective-permute-start | bytes 1769480 | tf_op jit(solution)/shard_map/ppermute | solution.py:357
  9.4 111.3 %collective-permute-start.11 = (bf16[384,768]{1,0:T(8,128)(2,1)}, bf16[384,768]{1,0:T(8,128)(2,1)}, u32[]{:S(2)}, u32[]{:S(2)}) collective-permute-start(bf16[384,768]{1,0:T(8,128)(2,1)} %bitcast.2), channel_id=1, source_target_pairs={{0,1},{1,0},{2,3},{3,2},{4,5},{5,4},{6,7},{7,6},{8,9},{9,8},{10,11... | collective-permute-start | bytes 1769480 | tf_op jit(solution)/shard_map/ppermute | solution.py:357
  11.5 41.0 %collective-permute-start.4 = (bf16[384,768]{1,0:T(8,128)(2,1)}, bf16[384,768]{1,0:T(8,128)(2,1)}, u32[]{:S(2)}, u32[]{:S(2)}) collective-permute-start(bf16[384,768]{1,0:T(8,128)(2,1)} %param.18), channel_id=1, source_target_pairs={{0,16},{8,24},{16,0},{24,8},{1,17},{9,25},{17,1},{25,9},{2,18},{10... | collective-permute-start | bytes 1769480 | tf_op jit(solution)/shard_map/ppermute | solution.py:357
  59.2 63.5 %collective-permute-start.12 = (bf16[384,768]{1,0:T(8,128)(2,1)}, bf16[384,768]{1,0:T(8,128)(2,1)}, u32[]{:S(2)}, u32[]{:S(2)}) collective-permute-start(bf16[384,768]{1,0:T(8,128)(2,1)} %bitcast.2), channel_id=1, source_target_pairs={{0,2},{1,3},{2,0},{3,1},{4,6},{5,7},{6,4},{7,5},{8,10},{9,11},{10,... | collective-permute-start | bytes 1769480 | tf_op jit(solution)/shard_map/ppermute | solution.py:357
  62.1 60.6 %collective-permute-start.13 = (bf16[384,768]{1,0:T(8,128)(2,1)}, bf16[384,768]{1,0:T(8,128)(2,1)}, u32[]{:S(2)}, u32[]{:S(2)}) collective-permute-start(bf16[384,768]{1,0:T(8,128)(2,1)} %bitcast.2), channel_id=1, source_target_pairs={{0,3},{1,2},{2,1},{3,0},{4,7},{5,6},{6,5},{7,4},{8,11},{9,10},{10,... | collective-permute-start | bytes 1769480 | tf_op jit(solution)/shard_map/ppermute | solution.py:357
  128.6 246.1 %collective-permute-start.23 = (bf16[384,2304]{1,0:T(8,128)(2,1)}, bf16[384,2304]{1,0:T(8,128)(2,1)}, u32[]{:S(2)}, u32[]{:S(2)}) collective-permute-start(bf16[384,2304]{1,0:T(8,128)(2,1)} %constant_dynamic-update-slice_fusion.23), channel_id=1, source_target_pairs={{0,16},{8,24},{16,0},{24,8},{1,17},{9,25},{17,1},{25,9},{2,18},{10... | collective-permute-start | bytes 5308424 | tf_op jit(solution)/shard_map/ppermute | solution.py:357
  150.8 96.7 %collective-permute-start.64 = (f32[384,768]{1,0:T(8,128)}, f32[384,768]{1,0:T(8,128)}, u32[]{:S(2)}, u32[]{:S(2)}) collective-permute-start(f32[384,768]{1,0:T(8,128)} %constant_dynamic-slice_fusion.1), channel_id=1, source_target_pairs={{0,8},{8,0},{16,24},{24,16},{1,9},{9,1},{17,25},{25,17},{2,10},{10... | collective-permute-start | bytes 3538952 | tf_op jit(solution)/shard_map/ppermute | solution.py:357
  184.8 24.5 %collective-permute-start.34 = (f32[256,256]{1,0:T(8,128)S(1)}, f32[256,256]{1,0:T(8,128)S(1)}, u32[]{:S(2)}, u32[]{:S(2)}) collective-permute-start(f32[256,256]{1,0:T(8,128)S(1)} %get-tuple-element.173), channel_id=1, source_target_pairs={{0,1},{1,0},{2,3},{3,2},{4,5},{5,4},{6,7},{7,6},{8,9},{9,8},{10,11... | collective-permute-start | bytes 786440 | tf_op jit(solution)/shard_map/ppermute | solution.py:357
  185.1 24.3 %collective-permute-start.35 = (f32[256,256]{1,0:T(8,128)S(1)}, f32[256,256]{1,0:T(8,128)S(1)}, u32[]{:S(2)}, u32[]{:S(2)}) collective-permute-start(f32[256,256]{1,0:T(8,128)S(1)} %get-tuple-element.175), channel_id=1, source_target_pairs={{0,2},{1,3},{2,0},{3,1},{4,6},{5,7},{6,4},{7,5},{8,10},{9,11},{10,... | collective-permute-start | bytes 786440 | tf_op jit(solution)/shard_map/ppermute | solution.py:357
  221.5 31.6 %collective-permute-start.32 = (bf16[256,1536]{1,0:T(8,128)(2,1)}, bf16[256,1536]{1,0:T(8,128)(2,1)}, u32[]{:S(2)}, u32[]{:S(2)}) collective-permute-start(bf16[256,1536]{1,0:T(8,128)(2,1)} %fusion.10), channel_id=1, source_target_pairs={{0,1},{3,2},{4,5},{7,6},{8,9},{11,10},{12,13},{15,14},{16,17},{19,... | collective-permute-start | bytes 2359304 | tf_op jit(solution)/shard_map/ppermute | solution.py:403
  256.1 32.7 %collective-permute-start.30 = (bf16[256,1536]{1,0:T(8,128)(2,1)}, bf16[256,1536]{1,0:T(8,128)(2,1)S(1)}, u32[]{:S(2)}, u32[]{:S(2)}) collective-permute-start(bf16[256,1536]{1,0:T(8,128)(2,1)} %fusion.10), channel_id=1, source_target_pairs={{1,2},{2,1},{5,6},{6,5},{9,10},{10,9},{13,14},{14,13},{17,18},{18,... | collective-permute-start | bytes 2359304 | tf_op jit(solution)/shard_map/ppermute | solution.py:404
  260.5 28.2 %collective-permute-start.31 = (bf16[256,1536]{1,0:T(8,128)(2,1)S(1)}, bf16[256,1536]{1,0:T(8,128)(2,1)S(1)}, u32[]{:S(2)}, u32[]{:S(2)}) collective-permute-start(bf16[256,1536]{1,0:T(8,128)(2,1)S(1)} %copy-done.28), channel_id=1, source_target_pairs={{0,1},{1,0},{2,3},{3,2},{4,5},{5,4},{6,7},{7,6},{8,9},{9,8},{10,11... | collective-permute-start | bytes 2359304 | tf_op jit(solution)/shard_map/ppermute | solution.py:357
  266.2 49.4 %collective-permute-start.33 = (bf16[256,1536]{1,0:T(8,128)(2,1)S(1)}, bf16[256,1536]{1,0:T(8,128)(2,1)S(1)}, u32[]{:S(2)}, u32[]{:S(2)}) collective-permute-start(bf16[256,1536]{1,0:T(8,128)(2,1)S(1)} %fusion.9), channel_id=1, source_target_pairs={{0,2},{1,3},{2,0},{3,1},{4,6},{5,7},{6,4},{7,5},{8,10},{9,11},{10,... | collective-permute-start | bytes 2359304 | tf_op jit(solution)/shard_map/ppermute | solution.py:357
  274.6 86.8 %collective-permute-start.63 = (f32[384,768]{1,0:T(8,128)}, f32[384,768]{1,0:T(8,128)}, u32[]{:S(2)}, u32[]{:S(2)}) collective-permute-start(f32[384,768]{1,0:T(8,128)} %get-tuple-element.162), channel_id=1, source_target_pairs={{0,8},{8,0},{16,24},{24,16},{1,9},{9,1},{17,25},{25,17},{2,10},{10... | collective-permute-start | bytes 3538952 | tf_op jit(solution)/shard_map/ppermute | solution.py:357
  327.8 33.5 %collective-permute-start.65 = (f32[384,768]{1,0:T(8,128)S(1)}, f32[384,768]{1,0:T(8,128)S(1)}, u32[]{:S(2)}, u32[]{:S(2)}) collective-permute-start(f32[384,768]{1,0:T(8,128)S(1)} %copy-done.26), channel_id=1, source_target_pairs={{0,16},{8,24},{16,0},{24,8},{1,17},{9,25},{17,1},{25,9},{2,18},{10... | collective-permute-start | bytes 3538952 | tf_op jit(solution)/shard_map/ppermute | solution.py:357
  329.4 63.9 %collective-permute-start.51 = (f32[384,768]{1,0:T(8,128)}, f32[384,768]{1,0:T(8,128)}, u32[]{:S(2)}, u32[]{:S(2)}) collective-permute-start(f32[384,768]{1,0:T(8,128)} %get-tuple-element.164), channel_id=1, source_target_pairs={{0,8},{8,0},{16,24},{24,16},{1,9},{9,1},{17,25},{25,17},{2,10},{10... | collective-permute-start | bytes 3538952 | tf_op jit(solution)/shard_map/ppermute | solution.py:357
  355.6 37.7 %collective-permute-start.53 = (f32[384,768]{1,0:T(8,128)}, f32[384,768]{1,0:T(8,128)}, u32[]{:S(2)}, u32[]{:S(2)}) collective-permute-start(f32[384,768]{1,0:T(8,128)} %get-tuple-element.165), channel_id=1, source_target_pairs={{0,16},{8,24},{16,0},{24,8},{1,17},{9,25},{17,1},{25,9},{2,18},{10... | collective-permute-start | bytes 3538952 | tf_op jit(solution)/shard_map/ppermute | solution.py:357
  374.7 72.7 %collective-permute-start.22 = (bf16[384,2304]{1,0:T(8,128)(2,1)}, bf16[384,2304]{1,0:T(8,128)(2,1)S(1)}, u32[]{:S(2)}, u32[]{:S(2)}) collective-permute-start(bf16[384,2304]{1,0:T(8,128)(2,1)} %constant_dynamic-update-slice_fusion.23), channel_id=1, source_target_pairs={{0,8},{8,0},{16,24},{24,16},{1,9},{9,1},{17,25},{25,17},{2,10},{10... | collective-permute-start | bytes 5308424 | tf_op jit(solution)/shard_map/ppermute | solution.py:357
  378.4 73.8 %collective-permute-start.17 = (bf16[256,768]{1,0:T(8,128)(2,1)S(1)}, bf16[256,768]{1,0:T(8,128)(2,1)S(1)}, u32[]{:S(2)}, u32[]{:S(2)}) collective-permute-start(bf16[256,768]{1,0:T(8,128)(2,1)S(1)} %copy-done.34), channel_id=1, source_target_pairs={{0,1},{1,0},{2,3},{3,2},{4,5},{5,4},{6,7},{7,6},{8,9},{9,8},{10,11... | collective-permute-start | bytes 1179656 | tf_op jit(solution)/shard_map/ppermute | solution.py:357
  392.3 55.1 %collective-permute-start.24 = (bf16[384,2304]{1,0:T(8,128)(2,1)}, bf16[384,2304]{1,0:T(8,128)(2,1)S(1)}, u32[]{:S(2)}, u32[]{:S(2)}) collective-permute-start(bf16[384,2304]{1,0:T(8,128)(2,1)} %collective-permute-done.23), channel_id=1, source_target_pairs={{0,8},{8,0},{16,24},{24,16},{1,9},{9,1},{17,25},{25,17},{2,10},{10... | collective-permute-start | bytes 5308424 | tf_op jit(solution)/shard_map/ppermute | solution.py:357
  420.1 24.8 %collective-permute-start.49 = (bf16[128,1536]{1,0:T(8,128)(2,1)S(1)}, bf16[128,1536]{1,0:T(8,128)(2,1)S(1)}, u32[]{:S(2)}, u32[]{:S(2)}) collective-permute-start(bf16[128,1536]{1,0:T(8,128)(2,1)S(1)} %collective-permute-done.48), channel_id=1, source_target_pairs={{1,0},{2,3},{5,4},{6,7},{9,8},{10,11},{13,12},{14,15},{17,16},{18,... | collective-permute-start | bytes 1179656 | tf_op jit(solution)/shard_map/ppermute | solution.py:426
  427.5 35.8 %collective-permute-start.18 = (bf16[256,768]{1,0:T(8,128)(2,1)S(1)}, bf16[256,768]{1,0:T(8,128)(2,1)S(1)}, u32[]{:S(2)}, u32[]{:S(2)}) collective-permute-start(bf16[256,768]{1,0:T(8,128)(2,1)S(1)} %copy-done.33), channel_id=1, source_target_pairs={{0,2},{1,3},{2,0},{3,1},{4,6},{5,7},{6,4},{7,5},{8,10},{9,11},{10,... | collective-permute-start | bytes 1179656 | tf_op jit(solution)/shard_map/ppermute | solution.py:357
  447.4 24.0 %collective-permute-start.55 = (f32[384,896]{1,0:T(8,128)S(1)}, f32[384,896]{1,0:T(8,128)S(1)}, u32[]{:S(2)}, u32[]{:S(2)}) collective-permute-start(f32[384,896]{1,0:T(8,128)S(1)} %copy-done.25), channel_id=1, source_target_pairs={{0,8},{8,0},{16,24},{24,16},{1,9},{9,1},{17,25},{25,17},{2,10},{10... | collective-permute-start | bytes 4128776 | tf_op jit(solution)/shard_map/ppermute | solution.py:357
  447.4 32.6 %collective-permute-start.57 = (f32[384,896]{1,0:T(8,128)S(1)}, f32[384,896]{1,0:T(8,128)S(1)}, u32[]{:S(2)}, u32[]{:S(2)}) collective-permute-start(f32[384,896]{1,0:T(8,128)S(1)} %copy-done.24), channel_id=1, source_target_pairs={{0,16},{8,24},{16,0},{24,8},{1,17},{9,25},{17,1},{25,9},{2,18},{10... | collective-permute-start | bytes 4128776 | tf_op jit(solution)/shard_map/ppermute | solution.py:357
  452.2 31.8 %collective-permute-start.66 = (f32[192,768]{1,0:T(8,128)S(1)}, f32[192,768]{1,0:T(8,128)S(1)}, u32[]{:S(2)}, u32[]{:S(2)}) collective-permute-start(f32[192,768]{1,0:T(8,128)S(1)} %constant_dynamic-slice_fusion), channel_id=1, source_target_pairs={{0,4},{4,0},{1,5},{5,1},{2,6},{6,2},{3,7},{7,3},{8,12},{12,8},{9,1... | collective-permute-start | bytes 1769480 | tf_op jit(solution)/shard_map/ppermute | solution.py:357
  464.6 26.1 %collective-permute-start.54 = (f32[192,768]{1,0:T(8,128)S(1)}, f32[192,768]{1,0:T(8,128)S(1)}, u32[]{:S(2)}, u32[]{:S(2)}) collective-permute-start(f32[192,768]{1,0:T(8,128)S(1)} %constant_dynamic-slice_fusion.9), channel_id=1, source_target_pairs={{0,4},{4,0},{1,5},{5,1},{2,6},{6,2},{3,7},{7,3},{8,12},{12,8},{9,1... | collective-permute-start | bytes 1769480 | tf_op jit(solution)/shard_map/ppermute | solution.py:357
  481.6 35.5 %collective-permute-start.58 = (f32[192,896]{1,0:T(8,128)S(1)}, f32[192,896]{1,0:T(8,128)S(1)}, u32[]{:S(2)}, u32[]{:S(2)}) collective-permute-start(f32[192,896]{1,0:T(8,128)S(1)} %constant_dynamic-slice_fusion.6), channel_id=1, source_target_pairs={{0,4},{4,0},{1,5},{5,1},{2,6},{6,2},{3,7},{7,3},{8,12},{12,8},{9,1... | collective-permute-start | bytes 2064392 | tf_op jit(solution)/shard_map/ppermute | solution.py:357
  481.7 37.1 %collective-permute-start.25 = (bf16[256,1536]{1,0:T(8,128)(2,1)}, bf16[256,1536]{1,0:T(8,128)(2,1)}, u32[]{:S(2)}, u32[]{:S(2)}) collective-permute-start(bf16[256,1536]{1,0:T(8,128)(2,1)} %get-tuple-element.189), channel_id=1, source_target_pairs={{0,1},{1,0},{2,3},{3,2},{4,5},{5,4},{6,7},{7,6},{8,9},{9,8},{10,11... | collective-permute-start | bytes 2359304 | tf_op jit(solution)/shard_map/ppermute | solution.py:357
  484.0 31.9 %collective-permute-start.26 = (bf16[256,1536]{1,0:T(8,128)(2,1)}, bf16[256,1536]{1,0:T(8,128)(2,1)}, u32[]{:S(2)}, u32[]{:S(2)}) collective-permute-start(bf16[256,1536]{1,0:T(8,128)(2,1)} %get-tuple-element.189), channel_id=1, source_target_pairs={{0,2},{3,1},{4,6},{7,5},{8,10},{11,9},{12,14},{15,13},{16,18},{19,... | collective-permute-start | bytes 2359304 | tf_op jit(solution)/shard_map/ppermute | solution.py:422
  488.5 32.4 %collective-permute-start.28 = (bf16[256,1536]{1,0:T(8,128)(2,1)}, bf16[256,1536]{1,0:T(8,128)(2,1)}, u32[]{:S(2)}, u32[]{:S(2)}) collective-permute-start(bf16[256,1536]{1,0:T(8,128)(2,1)} %collective-permute-done.27), channel_id=1, source_target_pairs={{1,0},{2,3},{5,4},{6,7},{9,8},{10,11},{13,12},{14,15},{17,16},{18,... | collective-permute-start | bytes 2359304 | tf_op jit(solution)/shard_map/ppermute | solution.py:426
  (113 other events, 1421.8 us)
